TPU v7x, 128 devices: a whole 4x4x4 slice. The times are simulated.
128 devices in a mesh: seq: 8 (over z, core), exp: 16 (over y, x).
Axes of the slice: x: 4, y: 4, z: 4, core: 2. Of those that a mesh axis runs over, the one named last changes fastest.
Arguments:
- attn_query: bfloat16 [2048, 6144], P('seq', 'exp'), may hold values from -6 to 6
- attn_key: bfloat16 [2048, 6144], P('seq', 'exp'), may hold values from -6 to 6
- attn_value: bfloat16 [2048, 6144], P('seq', 'exp'), may hold values from -40 to 40
- log_decay: float32 [48, 2048], P('exp', 'seq'), may hold values from -1.5 to 0
- residual: bfloat16 [2048, 6144], P('seq', 'exp'), may hold values from -6 to 6
- norm_gain: bfloat16 [6144], P('exp'), may hold values from 0.099609375 to 1.8984375
- expert_ids: int32 [2048, 2], P('seq'), may hold values from 0 to 15, as said below
- router_weight: bfloat16 [6144, 16], P(None, 'seq'), may hold values from -0.078125 to 0.078125
- gate_weight: bfloat16 [16, 6144, 4608], P('seq', None, 'exp'), may hold values from -0.078125 to 0.078125
- up_weight: bfloat16 [16, 6144, 4608], P('seq', None, 'exp'), may hold values from -0.078125 to 0.078125
- down_weight: bfloat16 [16, 4608, 6144], P('seq', 'exp'), may hold values from -0.125 to 0.125
Outputs:
- layer_out: bfloat16 [2048, 6144], P('seq', 'exp')
Inputs may be any that keep to these rules, and one draw needn't show every extreme that they name: `expert_ids`: each row names two different experts. In every section of 256 consecutive rows no expert is named more than 64 times, and in every section some experts are named exactly 64 times.
All inputs are finite; a program needn't handle non-finite values.
Results may differ from a plain program's by a relative error of at most 0.017.
Values may be sent and summed in bfloat16 or wider, within the bound.
A program may use at most 192 MiB of HBM per device.

v0:
```python
import jax
import jax.numpy as jnp
from jax import lax
from jax.sharding import PartitionSpec as P


def shifted(array, axis, by):
    count = lax.axis_size(axis)
    pairs = [(i, i + by) for i in range(count) if 0 <= i + by < count]
    return lax.ppermute(array, axis, pairs)


def on_device(
    attn_query,
    attn_key,
    attn_value,
    log_decay,
    residual,
    norm_gain,
    expert_ids,
    router_weight,
    gate_weight,
    up_weight,
    down_weight,
):
    heads_here = log_decay.shape[0]
    length = log_decay.shape[1]
    head_size = attn_query.shape[1] // heads_here
    query_rows = attn_query.reshape(length, heads_here, head_size)
    key_rows = attn_key.reshape(length, heads_here, head_size)
    value_rows = attn_value.reshape(length, heads_here, head_size)
    cumulative = jnp.cumsum(log_decay, axis=1)
    causal = lax.broadcasted_iota(jnp.int32, (length, length), 0) >= lax.broadcasted_iota(
        jnp.int32, (length, length), 1
    )
    decay_gap = jnp.where(causal[None], cumulative[:, :, None] - cumulative[:, None, :], 0.0)
    decay_mask = jnp.where(causal[None], jnp.exp(decay_gap), 0.0)
    scores = jnp.einsum("thd,shd->hts", query_rows, key_rows, preferred_element_type=jnp.float32)
    weights = (scores * decay_mask).astype(jnp.bfloat16)
    intra_part = jnp.einsum("hts,shd->thd", weights, value_rows, preferred_element_type=jnp.float32)
    key_fade = jnp.exp(cumulative[:, -1:] - cumulative)
    scaled = (key_fade.T[:, :, None] * key_rows.astype(jnp.float32)).astype(jnp.bfloat16)
    local_state = jnp.einsum("shd,she->hde", scaled, value_rows, preferred_element_type=jnp.float32)
    section_fade = jnp.exp(cumulative[:, -1])
    incoming = jnp.zeros_like(local_state)
    for repeat_index in range(lax.axis_size("seq") - 1):
        incoming = shifted(section_fade[:, None, None] * incoming + local_state, "seq", 1)
    inter_part = jnp.einsum(
        "thd,hde->the", query_rows.astype(jnp.float32), incoming, precision=lax.Precision.HIGHEST
    )
    attn_out = intra_part + jnp.exp(cumulative).T[:, :, None] * inter_part
    mean_square = jnp.mean(attn_out * attn_out, axis=2, keepdims=True)
    normed = (attn_out / jnp.sqrt(mean_square + 1e-06)).reshape(length, heads_here * head_size)
    stream = (residual.astype(jnp.float32) + norm_gain.astype(jnp.float32) * normed).astype(
        jnp.bfloat16
    )
    experts_here = router_weight.shape[1]
    groups = lax.axis_size("seq")
    expert_count = experts_here * groups
    capacity = 4 * length // expert_count
    features = stream.shape[1]
    choices_per_token = expert_ids.shape[1]
    flat_ids = expert_ids.reshape(-1)
    expert_iota = lax.broadcasted_iota(jnp.int32, (1, expert_count), 1)
    onehot = (flat_ids[:, None] == expert_iota).astype(jnp.int32)
    running = jnp.cumsum(onehot, axis=0)
    slot_index = jnp.sum(running * onehot, axis=1) - 1
    target = flat_ids * capacity + slot_index
    place_iota = lax.broadcasted_iota(jnp.int32, (expert_count * capacity, 1), 0)
    route_matrix = (
        (place_iota == target[None, :])
        .astype(jnp.bfloat16)
        .reshape(expert_count * capacity, length, choices_per_token)
        .sum(axis=2)
    )
    outgoing = jnp.dot(route_matrix, stream, preferred_element_type=jnp.float32).astype(
        jnp.bfloat16
    )
    outgoing = outgoing.reshape(groups, experts_here, capacity, features)
    portion = lax.all_gather(
        lax.all_to_all(outgoing, "seq", split_axis=0, concat_axis=0, tiled=True),
        "exp",
        axis=3,
        tiled=True,
    )
    gate_acc = jnp.einsum(
        "sjcd,jdf->sjcf", portion, gate_weight, preferred_element_type=jnp.float32
    )
    upward = jnp.einsum("sjcd,jdf->sjcf", portion, up_weight, preferred_element_type=jnp.float32)
    logits = jnp.einsum("sjcd,dj->sjc", portion, router_weight, preferred_element_type=jnp.float32)
    hidden_act = (jax.nn.silu(gate_acc) * upward).astype(jnp.bfloat16)
    expert_out = lax.psum_scatter(
        jnp.einsum(
            "sjcf,jfd->dsjc", hidden_act, down_weight, preferred_element_type=jnp.float32
        ).astype(jnp.bfloat16),
        "exp",
        scatter_dimension=0,
        tiled=True,
    ).astype(jnp.float32)
    routed = (jax.nn.sigmoid(logits)[None] * expert_out).astype(jnp.bfloat16)
    returned = lax.all_to_all(routed, "seq", split_axis=1, concat_axis=1, tiled=True)
    returned = returned.reshape(features, expert_count * capacity)
    combined = lax.dot_general(
        route_matrix, returned, (((0,), (1,)), ((), ())), preferred_element_type=jnp.float32
    )
    return (stream.astype(jnp.float32) + combined).astype(jnp.bfloat16)


def solution(mesh):
    in_specs = (
        P("seq", "exp"),
        P("seq", "exp"),
        P("seq", "exp"),
        P("exp", "seq"),
        P("seq", "exp"),
        P("exp"),
        P("seq", None),
        P(None, "seq"),
        P("seq", None, "exp"),
        P("seq", None, "exp"),
        P("seq", "exp", None),
    )
    out_specs = P("seq", "exp")
    return jax.shard_map(
        on_device, mesh=mesh, in_specs=in_specs, out_specs=out_specs, check_vma=False
    )
```

profile of v0, /device:TPU:1, one launch (start us, length us, event | category | flops | bytes accessed | tf_op | source)
XLA Modules:
  0.0 400.8 jit_solution(6427846024970069958)
XLA Ops:
  11.2 4.9 %collective-permute-start = (f32[3,128,128]{2,1,0:T(8,128)S(1)}, f32[3,128,128]{2,1,0:T(8,128)S(1)}, u32[]{:S(2)}, u32[]{:S(2)}) collective-permute-start(f32[3,128,128]{2,1,0:T(8,128)S(1)} %get-tuple-element.9), channel_id=1, source_target_pairs={{0,16},{16,32},{32,48},{48,64},{64,80},{80,96},{96,112},{1,17},{17... | collective-permute-start | bytes 589832 | tf_op jit(solution)/shard_map/ppermute | solution.py:10
  18.8 4.4 %collective-permute-start.1 = (f32[3,128,128]{2,1,0:T(8,128)S(1)}, f32[3,128,128]{2,1,0:T(8,128)S(1)}, u32[]{:S(2)}, u32[]{:S(2)}) collective-permute-start(f32[3,128,128]{2,1,0:T(8,128)S(1)} %multiply_add_fusion.5), channel_id=1, source_target_pairs={{0,16},{16,32},{32,48},{48,64},{64,80},{80,96},{96,112},{1,17},{17... | collective-permute-start | bytes 589832 | tf_op jit(solution)/shard_map/ppermute | solution.py:10
  24.4 1.4 collective-permute-done.1
  25.9 4.4 %collective-permute-start.2 = (f32[3,128,128]{2,1,0:T(8,128)S(1)}, f32[3,128,128]{2,1,0:T(8,128)S(1)}, u32[]{:S(2)}, u32[]{:S(2)}) collective-permute-start(f32[3,128,128]{2,1,0:T(8,128)S(1)} %multiply_add_fusion.4), channel_id=1, source_target_pairs={{0,16},{16,32},{32,48},{48,64},{64,80},{80,96},{96,112},{1,17},{17... | collective-permute-start | bytes 589832 | tf_op jit(solution)/shard_map/ppermute | solution.py:10
  30.7 2.2 collective-permute-done.2
  33.0 4.4 %collective-permute-start.3 = (f32[3,128,128]{2,1,0:T(8,128)S(1)}, f32[3,128,128]{2,1,0:T(8,128)S(1)}, u32[]{:S(2)}, u32[]{:S(2)}) collective-permute-start(f32[3,128,128]{2,1,0:T(8,128)S(1)} %multiply_add_fusion.3), channel_id=1, source_target_pairs={{0,16},{16,32},{32,48},{48,64},{64,80},{80,96},{96,112},{1,17},{17... | collective-permute-start | bytes 589832 | tf_op jit(solution)/shard_map/ppermute | solution.py:10
  38.7 1.3 collective-permute-done.3
  40.1 4.4 %collective-permute-start.4 = (f32[3,128,128]{2,1,0:T(8,128)S(1)}, f32[3,128,128]{2,1,0:T(8,128)S(1)}, u32[]{:S(2)}, u32[]{:S(2)}) collective-permute-start(f32[3,128,128]{2,1,0:T(8,128)S(1)} %multiply_add_fusion.2), channel_id=1, source_target_pairs={{0,16},{16,32},{32,48},{48,64},{64,80},{80,96},{96,112},{1,17},{17... | collective-permute-start | bytes 589832 | tf_op jit(solution)/shard_map/ppermute | solution.py:10
  45.2 1.9 collective-permute-done.4
  47.1 4.4 %collective-permute-start.5 = (f32[3,128,128]{2,1,0:T(8,128)S(1)}, f32[3,128,128]{2,1,0:T(8,128)S(1)}, u32[]{:S(2)}, u32[]{:S(2)}) collective-permute-start(f32[3,128,128]{2,1,0:T(8,128)S(1)} %multiply_add_fusion.1), channel_id=1, source_target_pairs={{0,16},{16,32},{32,48},{48,64},{64,80},{80,96},{96,112},{1,17},{17... | collective-permute-start | bytes 589832 | tf_op jit(solution)/shard_map/ppermute | solution.py:10
  52.0 2.1 collective-permute-done.5
  54.2 4.4 %collective-permute-start.6 = (f32[3,128,128]{2,1,0:T(8,128)S(1)}, f32[3,128,128]{2,1,0:T(8,128)S(1)}, u32[]{:S(2)}, u32[]{:S(2)}) collective-permute-start(f32[3,128,128]{2,1,0:T(8,128)S(1)} %multiply_add_fusion), channel_id=1, source_target_pairs={{0,16},{16,32},{32,48},{48,64},{64,80},{80,96},{96,112},{1,17},{17... | collective-permute-start | bytes 589832 | tf_op jit(solution)/shard_map/ppermute | solution.py:10
  59.1 2.1 collective-permute-done.6
  62.4 18.3 %all_to_all.10 = bf16[8,2,64,384]{3,2,1,0:T(8,128)(2,1)S(1)} all-to-all(bf16[8,2,64,384]{3,2,1,0:T(8,128)(2,1)S(1)} %bitcast.110), channel_id=1, replica_groups=mesh['seq'=8,'exp'=16] {'seq'}, dimensions={0} | all-to-all | bytes 1572864 | tf_op jit(solution)/shard_map/all_to_all | solution.py:81
  81.9 98.5 %all-gather.2.cloned.1.call-done = bf16[8,2,64,6144]{3,2,0,1:T(8,128)(2,1)} async-done(((bf16[8,2,64,384]{3,2,0,1:T(8,128)(2,1)}), bf16[8,2,64,6144]{3,2,0,1:T(8,128)(2,1)}) %all-gather.2.cloned.1.call-update) | async-done | bytes 12582928 | tf_op jit(solution)/shard_map/all_gather | solution.py:80
  180.3 11.8 %fusion.3 = f32[2,8,64,288]{3,2,1,0:T(8,128)S(1)} fusion(bf16[8,2,64,6144]{3,2,0,1:T(8,128)(2,1)} %all-gather.2.cloned.1.call-done, bf16[2,6144,288]{1,2,0:T(8,128)(2,1)} %param.19), kind=kOutput, calls=%fused_computation.4 | convolution fusion | flops 3623878656 | bytes 20840448 | tf_op jit(solution)/shard_map/sjcd,jdf->sjcf/dot_general | solution.py:86
  192.1 8.9 %fusion.6 = bf16[8,2,64,288]{3,2,0,1:T(8,128)(2,1)S(1)} fusion(f32[2,8,64,288]{3,2,1,0:T(8,128)S(1)} %fusion.3, bf16[8,2,64,6144]{3,2,0,1:T(8,128)(2,1)S(1)} %copy-done.1, bf16[2,6144,288]{1,2,0:T(8,128)(2,1)} %param.20), kind=kOutput, calls=%fused_computation.9 | convolution fusion | flops 3625648128 | bytes 21430272 | tf_op jit(solution)/shard_map/sjcd,jdf->sjcf/dot_general | solution.py:89
  201.1 12.6 %convert_bitcast_fusion = bf16[6144,8,2,64]{0,3,1,2:T(8,128)(2,1)} fusion(bf16[8,2,64,288]{3,2,0,1:T(8,128)(2,1)S(1)} %fusion.6, bf16[2,288,6144]{2,1,0:T(8,128)(2,1)} %param.21), kind=kOutput, calls=%fused_computation | convolution fusion | flops 3630170112 | bytes 20250624 | tf_op jit(solution)/shard_map/sjcf,jfd->dsjc/dot_general | solution.py:93
  213.7 29.7 %copy.107 = bf16[6144,8,2,64]{3,1,2,0:T(8,128)(2,1)} copy(bf16[6144,8,2,64]{0,3,1,2:T(8,128)(2,1)} %convert_bitcast_fusion) | data formatting | bytes 25165824
  243.4 33.4 %reshape.128 = bf16[6144,1024]{1,0:T(8,128)(2,1)} reshape(bf16[6144,2,8,64]{3,2,1,0:T(8,128)(2,1)} %bitcast.108) | data formatting | bytes 25165824
  276.8 7.9 %fusion.29 = f32[2,1,8,64]{3,1,2,0:T(1,128)S(1)} fusion(bf16[8,2,64,6144]{3,2,0,1:T(8,128)(2,1)} %all-gather.2.cloned.1.call-done, bf16[6144,2,1,1]{0,1,2,3:T(2,128)(2,1)S(1)} %bitcast.107), kind=kOutput, calls=%fused_computation.49 | convolution fusion | flops 12582912 | bytes 12611584 | tf_op jit(solution)/shard_map/sjcd,dj->sjc/dot_general | solution.py:90
  284.7 86.8 %reduce-scatter.4.cloned.1.call-done = bf16[384,1024]{1,0:T(8,128)(2,1)} async-done(((bf16[6144,1024]{1,0:T(8,128)(2,1)}), bf16[384,1024]{1,0:T(8,128)(2,1)}) %reduce-scatter.4.cloned.1.call-update) | async-done | bytes 786448
  371.5 2.5 reshape.129
  375.5 17.3 %all_to_all.11 = bf16[384,8,2,64]{0,3,2,1:T(8,128)(2,1)S(1)} all-to-all(bf16[384,8,2,64]{0,3,2,1:T(8,128)(2,1)S(1)} %copy.96), channel_id=1, replica_groups=mesh['seq'=8,'exp'=16] {'seq'}, dimensions={1} | all-to-all | bytes 1572864 | tf_op jit(solution)/shard_map/all_to_all | solution.py:101
  (63 shorter events, 17.2 us)
Async XLA Ops:
  6.5 270.3 %copy-start = (bf16[6144,2]{0,1:T(2,128)(2,1)S(1)}, bf16[6144,2]{0,1:T(2,128)(2,1)}, u32[]{:S(2)}) copy-start(bf16[6144,2]{0,1:T(2,128)(2,1)} %param.18) | copy-start | bytes 73732
  6.5 55.3 %copy-start.2 = (bf16[256,384]{1,0:T(8,128)(2,1)S(1)}, bf16[256,384]{1,0:T(8,128)(2,1)}, u32[]{:S(2)}) copy-start(bf16[256,384]{1,0:T(8,128)(2,1)} %param.15) | copy-start | bytes 589828
  6.5 173.8 %all-gather.2.cloned.1.call-start = ((), (), s32[]{:S(2)}) async-start(), calls=%async_computation.3 | async-start | bytes 13369344 | tf_op jit(solution)/shard_map/all_gather | solution.py:80
  11.2 7.5 %collective-permute-start = (f32[3,128,128]{2,1,0:T(8,128)S(1)}, f32[3,128,128]{2,1,0:T(8,128)S(1)}, u32[]{:S(2)}, u32[]{:S(2)}) collective-permute-start(f32[3,128,128]{2,1,0:T(8,128)S(1)} %get-tuple-element.9), channel_id=1, source_target_pairs={{0,16},{16,32},{32,48},{48,64},{64,80},{80,96},{96,112},{1,17},{17... | collective-permute-start | bytes 589832 | tf_op jit(solution)/shard_map/ppermute | solution.py:10
  18.8 7.0 %collective-permute-start.1 = (f32[3,128,128]{2,1,0:T(8,128)S(1)}, f32[3,128,128]{2,1,0:T(8,128)S(1)}, u32[]{:S(2)}, u32[]{:S(2)}) collective-permute-start(f32[3,128,128]{2,1,0:T(8,128)S(1)} %multiply_add_fusion.5), channel_id=1, source_target_pairs={{0,16},{16,32},{32,48},{48,64},{64,80},{80,96},{96,112},{1,17},{17... | collective-permute-start | bytes 589832 | tf_op jit(solution)/shard_map/ppermute | solution.py:10
  25.9 7.0 %collective-permute-start.2 = (f32[3,128,128]{2,1,0:T(8,128)S(1)}, f32[3,128,128]{2,1,0:T(8,128)S(1)}, u32[]{:S(2)}, u32[]{:S(2)}) collective-permute-start(f32[3,128,128]{2,1,0:T(8,128)S(1)} %multiply_add_fusion.4), channel_id=1, source_target_pairs={{0,16},{16,32},{32,48},{48,64},{64,80},{80,96},{96,112},{1,17},{17... | collective-permute-start | bytes 589832 | tf_op jit(solution)/shard_map/ppermute | solution.py:10
  33.0 7.0 %collective-permute-start.3 = (f32[3,128,128]{2,1,0:T(8,128)S(1)}, f32[3,128,128]{2,1,0:T(8,128)S(1)}, u32[]{:S(2)}, u32[]{:S(2)}) collective-permute-start(f32[3,128,128]{2,1,0:T(8,128)S(1)} %multiply_add_fusion.3), channel_id=1, source_target_pairs={{0,16},{16,32},{32,48},{48,64},{64,80},{80,96},{96,112},{1,17},{17... | collective-permute-start | bytes 589832 | tf_op jit(solution)/shard_map/ppermute | solution.py:10
  40.1 7.0 %collective-permute-start.4 = (f32[3,128,128]{2,1,0:T(8,128)S(1)}, f32[3,128,128]{2,1,0:T(8,128)S(1)}, u32[]{:S(2)}, u32[]{:S(2)}) collective-permute-start(f32[3,128,128]{2,1,0:T(8,128)S(1)} %multiply_add_fusion.2), channel_id=1, source_target_pairs={{0,16},{16,32},{32,48},{48,64},{64,80},{80,96},{96,112},{1,17},{17... | collective-permute-start | bytes 589832 | tf_op jit(solution)/shard_map/ppermute | solution.py:10
  47.1 7.0 %collective-permute-start.5 = (f32[3,128,128]{2,1,0:T(8,128)S(1)}, f32[3,128,128]{2,1,0:T(8,128)S(1)}, u32[]{:S(2)}, u32[]{:S(2)}) collective-permute-start(f32[3,128,128]{2,1,0:T(8,128)S(1)} %multiply_add_fusion.1), channel_id=1, source_target_pairs={{0,16},{16,32},{32,48},{48,64},{64,80},{80,96},{96,112},{1,17},{17... | collective-permute-start | bytes 589832 | tf_op jit(solution)/shard_map/ppermute | solution.py:10
  54.2 7.0 %collective-permute-start.6 = (f32[3,128,128]{2,1,0:T(8,128)S(1)}, f32[3,128,128]{2,1,0:T(8,128)S(1)}, u32[]{:S(2)}, u32[]{:S(2)}) collective-permute-start(f32[3,128,128]{2,1,0:T(8,128)S(1)} %multiply_add_fusion), channel_id=1, source_target_pairs={{0,16},{16,32},{32,48},{48,64},{64,80},{80,96},{96,112},{1,17},{17... | collective-permute-start | bytes 589832 | tf_op jit(solution)/shard_map/ppermute | solution.py:10
  81.6 289.9 %reduce-scatter.4.cloned.1.call-start = ((), (), s32[]{:S(2)}) async-start(), calls=%async_computation.4 | async-start | bytes 13369344
  180.3 11.8 %copy-start.1 = (bf16[8,2,64,6144]{3,2,0,1:T(8,128)(2,1)S(1)}, bf16[8,2,64,6144]{3,2,0,1:T(8,128)(2,1)}, u32[]{:S(2)}) copy-start(bf16[8,2,64,6144]{3,2,0,1:T(8,128)(2,1)} %all-gather.2.cloned.1.call-done) | copy-start | bytes 37748740
Sparse Core Ops, SparseCore 0:
  81.7 98.5 all-gather.1
  276.9 94.5 reduce-scatter.3
where the time goes:
time: 403 us; the launch traced here: 401 us
  waiting for transfers between devices  197 us (49%)
  local copies, waits for them, and re-layouts  73.9 us (18%)
  matrix products  43.9 us (11%)
  blocking collectives  35.6 us (9%)
  starting transfers between devices  31.5 us (8%)
  between operations  13.7 us (3%)
  other arithmetic  5.1 us (1%)
    all_gather x1, waiting for transfers between devices, on_device(): lax.all_gather(lax.all_to_all(outgoing, 'seq', split_axis=0, concat_axis=...  98.5 us
    unnamed x3, waiting for transfers between devices  86.8 us
    unnamed x16, local copies, waits for them, and re-layouts  70.9 us
    ppermute x7, starting transfers between devices, shifted(): return lax.ppermute(array, axis, pairs)  31.3 us
    all_to_all x1, blocking collectives, on_device(): lax.all_to_all(outgoing, 'seq', split_axis=0, concat_axis=0, tiled=True)  18.3 us
    all_to_all x1, blocking collectives, on_device(): lax.all_to_all(routed, 'seq', split_axis=1, concat_axis=1, tiled=True)  17.3 us
    dot_general x1, matrix products, on_device(): jnp.einsum('sjcf,jfd->dsjc', hidden_act, down_weight, preferred_element_t...  12.6 us
    dot_general x1, matrix products, on_device(): jnp.einsum('sjcd,jdf->sjcf', portion, gate_weight, preferred_element_type...  11.8 us
  transfers between devices with their start and end apart: 9, of which 9 were waited for; matrix products, arithmetic and copies ran while one was open for 4% of the time, Pallas kernels for 0%

commit v1 on v0

--- a/solution.py
+++ b/solution.py
@@ -1,13 +1,54 @@
+import functools
+
 import jax
 import jax.numpy as jnp
 from jax import lax
 from jax.sharding import PartitionSpec as P
+from jax.experimental import pallas as pl
+from jax.experimental.pallas import tpu as pltpu
 
 
 def shifted(array, axis, by):
     count = lax.axis_size(axis)
     pairs = [(i, i + by) for i in range(count) if 0 <= i + by < count]
     return lax.ppermute(array, axis, pairs)
+
+
+def down_kernel(blocks_per_step, block_width, h_ref, w_ref, o_ref):
+    sections, capacity, hidden = h_ref.shape
+    rows = h_ref[...].reshape(sections * capacity, hidden)
+    product = jnp.dot(rows, w_ref[...], preferred_element_type=jnp.float32)
+    for i in range(blocks_per_step):
+        piece = product[:, i * block_width : (i + 1) * block_width]
+        o_ref[i] = piece.astype(o_ref.dtype).reshape(sections, capacity, block_width)
+
+
+def down_projection(hidden_act, down_weight, shards):
+    sections, experts_here, capacity, hidden = hidden_act.shape
+    features = down_weight.shape[2]
+    block_width = features // shards
+    blocks_per_step = 4
+    steps = shards // blocks_per_step
+    return pl.pallas_call(
+        functools.partial(down_kernel, blocks_per_step, block_width),
+        out_shape=jax.ShapeDtypeStruct(
+            (shards, sections, experts_here, capacity, block_width), jnp.bfloat16
+        ),
+        grid=(experts_here, steps),
+        in_specs=[
+            pl.BlockSpec((sections, None, capacity, hidden), lambda j, b: (0, j, 0, 0)),
+            pl.BlockSpec((None, hidden, blocks_per_step * block_width), lambda j, b: (j, 0, b)),
+        ],
+        out_specs=pl.BlockSpec(
+            (blocks_per_step, sections, None, capacity, block_width),
+            lambda j, b: (b, 0, j, 0, 0),
+        ),
+        cost_estimate=pl.CostEstimate(
+            flops=2 * sections * experts_here * capacity * hidden * features,
+            bytes_accessed=2 * (hidden_act.size + down_weight.size + hidden_act.size // hidden * features),
+            transcendentals=0,
+        ),
+    )(hidden_act, down_weight)
 
 
 def on_device(
@@ -41,10 +82,26 @@
     key_fade = jnp.exp(cumulative[:, -1:] - cumulative)
     scaled = (key_fade.T[:, :, None] * key_rows.astype(jnp.float32)).astype(jnp.bfloat16)
     local_state = jnp.einsum("shd,she->hde", scaled, value_rows, preferred_element_type=jnp.float32)
-    section_fade = jnp.exp(cumulative[:, -1])
-    incoming = jnp.zeros_like(local_state)
-    for repeat_index in range(lax.axis_size("seq") - 1):
-        incoming = shifted(section_fade[:, None, None] * incoming + local_state, "seq", 1)
+    section_log_fade = cumulative[:, -1]
+    sections_total = lax.axis_size("seq")
+    packed = jnp.concatenate(
+        [local_state, jnp.broadcast_to(section_log_fade[:, None, None], (heads_here, 8, head_size))],
+        axis=1,
+    )
+    gathered = lax.all_gather(packed, "seq", axis=0)
+    all_states = gathered[:, :, :head_size, :]
+    all_log_fades = gathered[:, :, head_size, 0]
+    me = lax.axis_index("seq")
+    section_iota = lax.broadcasted_iota(jnp.int32, (sections_total, sections_total), 0)
+    between_iota = lax.broadcasted_iota(jnp.int32, (sections_total, sections_total), 1)
+    between = (between_iota > section_iota) & (between_iota < me)
+    log_weight = jnp.sum(
+        jnp.where(between[:, :, None], all_log_fades[None, :, :], 0.0), axis=1
+    )
+    state_weight = jnp.where(
+        lax.broadcasted_iota(jnp.int32, (sections_total, 1), 0) < me, jnp.exp(log_weight), 0.0
+    )
+    incoming = jnp.sum(state_weight[:, :, None, None] * all_states, axis=0)
     inter_part = jnp.einsum(
         "thd,hde->the", query_rows.astype(jnp.float32), incoming, precision=lax.Precision.HIGHEST
     )
@@ -89,19 +146,18 @@
     upward = jnp.einsum("sjcd,jdf->sjcf", portion, up_weight, preferred_element_type=jnp.float32)
     logits = jnp.einsum("sjcd,dj->sjc", portion, router_weight, preferred_element_type=jnp.float32)
     hidden_act = (jax.nn.silu(gate_acc) * upward).astype(jnp.bfloat16)
+    shards = lax.axis_size("exp")
     expert_out = lax.psum_scatter(
-        jnp.einsum(
-            "sjcf,jfd->dsjc", hidden_act, down_weight, preferred_element_type=jnp.float32
-        ).astype(jnp.bfloat16),
+        down_projection(hidden_act, down_weight, shards),
         "exp",
         scatter_dimension=0,
         tiled=True,
-    ).astype(jnp.float32)
-    routed = (jax.nn.sigmoid(logits)[None] * expert_out).astype(jnp.bfloat16)
-    returned = lax.all_to_all(routed, "seq", split_axis=1, concat_axis=1, tiled=True)
-    returned = returned.reshape(features, expert_count * capacity)
+    )[0].astype(jnp.float32)
+    routed = (jax.nn.sigmoid(logits)[..., None] * expert_out).astype(jnp.bfloat16)
+    returned = lax.all_to_all(routed, "seq", split_axis=0, concat_axis=0, tiled=True)
+    returned = returned.reshape(expert_count * capacity, features)
     combined = lax.dot_general(
-        route_matrix, returned, (((0,), (1,)), ((), ())), preferred_element_type=jnp.float32
+        route_matrix, returned, (((0,), (0,)), ((), ())), preferred_element_type=jnp.float32
     )
     return (stream.astype(jnp.float32) + combined).astype(jnp.bfloat16)
 

time: 403 us -> 317 us (0.79)
  local copies, waits for them, and re-layouts: 73.9 us -> 8.29 us
  starting transfers between devices: 31.5 us -> 0.09 us
  Pallas kernels: 0 us -> 12.8 us
  waiting for transfers between devices: 197 us -> 208 us
  matrix products: 43.9 us -> 33.4 us
    unnamed x16 -> x17, local copies, waits for them, and re-layouts: 70.9 us -> 4.25 us
    ppermute x7 -> x0, starting transfers between devices: 31.3 us -> none  [shifted(): return lax.ppermute(array, axis, pairs)]
    all_gather x0 -> x1, waiting for transfers between devices: none -> 22.6 us  [on_device(): gathered = lax.all_gather(packed, 'seq', axis=0)]
    pallas_call x0 -> x1, Pallas kernels: none -> 12.8 us  [down_projection(): pl.pallas_call(functools.partial(down_kernel, blocks_per_step, block_widt...]
    dot_general x2 -> x1, matrix products: 13.7 us -> 1.15 us  [on_device(): lax.dot_general(route_matrix, returned, (((0,), (0,)), ((), ())), preferr...]
    ppermute x7 -> x0, waiting for transfers between devices: 11.8 us -> none  [shifted(): return lax.ppermute(array, axis, pairs)]
    unnamed x3 -> x4, waiting for transfers between devices: 86.8 us -> 86.7 us
  transfers between devices with their start and end apart: 9 -> 3, of which waited for: 9 -> 3; matrix products, arithmetic and copies ran while one was open for 4% -> 4% of each run, Pallas kernels for 0% -> 0%
where the time goes in v1:
time: 317 us
  waiting for transfers between devices  208 us (66%)
  matrix products  33.4 us (11%)
  blocking collectives  32.8 us (10%)
  between operations  13.3 us (4%)
  Pallas kernels  12.8 us (4%)
  local copies, waits for them, and re-layouts  8.29 us (3%)
  other arithmetic  8.14 us (3%)
    all_gather x1, waiting for transfers between devices, on_device(): lax.all_gather(lax.all_to_all(outgoing, 'seq', split_axis=0, concat_axis=...  98.4 us
    unnamed x4, waiting for transfers between devices  86.7 us
    all_gather x1, waiting for transfers between devices, on_device(): gathered = lax.all_gather(packed, 'seq', axis=0)  22.6 us
    all_to_all x1, blocking collectives, on_device(): lax.all_to_all(routed, 'seq', split_axis=0, concat_axis=0, tiled=True)  17.3 us
    all_to_all x1, blocking collectives, on_device(): lax.all_to_all(outgoing, 'seq', split_axis=0, concat_axis=0, tiled=True)  15.5 us
    pallas_call x1, Pallas kernels, down_projection(): pl.pallas_call(functools.partial(down_kernel, blocks_per_step, block_widt...  12.8 us
    dot_general x1, matrix products, on_device(): jnp.einsum('sjcd,jdf->sjcf', portion, up_weight, preferred_element_type=j...  12.7 us
    dot_general x1, matrix products, on_device(): jnp.einsum('sjcd,jdf->sjcf', portion, gate_weight, preferred_element_type...  10 us
  transfers between devices with their start and end apart: 3, of which 3 were waited for; matrix products, arithmetic and copies ran while one was open for 4% of the time, Pallas kernels for 0%

profile of v1, /device:TPU:1, one launch (start us, length us, event | category | flops | bytes accessed | tf_op | source)
XLA Modules:
  0.0 316.6 jit_solution(7939801569990296718)
XLA Ops:
  6.5 0.7 reshape.157
  7.3 0.9 reduce-window.14
  8.8 1.1 copy.91
  9.9 1.1 copy.96
  11.3 0.7 pad_maximum_fusion
  12.0 0.8 copy.104
  13.2 0.7 convert_element_type.52
  13.8 1.1 reduce-window.16
  15.6 1.1 copy.90
  16.7 0.7 multiply_add_fusion
  17.9 22.6 %all-gather.6.cloned.1.call-done = f32[24,136,128]{2,1,0:T(8,128)} async-done(((f32[3,136,128]{2,1,0:T(8,128)}), f32[24,136,128]{2,1,0:T(8,128)}) %all-gather.6.cloned.1.call-update) | async-done | bytes 1671184 | tf_op jit(solution)/shard_map/all_gather | solution.py:91
  40.5 0.9 slice.31
  41.7 1.6 fusion.7
  44.9 15.5 %all_to_all.10 = bf16[8,2,64,384]{3,2,1,0:T(8,128)(2,1)S(1)} all-to-all(bf16[8,2,64,384]{3,2,1,0:T(8,128)(2,1)S(1)} %bitcast.100), channel_id=1, replica_groups=mesh['seq'=8,'exp'=16] {'seq'}, dimensions={0} | all-to-all | bytes 1572864 | tf_op jit(solution)/shard_map/all_to_all | solution.py:138
  60.4 1.0 copy.108
  61.5 98.4 %all-gather.4.cloned.1.call-done = bf16[8,2,64,6144]{3,2,0,1:T(8,128)(2,1)} async-done(((bf16[8,2,64,384]{3,2,0,1:T(8,128)(2,1)}), bf16[8,2,64,6144]{3,2,0,1:T(8,128)(2,1)}) %all-gather.4.cloned.1.call-update) | async-done | bytes 12582928 | tf_op jit(solution)/shard_map/all_gather | solution.py:137
  159.9 12.7 %fusion.2 = f32[2,8,64,288]{3,2,0,1:T(8,128)} fusion(bf16[8,2,64,6144]{3,2,0,1:T(8,128)(2,1)} %all-gather.4.cloned.1.call-done, bf16[2,6144,288]{1,2,0:T(8,128)(2,1)} %param.20), kind=kOutput, calls=%fused_computation.2 | convolution fusion | flops 3623878656 | bytes 20840448 | tf_op jit(solution)/shard_map/sjcd,jdf->sjcf/dot_general | solution.py:146
  172.7 10.0 %fusion.9.h_ref = bf16[8,2,64,288]{3,2,1,0:T(8,128)(2,1)} fusion(f32[2,8,64,288]{3,2,0,1:T(8,128)} %fusion.2, bf16[2,6144,288]{1,2,0:T(8,128)(2,1)} %param.19, bf16[8,2,64,6144]{3,2,0,1:T(8,128)(2,1)S(1)} %copy-done.1), kind=kOutput, calls=%fused_computation.13 | convolution fusion | flops 3625648128 | bytes 21430272 | tf_op jit(solution)/shard_map/sjcd,jdf->sjcf/dot_general | solution.py:143
  182.7 12.8 %shard_map.109 = bf16[16,8,2,64,384]{4,3,2,1,0:T(8,128)(2,1)} custom-call(bf16[8,2,64,288]{3,2,1,0:T(8,128)(2,1)} %fusion.9.h_ref, bf16[2,288,6144]{2,1,0:T(8,128)(2,1)} %w_ref.1), custom_call_target="tpu_custom_call" | custom-call | flops 3623878656 | bytes 20250624 | tf_op jit(solution)/shard_map/pallas_call | solution.py:32
  195.6 7.9 %fusion.34 = f32[2,1,8,64]{3,1,2,0:T(1,128)S(1)} fusion(bf16[8,2,64,6144]{3,2,0,1:T(8,128)(2,1)} %all-gather.4.cloned.1.call-done, bf16[6144,2,1,1]{0,1,2,3:T(2,128)(2,1)S(1)} %bitcast.99), kind=kOutput, calls=%fused_computation.46 | convolution fusion | flops 12582912 | bytes 12611584 | tf_op jit(solution)/shard_map/sjcd,dj->sjc/dot_general | solution.py:147
  203.5 86.7 %reduce-scatter.4.cloned.1.call-done = bf16[1,8,2,64,384]{4,3,2,1,0:T(8,128)(2,1)} async-done(((bf16[16,8,2,64,384]{4,3,2,1,0:T(8,128)(2,1)}), bf16[1,8,2,64,384]{4,3,2,1,0:T(8,128)(2,1)}) %reduce-scatter.4.cloned.1.call-update) | async-done | bytes 786448
  290.2 1.3 fusion.8
  291.6 17.3 %all_to_all.11 = bf16[8,2,64,384]{3,2,1,0:T(8,128)(2,1)S(1)} all-to-all(bf16[8,2,64,384]{3,2,1,0:T(8,128)(2,1)S(1)} %fusion.8), channel_id=1, replica_groups=mesh['seq'=8,'exp'=16] {'seq'}, dimensions={0} | all-to-all | bytes 1572864 | tf_op jit(solution)/shard_map/all_to_all | solution.py:157
  308.9 1.1 fusion.22
  (54 shorter events, 4.3 us)
Async XLA Ops:
  6.5 189.0 %copy-start = (bf16[6144,2]{0,1:T(2,128)(2,1)S(1)}, bf16[6144,2]{0,1:T(2,128)(2,1)}, u32[]{:S(2)}) copy-start(bf16[6144,2]{0,1:T(2,128)(2,1)} %param.18) | copy-start | bytes 73732
  6.5 37.9 %copy-start.4 = (bf16[256,384]{1,0:T(8,128)(2,1)S(1)}, bf16[256,384]{1,0:T(8,128)(2,1)}, u32[]{:S(2)}) copy-start(bf16[256,384]{1,0:T(8,128)(2,1)} %param.15) | copy-start | bytes 589828
  6.5 33.9 %all-gather.6.cloned.1.call-start = ((), (), s32[]{:S(2)}) async-start(), calls=%async_computation.4 | async-start | bytes 1880064 | tf_op jit(solution)/shard_map/all_gather | solution.py:91
  12.0 147.9 %all-gather.4.cloned.1.call-start = ((), (), s32[]{:S(2)}) async-start(), calls=%async_computation.3 | async-start | bytes 13369344 | tf_op jit(solution)/shard_map/all_gather | solution.py:137
  17.9 43.7 %copy-start.2 = (bf16[1024,256]{1,0:T(8,128)(2,1)}, bf16[1024,256]{1,0:T(8,128)(2,1)S(1)}, u32[]{:S(2)}) copy-start(bf16[1024,256]{1,0:T(8,128)(2,1)S(1)} %fusion.23) | copy-start | bytes 1572868
  61.5 228.8 %reduce-scatter.4.cloned.1.call-start = ((), (), s32[]{:S(2)}) async-start(), calls=%async_computation.5 | async-start | bytes 13369344
  159.9 12.7 %copy-start.1 = (bf16[8,2,64,6144]{3,2,0,1:T(8,128)(2,1)S(1)}, bf16[8,2,64,6144]{3,2,0,1:T(8,128)(2,1)}, u32[]{:S(2)}) copy-start(bf16[8,2,64,6144]{3,2,0,1:T(8,128)(2,1)} %all-gather.4.cloned.1.call-done) | copy-start | bytes 37748740
  195.6 113.3 %copy-start.3 = (bf16[1024,256]{1,0:T(8,128)(2,1)S(1)}, bf16[1024,256]{1,0:T(8,128)(2,1)}, u32[]{:S(2)}) copy-start(bf16[1024,256]{1,0:T(8,128)(2,1)} %copy-done.2) | copy-start | bytes 1572868
Sparse Core Ops, SparseCore 0:
  12.1 28.3 all-gather.5
  61.6 98.2 all-gather.3
  195.7 94.5 reduce-scatter.3

commit v2 on v1

--- a/solution.py
+++ b/solution.py
@@ -130,35 +130,43 @@
         .reshape(expert_count * capacity, length, choices_per_token)
         .sum(axis=2)
     )
-    outgoing = jnp.dot(route_matrix, stream, preferred_element_type=jnp.float32).astype(
-        jnp.bfloat16
-    )
-    outgoing = outgoing.reshape(groups, experts_here, capacity, features)
-    portion = lax.all_gather(
-        lax.all_to_all(outgoing, "seq", split_axis=0, concat_axis=0, tiled=True),
-        "exp",
-        axis=3,
-        tiled=True,
-    )
-    gate_acc = jnp.einsum(
-        "sjcd,jdf->sjcf", portion, gate_weight, preferred_element_type=jnp.float32
-    )
-    upward = jnp.einsum("sjcd,jdf->sjcf", portion, up_weight, preferred_element_type=jnp.float32)
-    logits = jnp.einsum("sjcd,dj->sjc", portion, router_weight, preferred_element_type=jnp.float32)
-    hidden_act = (jax.nn.silu(gate_acc) * upward).astype(jnp.bfloat16)
     shards = lax.axis_size("exp")
-    expert_out = lax.psum_scatter(
-        down_projection(hidden_act, down_weight, shards),
-        "exp",
-        scatter_dimension=0,
-        tiled=True,
-    )[0].astype(jnp.float32)
-    routed = (jax.nn.sigmoid(logits)[..., None] * expert_out).astype(jnp.bfloat16)
-    returned = lax.all_to_all(routed, "seq", split_axis=0, concat_axis=0, tiled=True)
-    returned = returned.reshape(expert_count * capacity, features)
-    combined = lax.dot_general(
-        route_matrix, returned, (((0,), (0,)), ((), ())), preferred_element_type=jnp.float32
-    )
+    route_blocks = route_matrix.reshape(groups, experts_here, capacity, length)
+    combined = jnp.zeros((length, features), jnp.float32)
+    for j in range(experts_here):
+        route_j = route_blocks[:, j].reshape(groups * capacity, length)
+        outgoing = jnp.dot(route_j, stream, preferred_element_type=jnp.float32).astype(
+            jnp.bfloat16
+        )
+        outgoing = outgoing.reshape(groups, capacity, features)
+        portion = lax.all_gather(
+            lax.all_to_all(outgoing, "seq", split_axis=0, concat_axis=0, tiled=True),
+            "exp",
+            axis=2,
+            tiled=True,
+        )
+        gate_acc = jnp.einsum(
+            "scd,df->scf", portion, gate_weight[j], preferred_element_type=jnp.float32
+        )
+        upward = jnp.einsum(
+            "scd,df->scf", portion, up_weight[j], preferred_element_type=jnp.float32
+        )
+        logits = jnp.einsum(
+            "scd,d->sc", portion, router_weight[:, j], preferred_element_type=jnp.float32
+        )
+        hidden_act = (jax.nn.silu(gate_acc) * upward).astype(jnp.bfloat16)
+        expert_out = lax.psum_scatter(
+            down_projection(hidden_act[:, None], down_weight[j : j + 1], shards),
+            "exp",
+            scatter_dimension=0,
+            tiled=True,
+        )[0, :, 0].astype(jnp.float32)
+        routed = (jax.nn.sigmoid(logits)[..., None] * expert_out).astype(jnp.bfloat16)
+        returned = lax.all_to_all(routed, "seq", split_axis=0, concat_axis=0, tiled=True)
+        returned = returned.reshape(groups * capacity, features)
+        combined = combined + lax.dot_general(
+            route_j, returned, (((0,), (0,)), ((), ())), preferred_element_type=jnp.float32
+        )
     return (stream.astype(jnp.float32) + combined).astype(jnp.bfloat16)
 
 

time: 317 us -> 384 us (1.21)
  waiting for transfers between devices: 208 us -> 258 us
  starting transfers between devices: 0.09 us -> 12.7 us
  blocking collectives: 32.8 us -> 23.5 us
  local copies, waits for them, and re-layouts: 8.29 us -> 14.3 us
    unnamed x4 -> x7, waiting for transfers between devices: 86.7 us -> 131 us
    all_to_all x1 -> x0, blocking collectives: 17.3 us -> none  [on_device(): lax.all_to_all(routed, 'seq', split_axis=0, concat_axis=0, tiled=True)]
    all_to_all x0 -> x2, starting transfers between devices: none -> 12.3 us  [on_device(): lax.all_to_all(routed, 'seq', split_axis=0, concat_axis=0, tiled=True)]
    all_to_all x1 -> x2, blocking collectives: 15.5 us -> 23.5 us  [on_device(): lax.all_to_all(outgoing, 'seq', split_axis=0, concat_axis=0, tiled=True)]
    all_to_all x0 -> x2, waiting for transfers between devices: none -> 7.75 us  [on_device(): lax.all_to_all(routed, 'seq', split_axis=0, concat_axis=0, tiled=True)]
    slice x2 -> x4, local copies, waits for them, and re-layouts: 0.18 us -> 7.16 us  [the longest x1 6.95 us: on_device(): down_weight[j:j + 1]]
    dot_general x5 -> x10, matrix products: 32.3 us -> 35.8 us  [the longest x2 13.5 us: on_device(): jnp.einsum('scd,df->scf', portion, gate_weight[j], preferred_element_type...]
    all_gather x1 -> x2, waiting for transfers between devices: 98.4 us -> 95.8 us  [on_device(): lax.all_gather(lax.all_to_all(outgoing, 'seq', split_axis=0, concat_axis=...]
  transfers between devices with their start and end apart: 3 -> 7, of which waited for: 3 -> 6; matrix products, arithmetic and copies ran while one was open for 4% -> 13% of each run, Pallas kernels for 0% -> 4%
where the time goes in v2:
time: 384 us; the launch traced here: 383 us
  waiting for transfers between devices  258 us (67%)
  matrix products  36.9 us (10%)
  blocking collectives  23.5 us (6%)
  Pallas kernels  14.5 us (4%)
  local copies, waits for them, and re-layouts  14.3 us (4%)
  between operations  13.4 us (3%)
  starting transfers between devices  12.7 us (3%)
  other arithmetic  10.6 us (3%)
    unnamed x7, waiting for transfers between devices  131 us
    all_gather x2, waiting for transfers between devices, on_device(): lax.all_gather(lax.all_to_all(outgoing, 'seq', split_axis=0, concat_axis=...  95.8 us
    all_to_all x2, blocking collectives, on_device(): lax.all_to_all(outgoing, 'seq', split_axis=0, concat_axis=0, tiled=True)  23.5 us
    all_gather x1, waiting for transfers between devices, on_device(): gathered = lax.all_gather(packed, 'seq', axis=0)  22.6 us
    pallas_call x2, Pallas kernels, down_projection(): pl.pallas_call(functools.partial(down_kernel, blocks_per_step, block_widt...  14.5 us
    dot_general x2, matrix products, on_device(): jnp.einsum('scd,df->scf', portion, gate_weight[j], preferred_element_type...  13.5 us
    dot_general x2, matrix products, on_device(): jnp.einsum('scd,df->scf', portion, up_weight[j], preferred_element_type=j...  12.4 us
    all_to_all x2, starting transfers between devices, on_device(): lax.all_to_all(routed, 'seq', split_axis=0, concat_axis=0, tiled=True)  12.3 us
  transfers between devices with their start and end apart: 7, of which 6 were waited for; matrix products, arithmetic and copies ran while one was open for 13% of the time, Pallas kernels for 4%

profile of v2, /device:TPU:1, one launch (start us, length us, event | category | flops | bytes accessed | tf_op | source)
XLA Modules:
  0.0 383.5 jit_solution(16165812320547848480)
XLA Ops:
  13.8 1.1 reduce-window.16
  15.6 1.1 copy.82
  17.9 22.6 %all-gather.9.cloned.1.call-done = f32[24,136,128]{2,1,0:T(8,128)} async-done(((f32[3,136,128]{2,1,0:T(8,128)}), f32[24,136,128]{2,1,0:T(8,128)}) %all-gather.9.cloned.1.call-update) | async-done | bytes 1671184 | tf_op jit(solution)/shard_map/all_gather | solution.py:91
  41.7 1.6 fusion.13
  44.8 11.5 %all_to_all.20 = bf16[8,64,384]{2,1,0:T(8,128)(2,1)} all-to-all(bf16[8,64,384]{2,1,0:T(8,128)(2,1)S(1)} %bitcast.132), channel_id=1, replica_groups=mesh['seq'=8,'exp'=16] {'seq'}, dimensions={0} | all-to-all | bytes 786432 | tf_op jit(solution)/shard_map/all_to_all | solution.py:143
  56.6 12.0 %all_to_all.21 = bf16[8,64,384]{2,1,0:T(8,128)(2,1)} all-to-all(bf16[8,64,384]{2,1,0:T(8,128)(2,1)S(1)} %bitcast.133), channel_id=1, replica_groups=mesh['seq'=8,'exp'=16] {'seq'}, dimensions={0} | all-to-all | bytes 786432 | tf_op jit(solution)/shard_map/all_to_all | solution.py:143
  68.7 6.9 %fusion.63 = (bf16[1,288,6144]{2,1,0:T(8,128)(2,1)}, bf16[1,288,6144]{2,1,0:T(8,128)(2,1)}) fusion(bf16[2,288,6144]{2,1,0:T(8,128)(2,1)} %param.21), kind=kLoop, calls=%fused_computation.84 | loop fusion | bytes 14155776 | tf_op jit(solution)/shard_map/slice | solution.py:159
  75.7 47.0 %all-gather.5.cloned.1.call-done = bf16[8,64,6144]{2,1,0:T(8,128)(2,1)} async-done(((bf16[8,64,384]{2,1,0:T(8,128)(2,1)}), bf16[8,64,6144]{2,1,0:T(8,128)(2,1)}) %all-gather.5.cloned.1.call-update) | async-done | bytes 6291472 | tf_op jit(solution)/shard_map/all_gather | solution.py:142
  122.7 6.7 %fusion.6 = f32[8,64,288]{2,1,0:T(8,128)S(1)} fusion(bf16[8,64,6144]{2,1,0:T(8,128)(2,1)} %all-gather.5.cloned.1.call-done, bf16[2,6144,288]{1,2,0:T(8,128)(2,1)} %param.19), kind=kOutput, calls=%fused_computation.6 | convolution fusion | flops 1811939328 | bytes 10420224 | tf_op jit(solution)/shard_map/scd,df->scf/dot_general | solution.py:148
  129.5 6.2 %fusion.32.h_ref = bf16[8,1,64,288]{3,2,1,0:T(8,128)(2,1)} fusion(bf16[8,64,6144]{2,1,0:T(8,128)(2,1)S(1)} %copy-done, bf16[2,6144,288]{1,2,0:T(8,128)(2,1)} %param.20, f32[8,64,288]{2,1,0:T(8,128)S(1)} %fusion.6), kind=kOutput, calls=%fused_computation.31 | convolution fusion | flops 1812824064 | bytes 10715136 | tf_op jit(solution)/shard_map/scd,df->scf/dot_general | solution.py:151
  135.6 7.3 %shard_map.109 = bf16[16,8,1,64,384]{4,3,2,1,0:T(8,128)(2,1)} custom-call(bf16[8,1,64,288]{3,2,1,0:T(8,128)(2,1)} %fusion.32.h_ref, bf16[1,288,6144]{2,1,0:T(8,128)(2,1)} %get-tuple-element.6.w_ref), custom_call_target="tpu_custom_call" | custom-call | flops 1811939328 | bytes 10125312 | tf_op jit(solution)/shard_map/pallas_call | solution.py:32
  143.2 48.8 %all-gather.7.cloned.1.call-done = bf16[8,64,6144]{2,1,0:T(8,128)(2,1)} async-done(((bf16[8,64,384]{2,1,0:T(8,128)(2,1)}), bf16[8,64,6144]{2,1,0:T(8,128)(2,1)}) %all-gather.7.cloned.1.call-update) | async-done | bytes 6291472 | tf_op jit(solution)/shard_map/all_gather | solution.py:142
  192.0 6.7 %fusion.2 = f32[8,64,288]{2,1,0:T(8,128)S(1)} fusion(bf16[8,64,6144]{2,1,0:T(8,128)(2,1)} %all-gather.7.cloned.1.call-done, bf16[2,6144,288]{1,2,0:T(8,128)(2,1)} %param.19), kind=kOutput, calls=%fused_computation.2 | convolution fusion | flops 1811939328 | bytes 10420224 | tf_op jit(solution)/shard_map/scd,df->scf/dot_general | solution.py:148
  198.7 6.2 %fusion.35.h_ref = bf16[8,1,64,288]{3,2,1,0:T(8,128)(2,1)} fusion(bf16[8,64,6144]{2,1,0:T(8,128)(2,1)S(1)} %copy-done.1, bf16[2,6144,288]{1,2,0:T(8,128)(2,1)} %param.20, f32[8,64,288]{2,1,0:T(8,128)S(1)} %fusion.2), kind=kOutput, calls=%fused_computation.32 | convolution fusion | flops 1812824064 | bytes 10715136 | tf_op jit(solution)/shard_map/scd,df->scf/dot_general | solution.py:151
  204.9 7.2 %shard_map.110 = bf16[16,8,1,64,384]{4,3,2,1,0:T(8,128)(2,1)} custom-call(bf16[8,1,64,288]{3,2,1,0:T(8,128)(2,1)} %fusion.35.h_ref, bf16[1,288,6144]{2,1,0:T(8,128)(2,1)} %get-tuple-element.5.w_ref), custom_call_target="tpu_custom_call" | custom-call | flops 1811939328 | bytes 10125312 | tf_op jit(solution)/shard_map/pallas_call | solution.py:32
  212.2 5.5 %fusion.57 = f32[1,8,64]{2,0,1:T(1,128)S(1)} fusion(bf16[8,64,6144]{2,1,0:T(8,128)(2,1)} %all-gather.5.cloned.1.call-done, bf16[6144,2]{0,1:T(2,128)(2,1)S(1)} %copy-done.3), kind=kOutput, calls=%fused_computation.65 | convolution fusion | flops 6291456 | bytes 6318080 | tf_op jit(solution)/shard_map/scd,d->sc/dot_general | solution.py:154
  217.8 2.5 fusion.55
  220.3 55.5 %reduce-scatter.7.cloned.1.call-done = bf16[1,8,1,64,384]{4,3,2,1,0:T(8,128)(2,1)} async-done(((bf16[16,8,1,64,384]{4,3,2,1,0:T(8,128)(2,1)}), bf16[1,8,1,64,384]{4,3,2,1,0:T(8,128)(2,1)}) %reduce-scatter.7.cloned.1.call-update) | async-done | bytes 393232
  275.8 1.9 fusion.41
  277.7 6.2 %all-to-all-start.1 = ((bf16[8,64,384]{2,1,0:T(8,128)(2,1)}), bf16[8,64,384]{2,1,0:T(8,128)(2,1)S(1)}, u32[]{:S(2)}, u32[]{:S(2)}) async-start(bf16[8,64,384]{2,1,0:T(8,128)(2,1)} %fusion.41), calls=%async_computation.1 | async-start | bytes 786432 | tf_op jit(solution)/shard_map/all_to_all | solution.py:165
  283.9 75.9 %reduce-scatter.9.cloned.1.call-done = bf16[1,8,1,64,384]{4,3,2,1,0:T(8,128)(2,1)} async-done(((bf16[16,8,1,64,384]{4,3,2,1,0:T(8,128)(2,1)}), bf16[1,8,1,64,384]{4,3,2,1,0:T(8,128)(2,1)}) %reduce-scatter.9.cloned.1.call-update) | async-done | bytes 393232
  359.8 1.9 fusion.40
  361.7 6.2 %all-to-all-start.3 = ((bf16[8,64,384]{2,1,0:T(8,128)(2,1)}), bf16[8,64,384]{2,1,0:T(8,128)(2,1)S(1)}, u32[]{:S(2)}, u32[]{:S(2)}) async-start(bf16[8,64,384]{2,1,0:T(8,128)(2,1)} %fusion.40), calls=%async_computation.3 | async-start | bytes 786432 | tf_op jit(solution)/shard_map/all_to_all | solution.py:165
  368.2 7.8 %all-to-all-done.3 = bf16[8,64,384]{2,1,0:T(8,128)(2,1)S(1)} async-done(((bf16[8,64,384]{2,1,0:T(8,128)(2,1)}), bf16[8,64,384]{2,1,0:T(8,128)(2,1)S(1)}, u32[]{:S(2)}, u32[]{:S(2)}) %all-to-all-start.3) | async-done | bytes 393248 | tf_op jit(solution)/shard_map/all_to_all | solution.py:165
  (76 shorter events, 13.7 us)
Async XLA Ops:
  6.5 37.9 %copy-start.2 = (bf16[256,384]{1,0:T(8,128)(2,1)S(1)}, bf16[256,384]{1,0:T(8,128)(2,1)}, u32[]{:S(2)}) copy-start(bf16[256,384]{1,0:T(8,128)(2,1)} %param.15) | copy-start | bytes 589828
  6.5 33.9 %all-gather.9.cloned.1.call-start = ((), (), s32[]{:S(2)}) async-start(), calls=%async_computation.8 | async-start | bytes 1880064 | tf_op jit(solution)/shard_map/all_gather | solution.py:91
  12.0 110.7 %all-gather.5.cloned.1.call-start = ((), (), s32[]{:S(2)}) async-start(), calls=%async_computation.6 | async-start | bytes 6684672 | tf_op jit(solution)/shard_map/all_gather | solution.py:142
  56.3 135.7 %all-gather.7.cloned.1.call-start = ((), (), s32[]{:S(2)}) async-start(), calls=%async_computation.7 | async-start | bytes 6684672 | tf_op jit(solution)/shard_map/all_gather | solution.py:142
  68.7 207.1 %reduce-scatter.7.cloned.1.call-start = ((), (), s32[]{:S(2)}) async-start(), calls=%async_computation.9 | async-start | bytes 6684672
  122.7 6.7 %copy-start = (bf16[8,64,6144]{2,1,0:T(8,128)(2,1)S(1)}, bf16[8,64,6144]{2,1,0:T(8,128)(2,1)}, u32[]{:S(2)}) copy-start(bf16[8,64,6144]{2,1,0:T(8,128)(2,1)} %all-gather.5.cloned.1.call-done) | copy-start | bytes 18874372
  142.9 216.9 %reduce-scatter.9.cloned.1.call-start = ((), (), s32[]{:S(2)}) async-start(), calls=%async_computation.10 | async-start | bytes 6684672
  192.0 6.7 %copy-start.1 = (bf16[8,64,6144]{2,1,0:T(8,128)(2,1)S(1)}, bf16[8,64,6144]{2,1,0:T(8,128)(2,1)}, u32[]{:S(2)}) copy-start(bf16[8,64,6144]{2,1,0:T(8,128)(2,1)} %all-gather.7.cloned.1.call-done) | copy-start | bytes 18874372
  204.9 7.3 %copy-start.3 = (bf16[6144,2]{0,1:T(2,128)(2,1)S(1)}, bf16[6144,2]{0,1:T(2,128)(2,1)}, u32[]{:S(2)}) copy-start(bf16[6144,2]{0,1:T(2,128)(2,1)} %param.18) | copy-start | bytes 73732
  212.1 5.6 %slice-start = ((s8[6291456]{0:T(1024)(128)(4,1)}), s8[2097152]{0:T(1024)(128)(4,1)S(1)}, s32[]{:S(2)}) async-start(s8[6291456]{0:T(1024)(128)(4,1)} %bitcast.122), calls=%async_computation.11 | async-start | bytes 4194304
  212.2 5.6 %slice-start.1 = ((s8[6291456]{0:T(1024)(128)(4,1)}), s8[4194304]{0:T(1024)(128)(4,1)S(1)}, s32[]{:S(2)}) async-start(s8[6291456]{0:T(1024)(128)(4,1)} %bitcast.122), calls=%async_computation.12 | async-start | bytes 8388608
  277.7 84.0 %all-to-all-start.1 = ((bf16[8,64,384]{2,1,0:T(8,128)(2,1)}), bf16[8,64,384]{2,1,0:T(8,128)(2,1)S(1)}, u32[]{:S(2)}, u32[]{:S(2)}) async-start(bf16[8,64,384]{2,1,0:T(8,128)(2,1)} %fusion.41), calls=%async_computation.1 | async-start | bytes 786432 | tf_op jit(solution)/shard_map/all_to_all | solution.py:165
  361.7 14.2 %all-to-all-start.3 = ((bf16[8,64,384]{2,1,0:T(8,128)(2,1)}), bf16[8,64,384]{2,1,0:T(8,128)(2,1)S(1)}, u32[]{:S(2)}, u32[]{:S(2)}) async-start(bf16[8,64,384]{2,1,0:T(8,128)(2,1)} %fusion.40), calls=%async_computation.3 | async-start | bytes 786432 | tf_op jit(solution)/shard_map/all_to_all | solution.py:165
Sparse Core Ops, SparseCore 0:
  12.1 28.3 all-gather.8
  56.4 66.2 all-gather.4
  124.8 67.0 all-gather.6
  195.2 80.4 reduce-scatter.6
  279.1 80.7 reduce-scatter.8

commit v3 on v1

--- a/solution.py
+++ b/solution.py
@@ -134,19 +134,26 @@
         jnp.bfloat16
     )
     outgoing = outgoing.reshape(groups, experts_here, capacity, features)
+    shards = lax.axis_size("exp")
     portion = lax.all_gather(
         lax.all_to_all(outgoing, "seq", split_axis=0, concat_axis=0, tiled=True),
         "exp",
-        axis=3,
-        tiled=True,
+        axis=0,
     )
+    hidden_units = gate_weight.shape[2]
+    gate_blocks = gate_weight.reshape(experts_here, shards, features, hidden_units)
+    up_blocks = up_weight.reshape(experts_here, shards, features, hidden_units)
+    router_blocks = router_weight.reshape(shards, features, experts_here)
     gate_acc = jnp.einsum(
-        "sjcd,jdf->sjcf", portion, gate_weight, preferred_element_type=jnp.float32
+        "esjcd,jedf->sjcf", portion, gate_blocks, preferred_element_type=jnp.float32
     )
-    upward = jnp.einsum("sjcd,jdf->sjcf", portion, up_weight, preferred_element_type=jnp.float32)
-    logits = jnp.einsum("sjcd,dj->sjc", portion, router_weight, preferred_element_type=jnp.float32)
+    upward = jnp.einsum(
+        "esjcd,jedf->sjcf", portion, up_blocks, preferred_element_type=jnp.float32
+    )
+    logits = jnp.einsum(
+        "esjcd,edj->sjc", portion, router_blocks, preferred_element_type=jnp.float32
+    )
     hidden_act = (jax.nn.silu(gate_acc) * upward).astype(jnp.bfloat16)
-    shards = lax.axis_size("exp")
     expert_out = lax.psum_scatter(
         down_projection(hidden_act, down_weight, shards),
         "exp",

time: 317 us -> 307 us (0.968)
  waiting for transfers between devices: 208 us -> 185 us
  local copies, waits for them, and re-layouts: 8.29 us -> 20.7 us
    all_gather x1, waiting for transfers between devices: 98.4 us -> 76.7 us  [on_device(): lax.all_gather(lax.all_to_all(outgoing, 'seq', split_axis=0, concat_axis=...]
    unnamed x17 -> x24, local copies, waits for them, and re-layouts: 4.25 us -> 17.7 us
  transfers between devices with their start and end apart: 3 -> 3, of which waited for: 3 -> 3; matrix products, arithmetic and copies ran while one was open for 4% -> 9% of each run, Pallas kernels for 0% -> 0%
where the time goes in v3:
time: 307 us
  waiting for transfers between devices  185 us (60%)
  blocking collectives  32.9 us (11%)
  matrix products  32.2 us (10%)
  local copies, waits for them, and re-layouts  20.7 us (7%)
  between operations  13.3 us (4%)
  Pallas kernels  12.8 us (4%)
  other arithmetic  9.53 us (3%)
    unnamed x4, waiting for transfers between devices  85.5 us
    all_gather x1, waiting for transfers between devices, on_device(): lax.all_gather(lax.all_to_all(outgoing, 'seq', split_axis=0, concat_axis=...  76.7 us
    all_gather x1, waiting for transfers between devices, on_device(): gathered = lax.all_gather(packed, 'seq', axis=0)  22.6 us
    unnamed x24, local copies, waits for them, and re-layouts  17.7 us
    all_to_all x1, blocking collectives, on_device(): lax.all_to_all(routed, 'seq', split_axis=0, concat_axis=0, tiled=True)  17.3 us
    all_to_all x1, blocking collectives, on_device(): lax.all_to_all(outgoing, 'seq', split_axis=0, concat_axis=0, tiled=True)  15.6 us
    pallas_call x1, Pallas kernels, down_projection(): pl.pallas_call(functools.partial(down_kernel, blocks_per_step, block_widt...  12.8 us
    dot_general x1, matrix products, on_device(): jnp.einsum('esjcd,jedf->sjcf', portion, gate_blocks, preferred_element_ty...  11.9 us
  transfers between devices with their start and end apart: 3, of which 3 were waited for; matrix products, arithmetic and copies ran while one was open for 9% of the time, Pallas kernels for 0%

profile of v3, /device:TPU:1, one launch (start us, length us, event | category | flops | bytes accessed | tf_op | source)
XLA Modules:
  0.0 306.7 jit_solution(4207095889538538993)
XLA Ops:
  6.5 0.7 reshape.166
  7.3 0.9 reduce-window.14
  8.8 1.1 copy.99
  9.9 1.1 copy.104
  12.0 0.8 copy.112
  13.8 1.1 reduce-window.16
  15.6 1.1 copy.98
  17.9 22.6 %all-gather.5.cloned.1.call-done = f32[24,136,128]{2,1,0:T(8,128)} async-done(((f32[3,136,128]{2,1,0:T(8,128)}), f32[24,136,128]{2,1,0:T(8,128)}) %all-gather.5.cloned.1.call-update) | async-done | bytes 1671184 | tf_op jit(solution)/shard_map/all_gather | solution.py:91
  40.5 0.9 slice.31
  41.7 1.6 fusion.9
  44.9 15.6 %all_to_all.10 = bf16[8,2,64,384]{3,2,1,0:T(8,128)(2,1)} all-to-all(bf16[8,2,64,384]{3,2,1,0:T(8,128)(2,1)S(1)} %bitcast.123), channel_id=1, replica_groups=mesh['seq'=8,'exp'=16] {'seq'}, dimensions={0} | all-to-all | bytes 1572864 | tf_op jit(solution)/shard_map/all_to_all | solution.py:139
  60.8 7.9 %copy.139 = bf16[72,8,16,384]{3,2,1,0:T(8,128)(2,1)} copy(bf16[72,8,16,384]{3,1,2,0:T(8,128)(2,1)} %bitcast.117) | data formatting | bytes 14155776
  68.7 4.8 %copy.140 = bf16[72,8,16,384]{3,2,1,0:T(8,128)(2,1)} copy(bf16[72,8,16,384]{3,1,2,0:T(8,128)(2,1)S(1)} %bitcast.120) | data formatting | bytes 14155776
  73.5 76.7 %all-gather.7.cloned.1.call-done = bf16[128,2,64,384]{3,2,1,0:T(8,128)(2,1)} async-done(((bf16[8,2,64,384]{3,2,1,0:T(8,128)(2,1)}), bf16[128,2,64,384]{3,2,1,0:T(8,128)(2,1)}) %all-gather.7.cloned.1.call-update) | async-done | bytes 12582928 | tf_op jit(solution)/shard_map/all_gather | solution.py:138
  150.3 11.9 %fusion = f32[2,8,64,288,1]{3,2,1,0,4:T(8,128)S(1)} fusion(bf16[16,8,2,64,384]{4,3,2,1,0:T(8,128)(2,1)} %bitcast.142, bf16[2,16,384,288,1]{2,1,3,0,4:T(8,128)(2,1)} %bitcast.122), kind=kOutput, calls=%fused_computation | convolution fusion | flops 3623878656 | bytes 20840448 | tf_op jit(solution)/shard_map/esjcd,jedf->sjcf/dot_general | solution.py:147
  162.2 9.7 %fusion.15 = f32[2,8,64,288]{3,2,1,0:T(8,128)S(1)} fusion(bf16[2,16,384,288,1]{2,1,3,0,4:T(8,128)(2,1)S(1)} %bitcast.121, bf16[16,8,2,64,384]{4,3,2,1,0:T(8,128)(2,1)} %bitcast.143), kind=kOutput, calls=%fused_computation.21 | convolution fusion | flops 3623878656 | bytes 20840448 | tf_op jit(solution)/shard_map/esjcd,jedf->sjcf/dot_general | solution.py:150
  171.9 1.4 fusion.11.h_ref
  173.3 12.8 %shard_map.109 = bf16[16,8,2,64,384]{4,3,2,1,0:T(8,128)(2,1)} custom-call(bf16[8,2,64,288]{3,2,1,0:T(8,128)(2,1)} %fusion.11.h_ref, bf16[2,288,6144]{2,1,0:T(8,128)(2,1)} %w_ref.1), custom_call_target="tpu_custom_call" | custom-call | flops 3623878656 | bytes 20250624 | tf_op jit(solution)/shard_map/pallas_call | solution.py:32
  186.1 0.7 copy-done.4
  186.9 7.9 %fusion.2 = f32[2,1,8,64,1]{3,1,2,0,4:T(1,128)S(1)} fusion(bf16[16,8,2,64,384]{4,3,2,1,0:T(8,128)(2,1)} %bitcast.144, bf16[16,384,2,1,1]{1,0,2,3,4:T(8,128)(2,1)S(1)} %bitcast.135), kind=kOutput, calls=%fused_computation.2 | convolution fusion | flops 12582912 | bytes 12611584 | tf_op jit(solution)/shard_map/esjcd,edj->sjc/dot_general | solution.py:153
  194.8 85.5 %reduce-scatter.4.cloned.1.call-done = bf16[1,8,2,64,384]{4,3,2,1,0:T(8,128)(2,1)} async-done(((bf16[16,8,2,64,384]{4,3,2,1,0:T(8,128)(2,1)}), bf16[1,8,2,64,384]{4,3,2,1,0:T(8,128)(2,1)}) %reduce-scatter.4.cloned.1.call-update) | async-done | bytes 786448
  280.3 1.3 fusion.10
  281.6 17.3 %all_to_all.11 = bf16[8,2,64,384]{3,2,1,0:T(8,128)(2,1)S(1)} all-to-all(bf16[8,2,64,384]{3,2,1,0:T(8,128)(2,1)S(1)} %fusion.10), channel_id=1, replica_groups=mesh['seq'=8,'exp'=16] {'seq'}, dimensions={0} | all-to-all | bytes 1572864 | tf_op jit(solution)/shard_map/all_to_all | solution.py:164
  299.0 1.1 fusion.25
  (62 shorter events, 6.6 us)
Async XLA Ops:
  6.5 37.9 %copy-start.3 = (bf16[256,384]{1,0:T(8,128)(2,1)S(1)}, bf16[256,384]{1,0:T(8,128)(2,1)}, u32[]{:S(2)}) copy-start(bf16[256,384]{1,0:T(8,128)(2,1)} %param.15) | copy-start | bytes 589828
  6.5 33.9 %all-gather.5.cloned.1.call-start = ((), (), s32[]{:S(2)}) async-start(), calls=%async_computation.3 | async-start | bytes 1880064 | tf_op jit(solution)/shard_map/all_gather | solution.py:91
  12.0 138.3 %all-gather.7.cloned.1.call-start = ((), (), s32[]{:S(2)}) async-start(), calls=%async_computation.4 | async-start | bytes 13369344 | tf_op jit(solution)/shard_map/all_gather | solution.py:138
  44.5 16.1 %copy-start.1 = (bf16[256,384]{1,0:T(8,128)(2,1)}, bf16[256,384]{1,0:T(8,128)(2,1)S(1)}, u32[]{:S(2)}) copy-start(bf16[256,384]{1,0:T(8,128)(2,1)S(1)} %add_convert_fusion) | copy-start | bytes 589828
  60.5 8.2 %slice-start = ((s8[7077888]{0:T(1024)(128)(4,1)}), s8[2883584]{0:T(1024)(128)(4,1)S(1)}, s32[]{:S(2)}) async-start(s8[7077888]{0:T(1024)(128)(4,1)} %bitcast.118), calls=%async_computation.6 | async-start | bytes 5767168
  60.6 219.7 %reduce-scatter.4.cloned.1.call-start = ((), (), s32[]{:S(2)}) async-start(), calls=%async_computation.5 | async-start | bytes 13369344
  60.8 7.9 %slice-start.1 = ((s8[7077888]{0:T(1024)(128)(4,1)}), s8[4194304]{0:T(1024)(128)(4,1)S(1)}, s32[]{:S(2)}) async-start(s8[7077888]{0:T(1024)(128)(4,1)} %bitcast.118), calls=%async_computation.7 | async-start | bytes 8388608
  150.3 11.9 %copy-start = (bf16[72,8,16,384]{3,2,1,0:T(8,128)(2,1)S(1)}, bf16[72,8,16,384]{3,2,1,0:T(8,128)(2,1)}, u32[]{:S(2)}) copy-start(bf16[72,8,16,384]{3,2,1,0:T(8,128)(2,1)} %copy.140) | copy-start | bytes 21233668
  186.1 0.7 copy-start.4
  186.9 112.1 %copy-start.2 = (bf16[256,384]{1,0:T(8,128)(2,1)S(1)}, bf16[256,384]{1,0:T(8,128)(2,1)}, u32[]{:S(2)}) copy-start(bf16[256,384]{1,0:T(8,128)(2,1)} %copy-done.1) | copy-start | bytes 589828
Sparse Core Ops, SparseCore 0:
  12.1 28.3 all-gather.4
  60.7 89.5 all-gather.6
  186.3 93.9 reduce-scatter.3

commit v4 on v3

--- a/solution.py
+++ b/solution.py
@@ -51,6 +51,52 @@
     )(hidden_act, down_weight)
 
 
+def exchange_kernel(x_ref, o_ref, send_sem, recv_sem, local_sem):
+    n = x_ref.shape[0]
+    me = lax.axis_index("seq")
+    col = lax.axis_index("exp")
+    mesh_id = pl.DeviceIdType.MESH
+    barrier = pltpu.get_barrier_semaphore()
+    for k in range(1, n):
+        peer = lax.rem(me + k, n)
+        pl.semaphore_signal(barrier, inc=1, device_id=(peer, col), device_id_type=mesh_id)
+    pl.semaphore_wait(barrier, n - 1)
+    local = pltpu.make_async_copy(x_ref.at[me], o_ref.at[me], local_sem)
+    local.start()
+    copies = []
+    for k in range(1, n):
+        peer = lax.rem(me + k, n)
+        copy = pltpu.make_async_remote_copy(
+            src_ref=x_ref.at[peer],
+            dst_ref=o_ref.at[me],
+            send_sem=send_sem.at[k],
+            recv_sem=recv_sem.at[k],
+            device_id=(peer, col),
+            device_id_type=mesh_id,
+        )
+        copy.start()
+        copies.append(copy)
+    local.wait()
+    for copy in copies:
+        copy.wait()
+
+
+def exchange(x, collective_id):
+    n = x.shape[0]
+    return pl.pallas_call(
+        exchange_kernel,
+        out_shape=jax.ShapeDtypeStruct(x.shape, x.dtype),
+        in_specs=[pl.BlockSpec(memory_space=pltpu.VMEM)],
+        out_specs=pl.BlockSpec(memory_space=pltpu.VMEM),
+        scratch_shapes=[
+            pltpu.SemaphoreType.DMA((n,)),
+            pltpu.SemaphoreType.DMA((n,)),
+            pltpu.SemaphoreType.DMA,
+        ],
+        compiler_params=pltpu.CompilerParams(collective_id=collective_id, has_side_effects=True),
+    )(x)
+
+
 def on_device(
     attn_query,
     attn_key,
@@ -136,7 +182,7 @@
     outgoing = outgoing.reshape(groups, experts_here, capacity, features)
     shards = lax.axis_size("exp")
     portion = lax.all_gather(
-        lax.all_to_all(outgoing, "seq", split_axis=0, concat_axis=0, tiled=True),
+        exchange(outgoing, 0),
         "exp",
         axis=0,
     )
@@ -161,7 +207,7 @@
         tiled=True,
     )[0].astype(jnp.float32)
     routed = (jax.nn.sigmoid(logits)[..., None] * expert_out).astype(jnp.bfloat16)
-    returned = lax.all_to_all(routed, "seq", split_axis=0, concat_axis=0, tiled=True)
+    returned = exchange(routed, 1)
     returned = returned.reshape(expert_count * capacity, features)
     combined = lax.dot_general(
         route_matrix, returned, (((0,), (0,)), ((), ())), preferred_element_type=jnp.float32

time: 307 us -> 308 us (level)
  blocking collectives: 32.9 us -> 0 us
  Pallas kernels: 12.8 us -> 43.9 us
    all_to_all x2 -> x0, blocking collectives: 32.9 us -> none  [the longest x1 17.3 us: on_device(): lax.all_to_all(routed, 'seq', split_axis=0, concat_axis=0, tiled=True)]
    pallas_call x0 -> x2, Pallas kernels: none -> 31.1 us  [exchange(): pl.pallas_call(exchange_kernel, out_shape=jax.ShapeDtypeStruct(x.shape, x...]
where the time goes in v4:
time: 308 us; the launch traced here: 307 us
  waiting for transfers between devices  185 us (60%)
  Pallas kernels  43.9 us (14%)
  matrix products  34.2 us (11%)
  local copies, waits for them, and re-layouts  20.7 us (7%)
  between operations  13.4 us (4%)
  other arithmetic  10.4 us (3%)
    unnamed x4, waiting for transfers between devices  85.3 us
    all_gather x1, waiting for transfers between devices, on_device(): portion = lax.all_gather(exchange(outgoing, 0), 'exp', axis=0)  76.6 us
    pallas_call x2, Pallas kernels, exchange(): pl.pallas_call(exchange_kernel, out_shape=jax.ShapeDtypeStruct(x.shape, x...  31.1 us
    all_gather x1, waiting for transfers between devices, on_device(): gathered = lax.all_gather(packed, 'seq', axis=0)  22.6 us
    unnamed x24, local copies, waits for them, and re-layouts  17.7 us
    pallas_call x1, Pallas kernels, down_projection(): pl.pallas_call(functools.partial(down_kernel, blocks_per_step, block_widt...  12.8 us
    dot_general x1, matrix products, on_device(): jnp.einsum('esjcd,jedf->sjcf', portion, gate_blocks, preferred_element_ty...  11.9 us
    dot_general x1, matrix products, on_device(): jnp.einsum('esjcd,jedf->sjcf', portion, up_blocks, preferred_element_type...  9.71 us
  transfers between devices with their start and end apart: 3, of which 3 were waited for; matrix products, arithmetic and copies ran while one was open for 9% of the time, Pallas kernels for 0%

profile of v4, /device:TPU:1, one launch (start us, length us, event | category | flops | bytes accessed | tf_op | source)
XLA Modules:
  0.0 307.5 jit_solution(13355604847854290286)
XLA Ops:
  6.5 0.7 reshape.166
  7.3 0.9 reduce-window.14
  8.8 1.1 copy.123
  9.9 1.1 copy.128
  12.0 0.8 copy.136
  13.8 1.1 reduce-window.16
  15.6 1.1 copy.122
  17.9 22.6 %all-gather.5.cloned.1.call-done = f32[24,136,128]{2,1,0:T(8,128)} async-done(((f32[3,136,128]{2,1,0:T(8,128)}), f32[24,136,128]{2,1,0:T(8,128)}) %all-gather.5.cloned.1.call-update) | async-done | bytes 1671184 | tf_op jit(solution)/shard_map/all_gather | solution.py:137
  40.5 0.9 slice.31
  41.7 1.6 fusion.9
  44.5 1.3 convolution_convert_fusion
  45.8 14.8 %shard_map.109 = bf16[8,2,64,384]{3,2,1,0:T(8,128)(2,1)} custom-call(bf16[8,2,64,384]{3,2,1,0:T(8,128)(2,1)} %bitcast.123), custom_call_target="tpu_custom_call" | custom-call | tf_op jit(solution)/shard_map/pallas_call | solution.py:86
  60.9 8.0 %copy.164 = bf16[72,8,16,384]{3,2,1,0:T(8,128)(2,1)} copy(bf16[72,8,16,384]{3,1,2,0:T(8,128)(2,1)} %bitcast.117) | data formatting | bytes 14155776
  68.9 4.7 %copy.165 = bf16[72,8,16,384]{3,2,1,0:T(8,128)(2,1)} copy(bf16[72,8,16,384]{3,1,2,0:T(8,128)(2,1)S(1)} %bitcast.120) | data formatting | bytes 14155776
  73.6 76.6 %all-gather.7.cloned.1.call-done = bf16[128,2,64,384]{3,2,1,0:T(8,128)(2,1)} async-done(((bf16[8,2,64,384]{3,2,1,0:T(8,128)(2,1)}), bf16[128,2,64,384]{3,2,1,0:T(8,128)(2,1)}) %all-gather.7.cloned.1.call-update) | async-done | bytes 12582928 | tf_op jit(solution)/shard_map/all_gather | solution.py:184
  150.2 11.9 %fusion.15 = f32[2,8,64,288]{3,2,1,0:T(8,128)S(1)} fusion(bf16[2,16,384,288,1]{2,1,3,0,4:T(8,128)(2,1)} %bitcast.122, bf16[16,8,2,64,384]{4,3,2,1,0:T(8,128)(2,1)} %bitcast.142), kind=kOutput, calls=%fused_computation.21 | convolution fusion | flops 3623878656 | bytes 20840448 | tf_op jit(solution)/shard_map/esjcd,jedf->sjcf/dot_general | solution.py:193
  162.2 9.7 %fusion.20 = f32[2,8,64,288]{3,2,1,0:T(8,128)S(1)} fusion(bf16[2,16,384,288,1]{2,1,3,0,4:T(8,128)(2,1)S(1)} %bitcast.121, bf16[16,8,2,64,384]{4,3,2,1,0:T(8,128)(2,1)} %bitcast.143), kind=kOutput, calls=%fused_computation.22 | convolution fusion | flops 3623878656 | bytes 20840448 | tf_op jit(solution)/shard_map/esjcd,jedf->sjcf/dot_general | solution.py:196
  171.9 1.4 fusion.11.h_ref
  173.3 12.8 %shard_map.110 = bf16[16,8,2,64,384]{4,3,2,1,0:T(8,128)(2,1)} custom-call(bf16[8,2,64,288]{3,2,1,0:T(8,128)(2,1)} %fusion.11.h_ref, bf16[2,288,6144]{2,1,0:T(8,128)(2,1)} %w_ref.1), custom_call_target="tpu_custom_call" | custom-call | flops 3623878656 | bytes 20250624 | tf_op jit(solution)/shard_map/pallas_call | solution.py:32
  186.9 7.9 %fusion.2 = f32[2,1,8,64,1]{3,1,2,0,4:T(1,128)S(1)} fusion(bf16[16,8,2,64,384]{4,3,2,1,0:T(8,128)(2,1)} %bitcast.144, bf16[16,384,2,1,1]{1,0,2,3,4:T(8,128)(2,1)S(1)} %bitcast.135), kind=kOutput, calls=%fused_computation.2 | convolution fusion | flops 12582912 | bytes 12611584 | tf_op jit(solution)/shard_map/esjcd,edj->sjc/dot_general | solution.py:199
  194.8 85.3 %reduce-scatter.4.cloned.1.call-done = bf16[1,8,2,64,384]{4,3,2,1,0:T(8,128)(2,1)} async-done(((bf16[16,8,2,64,384]{4,3,2,1,0:T(8,128)(2,1)}), bf16[1,8,2,64,384]{4,3,2,1,0:T(8,128)(2,1)}) %reduce-scatter.4.cloned.1.call-update) | async-done | bytes 786448
  280.1 2.2 fusion.10.x_ref
  282.3 16.3 %shard_map.111 = bf16[8,2,64,384]{3,2,1,0:T(8,128)(2,1)} custom-call(bf16[8,2,64,384]{3,2,1,0:T(8,128)(2,1)} %fusion.10.x_ref), custom_call_target="tpu_custom_call" | custom-call | tf_op jit(solution)/shard_map/pallas_call | solution.py:86
  298.6 2.3 fusion.30
  (62 shorter events, 6.9 us)
Async XLA Ops:
  6.5 37.9 %copy-start.3 = (bf16[256,384]{1,0:T(8,128)(2,1)S(1)}, bf16[256,384]{1,0:T(8,128)(2,1)}, u32[]{:S(2)}) copy-start(bf16[256,384]{1,0:T(8,128)(2,1)} %param.15) | copy-start | bytes 589828
  6.5 33.9 %all-gather.5.cloned.1.call-start = ((), (), s32[]{:S(2)}) async-start(), calls=%async_computation.1 | async-start | bytes 1880064 | tf_op jit(solution)/shard_map/all_gather | solution.py:137
  12.0 138.3 %all-gather.7.cloned.1.call-start = ((), (), s32[]{:S(2)}) async-start(), calls=%async_computation.2 | async-start | bytes 13369344 | tf_op jit(solution)/shard_map/all_gather | solution.py:184
  44.5 16.1 %copy-start.1 = (bf16[256,384]{1,0:T(8,128)(2,1)}, bf16[256,384]{1,0:T(8,128)(2,1)S(1)}, u32[]{:S(2)}) copy-start(bf16[256,384]{1,0:T(8,128)(2,1)S(1)} %add_convert_fusion) | copy-start | bytes 589828
  60.6 8.3 %slice-start = ((s8[7077888]{0:T(1024)(128)(4,1)}), s8[2883584]{0:T(1024)(128)(4,1)S(1)}, s32[]{:S(2)}) async-start(s8[7077888]{0:T(1024)(128)(4,1)} %bitcast.118), calls=%async_computation.4 | async-start | bytes 5767168
  60.7 219.5 %reduce-scatter.4.cloned.1.call-start = ((), (), s32[]{:S(2)}) async-start(), calls=%async_computation.3 | async-start | bytes 13369344
  60.9 8.0 %slice-start.1 = ((s8[7077888]{0:T(1024)(128)(4,1)}), s8[4194304]{0:T(1024)(128)(4,1)S(1)}, s32[]{:S(2)}) async-start(s8[7077888]{0:T(1024)(128)(4,1)} %bitcast.118), calls=%async_computation.5 | async-start | bytes 8388608
  150.2 11.9 %copy-start = (bf16[72,8,16,384]{3,2,1,0:T(8,128)(2,1)S(1)}, bf16[72,8,16,384]{3,2,1,0:T(8,128)(2,1)}, u32[]{:S(2)}) copy-start(bf16[72,8,16,384]{3,2,1,0:T(8,128)(2,1)} %copy.165) | copy-start | bytes 21233668
  186.1 0.7 copy-start.4
  186.9 111.7 %copy-start.2 = (bf16[256,384]{1,0:T(8,128)(2,1)S(1)}, bf16[256,384]{1,0:T(8,128)(2,1)}, u32[]{:S(2)}) copy-start(bf16[256,384]{1,0:T(8,128)(2,1)} %copy-done.1) | copy-start | bytes 589828
Sparse Core Ops, SparseCore 0:
  12.1 28.3 all-gather.4
  60.8 89.4 all-gather.6
  186.3 93.7 reduce-scatter.3

commit v5 on v4

--- a/solution.py
+++ b/solution.py
@@ -27,7 +27,7 @@
     sections, experts_here, capacity, hidden = hidden_act.shape
     features = down_weight.shape[2]
     block_width = features // shards
-    blocks_per_step = 4
+    blocks_per_step = 8
     steps = shards // blocks_per_step
     return pl.pallas_call(
         functools.partial(down_kernel, blocks_per_step, block_width),
@@ -190,12 +190,14 @@
     gate_blocks = gate_weight.reshape(experts_here, shards, features, hidden_units)
     up_blocks = up_weight.reshape(experts_here, shards, features, hidden_units)
     router_blocks = router_weight.reshape(shards, features, experts_here)
-    gate_acc = jnp.einsum(
-        "esjcd,jedf->sjcf", portion, gate_blocks, preferred_element_type=jnp.float32
-    )
-    upward = jnp.einsum(
-        "esjcd,jedf->sjcf", portion, up_blocks, preferred_element_type=jnp.float32
-    )
+    gate_up = jnp.einsum(
+        "esjcd,jedf->sjcf",
+        portion,
+        jnp.concatenate([gate_blocks, up_blocks], axis=3),
+        preferred_element_type=jnp.float32,
+    )
+    gate_acc = gate_up[..., :hidden_units]
+    upward = gate_up[..., hidden_units:]
     logits = jnp.einsum(
         "esjcd,edj->sjc", portion, router_blocks, preferred_element_type=jnp.float32
     )

time: 308 us -> 299 us (0.971)
  matrix products: 34.2 us -> 26.7 us
    unnamed x24 -> x12, local copies, waits for them, and re-layouts: 17.7 us -> 4.94 us
    reshape x1 -> x2, local copies, waits for them, and re-layouts: 0.74 us -> 11.2 us  [the longest x1 10.5 us: on_device(): up_blocks = up_weight.reshape(experts_here, shards, features, hidden_units)]
    dot_general x2 -> x1, matrix products: 21.6 us -> 14.2 us  [on_device(): jnp.einsum('esjcd,jedf->sjcf', portion, jnp.concatenate([gate_blocks, up_...]
  transfers between devices with their start and end apart: 3 -> 3, of which waited for: 3 -> 3; matrix products, arithmetic and copies ran while one was open for 9% -> 8% of each run, Pallas kernels for 0% -> 0%
where the time goes in v5:
time: 299 us
  waiting for transfers between devices  187 us (63%)
  Pallas kernels  42.7 us (14%)
  matrix products  26.7 us (9%)
  local copies, waits for them, and re-layouts  18.4 us (6%)
  between operations  13.3 us (4%)
  other arithmetic  10.6 us (4%)
    unnamed x4, waiting for transfers between devices  85.4 us
    all_gather x1, waiting for transfers between devices, on_device(): portion = lax.all_gather(exchange(outgoing, 0), 'exp', axis=0)  79.1 us
    pallas_call x2, Pallas kernels, exchange(): pl.pallas_call(exchange_kernel, out_shape=jax.ShapeDtypeStruct(x.shape, x...  31.1 us
    all_gather x1, waiting for transfers between devices, on_device(): gathered = lax.all_gather(packed, 'seq', axis=0)  22.6 us
    dot_general x1, matrix products, on_device(): jnp.einsum('esjcd,jedf->sjcf', portion, jnp.concatenate([gate_blocks, up_...  14.2 us
    pallas_call x1, Pallas kernels, down_projection(): pl.pallas_call(functools.partial(down_kernel, blocks_per_step, block_widt...  11.5 us
    reshape x1, local copies, waits for them, and re-layouts, on_device(): up_blocks = up_weight.reshape(experts_here, shards, features, hidden_units)  10.5 us
    dot_general x1, matrix products, on_device(): jnp.einsum('esjcd,edj->sjc', portion, router_blocks, preferred_element_ty...  7.86 us
  transfers between devices with their start and end apart: 3, of which 3 were waited for; matrix products, arithmetic and copies ran while one was open for 8% of the time, Pallas kernels for 0%

profile of v5, /device:TPU:1, one launch (start us, length us, event | category | flops | bytes accessed | tf_op | source)
XLA Modules:
  0.0 298.8 jit_solution(863999900744207448)
XLA Ops:
  6.5 0.7 reshape.166
  7.3 0.9 reduce-window.14
  8.8 1.1 copy.115
  9.9 1.1 copy.120
  11.3 0.7 pad_maximum_fusion
  12.0 0.8 copy.128
  13.1 1.1 copy.114
  14.9 1.1 reduce-window.16
  17.9 22.6 %all-gather.5.cloned.1.call-done = f32[24,136,128]{2,1,0:T(8,128)} async-done(((f32[3,136,128]{2,1,0:T(8,128)}), f32[24,136,128]{2,1,0:T(8,128)}) %all-gather.5.cloned.1.call-update) | async-done | bytes 1671184 | tf_op jit(solution)/shard_map/all_gather | solution.py:137
  40.5 0.9 slice.39
  41.7 1.6 fusion.11
  44.5 1.3 convolution_convert_fusion
  45.8 14.8 %shard_map.109 = bf16[8,2,64,384]{3,2,1,0:T(8,128)(2,1)} custom-call(bf16[8,2,64,384]{3,2,1,0:T(8,128)(2,1)} %bitcast.97), custom_call_target="tpu_custom_call" | custom-call | tf_op jit(solution)/shard_map/pallas_call | solution.py:86
  60.7 10.5 %copy_bitcast_fusion = (bf16[2,16,384,288]{2,3,1,0:T(8,128)(2,1)}, bf16[2,16,384,288]{2,3,1,0:T(8,128)(2,1)}) fusion(bf16[2,36,16,8,384]{4,3,2,1,0:T(8,128)(2,1)} %bitcast.95, bf16[2,36,16,8,384]{4,3,2,1,0:T(8,128)(2,1)} %bitcast.96), kind=kLoop, calls=%fused_computation.7 | loop fusion | bytes 28311552 | tf_op jit(solution)/shard_map/reshape | solution.py:191
  71.1 79.1 %all-gather.7.cloned.1.call-done = bf16[128,2,64,384]{3,2,1,0:T(8,128)(2,1)} async-done(((bf16[8,2,64,384]{3,2,1,0:T(8,128)(2,1)}), bf16[128,2,64,384]{3,2,1,0:T(8,128)(2,1)}) %all-gather.7.cloned.1.call-update) | async-done | bytes 12582928 | tf_op jit(solution)/shard_map/all_gather | solution.py:184
  150.2 14.2 %fusion.7 = f32[8,2,64,576]{3,2,1,0:T(8,128)S(1)} fusion(bf16[16,8,2,64,384]{4,3,2,1,0:T(8,128)(2,1)} %bitcast.116, bf16[2,16,384,288]{2,3,1,0:T(8,128)(2,1)} %get-tuple-element.9, bf16[2,16,384,288]{2,3,1,0:T(8,128)(2,1)} %get-tuple-element.10), kind=kOutput, calls=%fused_computation.11 | convolution fusion | flops 7276068864 | bytes 29097984 | tf_op jit(solution)/shard_map/esjcd,jedf->sjcf/dot_general | solution.py:193
  164.4 1.5 fusion.10.h_ref
  165.9 11.5 %shard_map.110 = bf16[16,8,2,64,384]{4,3,2,1,0:T(8,128)(2,1)} custom-call(bf16[8,2,64,288]{3,2,1,0:T(8,128)(2,1)} %fusion.10.h_ref, bf16[2,288,6144]{2,1,0:T(8,128)(2,1)} %w_ref.1), custom_call_target="tpu_custom_call" | custom-call | flops 3623878656 | bytes 20250624 | tf_op jit(solution)/shard_map/pallas_call | solution.py:32
  177.5 0.7 copy-done.1
  178.2 7.9 %fusion.4 = f32[2,1,8,64,1]{3,1,2,0,4:T(1,128)S(1)} fusion(bf16[16,8,2,64,384]{4,3,2,1,0:T(8,128)(2,1)} %bitcast.117, bf16[16,384,2,1,1]{1,0,2,3,4:T(8,128)(2,1)S(1)} %bitcast.109), kind=kOutput, calls=%fused_computation.5 | convolution fusion | flops 12582912 | bytes 12611584 | tf_op jit(solution)/shard_map/esjcd,edj->sjc/dot_general | solution.py:201
  186.1 85.3 %reduce-scatter.4.cloned.1.call-done = bf16[1,8,2,64,384]{4,3,2,1,0:T(8,128)(2,1)} async-done(((bf16[16,8,2,64,384]{4,3,2,1,0:T(8,128)(2,1)}), bf16[1,8,2,64,384]{4,3,2,1,0:T(8,128)(2,1)}) %reduce-scatter.4.cloned.1.call-update) | async-done | bytes 786448
  271.4 2.2 fusion.12.x_ref
  273.6 16.4 %shard_map.111 = bf16[8,2,64,384]{3,2,1,0:T(8,128)(2,1)} custom-call(bf16[8,2,64,384]{3,2,1,0:T(8,128)(2,1)} %fusion.12.x_ref), custom_call_target="tpu_custom_call" | custom-call | tf_op jit(solution)/shard_map/pallas_call | solution.py:86
  290.0 2.3 fusion.18
  (49 shorter events, 5.3 us)
Async XLA Ops:
  6.5 37.9 %copy-start = (bf16[256,384]{1,0:T(8,128)(2,1)S(1)}, bf16[256,384]{1,0:T(8,128)(2,1)}, u32[]{:S(2)}) copy-start(bf16[256,384]{1,0:T(8,128)(2,1)} %param.15) | copy-start | bytes 589828
  6.5 33.9 %all-gather.5.cloned.1.call-start = ((), (), s32[]{:S(2)}) async-start(), calls=%async_computation.1 | async-start | bytes 1880064 | tf_op jit(solution)/shard_map/all_gather | solution.py:137
  12.0 138.2 %all-gather.7.cloned.1.call-start = ((), (), s32[]{:S(2)}) async-start(), calls=%async_computation.2 | async-start | bytes 13369344 | tf_op jit(solution)/shard_map/all_gather | solution.py:184
  60.6 210.8 %reduce-scatter.4.cloned.1.call-start = ((), (), s32[]{:S(2)}) async-start(), calls=%async_computation.3 | async-start | bytes 13369344
  177.4 0.7 copy-start.1
Sparse Core Ops, SparseCore 0:
  12.1 28.3 all-gather.4
  60.7 89.4 all-gather.6
  177.6 93.7 reduce-scatter.3

commit v6 on v5

--- a/solution.py
+++ b/solution.py
@@ -97,6 +97,65 @@
     )(x)
 
 
+def scan_kernel(x_ref, o_ref, state, received, send_sem, recv_sem):
+    n = lax.axis_size("seq")
+    me = lax.axis_index("seq")
+    col = lax.axis_index("exp")
+    mesh_id = pl.DeviceIdType.MESH
+    size = x_ref.shape[1] - 8
+    barrier = pltpu.get_barrier_semaphore()
+    for k in range(1, n):
+        peer = lax.rem(me + k, n)
+        pl.semaphore_signal(barrier, inc=1, device_id=(peer, col), device_id_type=mesh_id)
+    pl.semaphore_wait(barrier, n - 1)
+    shifts = [1, 1, 2, 4]
+    for r, d in enumerate(shifts):
+        source = x_ref if r == 0 else state.at[r - 1]
+        copy = pltpu.make_async_remote_copy(
+            src_ref=source,
+            dst_ref=received.at[r],
+            send_sem=send_sem.at[r],
+            recv_sem=recv_sem.at[r],
+            device_id=(lax.rem(me + d, n), col),
+            device_id_type=mesh_id,
+        )
+        copy.start()
+        copy.wait()
+        has_input = me - d >= 0
+        other = received[r]
+        if r == 0:
+            row = lax.broadcasted_iota(jnp.int32, other.shape, 1)
+            identity = jnp.where(row < size, 0.0, 1.0).astype(jnp.float32)
+            state[r] = jnp.where(has_input, other, identity)
+        else:
+            mine = state[r - 1]
+            fade = mine[:, size : size + 1, :]
+            combined_state = fade * other[:, :size, :] + mine[:, :size, :]
+            combined_fade = mine[:, size:, :] * other[:, size:, :]
+            state[r, :, :size, :] = jnp.where(has_input, combined_state, mine[:, :size, :])
+            state[r, :, size:, :] = jnp.where(has_input, combined_fade, mine[:, size:, :])
+
+    o_ref[...] = state[len(shifts) - 1, :, :size, :]
+
+
+def incoming_state(packed):
+    heads, rows, width = packed.shape
+    steps = 4
+    return pl.pallas_call(
+        scan_kernel,
+        out_shape=jax.ShapeDtypeStruct((heads, rows - 8, width), jnp.float32),
+        in_specs=[pl.BlockSpec(memory_space=pltpu.VMEM)],
+        out_specs=pl.BlockSpec(memory_space=pltpu.VMEM),
+        scratch_shapes=[
+            pltpu.VMEM((steps, heads, rows, width), jnp.float32),
+            pltpu.VMEM((steps, heads, rows, width), jnp.float32),
+            pltpu.SemaphoreType.DMA((steps,)),
+            pltpu.SemaphoreType.DMA((steps,)),
+        ],
+        compiler_params=pltpu.CompilerParams(collective_id=2, has_side_effects=True),
+    )(packed)
+
+
 def on_device(
     attn_query,
     attn_key,
@@ -128,26 +187,12 @@
     key_fade = jnp.exp(cumulative[:, -1:] - cumulative)
     scaled = (key_fade.T[:, :, None] * key_rows.astype(jnp.float32)).astype(jnp.bfloat16)
     local_state = jnp.einsum("shd,she->hde", scaled, value_rows, preferred_element_type=jnp.float32)
-    section_log_fade = cumulative[:, -1]
-    sections_total = lax.axis_size("seq")
+    section_fade = jnp.exp(cumulative[:, -1])
     packed = jnp.concatenate(
-        [local_state, jnp.broadcast_to(section_log_fade[:, None, None], (heads_here, 8, head_size))],
+        [local_state, jnp.broadcast_to(section_fade[:, None, None], (heads_here, 8, head_size))],
         axis=1,
     )
-    gathered = lax.all_gather(packed, "seq", axis=0)
-    all_states = gathered[:, :, :head_size, :]
-    all_log_fades = gathered[:, :, head_size, 0]
-    me = lax.axis_index("seq")
-    section_iota = lax.broadcasted_iota(jnp.int32, (sections_total, sections_total), 0)
-    between_iota = lax.broadcasted_iota(jnp.int32, (sections_total, sections_total), 1)
-    between = (between_iota > section_iota) & (between_iota < me)
-    log_weight = jnp.sum(
-        jnp.where(between[:, :, None], all_log_fades[None, :, :], 0.0), axis=1
-    )
-    state_weight = jnp.where(
-        lax.broadcasted_iota(jnp.int32, (sections_total, 1), 0) < me, jnp.exp(log_weight), 0.0
-    )
-    incoming = jnp.sum(state_weight[:, :, None, None] * all_states, axis=0)
+    incoming = incoming_state(packed)
     inter_part = jnp.einsum(
         "thd,hde->the", query_rows.astype(jnp.float32), incoming, precision=lax.Precision.HIGHEST
     )

time: 299 us -> 299 us (level)
  Pallas kernels: 42.7 us -> 67.6 us
  waiting for transfers between devices: 187 us -> 164 us
  other arithmetic: 10.6 us -> 7.46 us
    all_gather x1 -> x0, waiting for transfers between devices: 22.6 us -> none  [on_device(): gathered = lax.all_gather(packed, 'seq', axis=0)]
    pallas_call x0 -> x1, Pallas kernels: none -> 21.9 us  [incoming_state(): pl.pallas_call(scan_kernel, out_shape=jax.ShapeDtypeStruct((heads, rows -...]
    pallas_call x2, Pallas kernels: 31.1 us -> 34.2 us  [exchange(): pl.pallas_call(exchange_kernel, out_shape=jax.ShapeDtypeStruct(x.shape, x...]
    unnamed x4 -> x3, waiting for transfers between devices: 85.4 us -> 85.5 us
  transfers between devices with their start and end apart: 3 -> 2, of which waited for: 3 -> 2; matrix products, arithmetic and copies ran while one was open for 8% -> 6% of each run, Pallas kernels for 0% -> 0%
where the time goes in v6:
time: 299 us; the launch traced here: 298 us
  waiting for transfers between devices  164 us (55%)
  Pallas kernels  67.6 us (23%)
  matrix products  27.7 us (9%)
  local copies, waits for them, and re-layouts  17.4 us (6%)
  between operations  13.6 us (5%)
  other arithmetic  7.46 us (2%)
    unnamed x3, waiting for transfers between devices  85.5 us
    all_gather x1, waiting for transfers between devices, on_device(): portion = lax.all_gather(exchange(outgoing, 0), 'exp', axis=0)  78.9 us
    pallas_call x2, Pallas kernels, exchange(): pl.pallas_call(exchange_kernel, out_shape=jax.ShapeDtypeStruct(x.shape, x...  34.2 us
    pallas_call x1, Pallas kernels, incoming_state(): pl.pallas_call(scan_kernel, out_shape=jax.ShapeDtypeStruct((heads, rows -...  21.9 us
    dot_general x1, matrix products, on_device(): jnp.einsum('esjcd,jedf->sjcf', portion, jnp.concatenate([gate_blocks, up_...  14.2 us
    pallas_call x1, Pallas kernels, down_projection(): pl.pallas_call(functools.partial(down_kernel, blocks_per_step, block_widt...  11.5 us
    reshape x1, local copies, waits for them, and re-layouts, on_device(): up_blocks = up_weight.reshape(experts_here, shards, features, hidden_units)  10.5 us
    dot_general x1, matrix products, on_device(): jnp.einsum('esjcd,edj->sjc', portion, router_blocks, preferred_element_ty...  7.86 us
  transfers between devices with their start and end apart: 2, of which 2 were waited for; matrix products, arithmetic and copies ran while one was open for 6% of the time, Pallas kernels for 0%

profile of v6, /device:TPU:1, one launch (start us, length us, event | category | flops | bytes accessed | tf_op | source)
XLA Modules:
  0.0 298.1 jit_solution(14041287857370762596)
XLA Ops:
  6.6 0.8 copy.116
  7.7 0.7 reshape.127
  8.4 0.9 reduce-window.14
  10.0 1.1 copy.105
  11.1 1.1 copy.110
  12.4 0.7 pad_maximum_fusion.x_ref
  13.1 21.9 %shard_map.109 = f32[3,128,128]{2,1,0:T(8,128)} custom-call(f32[3,136,128]{2,1,0:T(8,128)} %pad_maximum_fusion.x_ref), custom_call_target="tpu_custom_call" | custom-call | tf_op jit(solution)/shard_map/pallas_call | solution.py:144
  35.0 1.1 copy.104
  36.1 1.3 fusion.16
  37.4 0.5 multiply_reduce_fusion
  38.2 1.2 reduce-window.16
  40.5 1.3 convolution_convert_fusion
  41.8 17.8 %shard_map.110 = bf16[8,2,64,384]{3,2,1,0:T(8,128)(2,1)} custom-call(bf16[8,2,64,384]{3,2,1,0:T(8,128)(2,1)} %bitcast.96), custom_call_target="tpu_custom_call" | custom-call | tf_op jit(solution)/shard_map/pallas_call | solution.py:86
  59.7 10.5 %copy_bitcast_fusion = (bf16[2,16,384,288]{2,3,1,0:T(8,128)(2,1)}, bf16[2,16,384,288]{2,3,1,0:T(8,128)(2,1)}) fusion(bf16[2,36,16,8,384]{4,3,2,1,0:T(8,128)(2,1)} %bitcast.94, bf16[2,36,16,8,384]{4,3,2,1,0:T(8,128)(2,1)} %bitcast.95), kind=kLoop, calls=%fused_computation.7 | loop fusion | bytes 28311552 | tf_op jit(solution)/shard_map/reshape | solution.py:236
  70.2 78.9 %all-gather.3.cloned.1.call-done = bf16[128,2,64,384]{3,2,1,0:T(8,128)(2,1)} async-done(((bf16[8,2,64,384]{3,2,1,0:T(8,128)(2,1)}), bf16[128,2,64,384]{3,2,1,0:T(8,128)(2,1)}) %all-gather.3.cloned.1.call-update) | async-done | bytes 12582928 | tf_op jit(solution)/shard_map/all_gather | solution.py:229
  149.1 14.2 %fusion.7 = f32[8,2,64,576]{3,2,1,0:T(8,128)S(1)} fusion(bf16[16,8,2,64,384]{4,3,2,1,0:T(8,128)(2,1)} %bitcast.111, bf16[2,16,384,288]{2,3,1,0:T(8,128)(2,1)} %get-tuple-element.9, bf16[2,16,384,288]{2,3,1,0:T(8,128)(2,1)} %get-tuple-element.10), kind=kOutput, calls=%fused_computation.11 | convolution fusion | flops 7276068864 | bytes 29097984 | tf_op jit(solution)/shard_map/esjcd,jedf->sjcf/dot_general | solution.py:238
  163.3 1.5 fusion.10.h_ref
  164.8 11.5 %shard_map.111 = bf16[16,8,2,64,384]{4,3,2,1,0:T(8,128)(2,1)} custom-call(bf16[8,2,64,288]{3,2,1,0:T(8,128)(2,1)} %fusion.10.h_ref, bf16[2,288,6144]{2,1,0:T(8,128)(2,1)} %w_ref.1), custom_call_target="tpu_custom_call" | custom-call | flops 3623878656 | bytes 20250624 | tf_op jit(solution)/shard_map/pallas_call | solution.py:32
  176.3 0.7 copy-done.1
  177.1 7.9 %fusion.4 = f32[2,1,8,64,1]{3,1,2,0,4:T(1,128)S(1)} fusion(bf16[16,8,2,64,384]{4,3,2,1,0:T(8,128)(2,1)} %bitcast.112, bf16[16,384,2,1,1]{1,0,2,3,4:T(8,128)(2,1)S(1)} %bitcast.106), kind=kOutput, calls=%fused_computation.5 | convolution fusion | flops 12582912 | bytes 12611584 | tf_op jit(solution)/shard_map/esjcd,edj->sjc/dot_general | solution.py:246
  185.0 85.4 %reduce-scatter.4.cloned.1.call-done = bf16[1,8,2,64,384]{4,3,2,1,0:T(8,128)(2,1)} async-done(((bf16[16,8,2,64,384]{4,3,2,1,0:T(8,128)(2,1)}), bf16[1,8,2,64,384]{4,3,2,1,0:T(8,128)(2,1)}) %reduce-scatter.4.cloned.1.call-update) | async-done | bytes 786448
  270.4 2.2 fusion.11.x_ref
  272.6 16.3 %shard_map.112 = bf16[8,2,64,384]{3,2,1,0:T(8,128)(2,1)} custom-call(bf16[8,2,64,384]{3,2,1,0:T(8,128)(2,1)} %fusion.11.x_ref), custom_call_target="tpu_custom_call" | custom-call | tf_op jit(solution)/shard_map/pallas_call | solution.py:86
  289.0 2.3 fusion.17
  (44 shorter events, 2.7 us)
Async XLA Ops:
  6.5 33.4 %copy-start.2 = (s32[256,2]{0,1:T(2,128)S(1)}, s32[256,2]{0,1:T(2,128)}, u32[]{:S(2)}) copy-start(s32[256,2]{0,1:T(2,128)} %param.17) | copy-start | bytes 6148
  6.5 31.6 %copy-start.3 = (bf16[384]{0:T(512)(128)(2,1)S(1)}, bf16[384]{0:T(512)(128)(2,1)}, u32[]{:S(2)}) copy-start(bf16[384]{0:T(512)(128)(2,1)} %param.16) | copy-start | bytes 2308
  6.5 33.9 %copy-start = (bf16[256,384]{1,0:T(8,128)(2,1)S(1)}, bf16[256,384]{1,0:T(8,128)(2,1)}, u32[]{:S(2)}) copy-start(bf16[256,384]{1,0:T(8,128)(2,1)} %param.15) | copy-start | bytes 589828
  6.5 142.6 %all-gather.3.cloned.1.call-start = ((), (), s32[]{:S(2)}) async-start(), calls=%async_computation.1 | async-start | bytes 13369344 | tf_op jit(solution)/shard_map/all_gather | solution.py:229
  59.7 210.7 %reduce-scatter.4.cloned.1.call-start = ((), (), s32[]{:S(2)}) async-start(), calls=%async_computation.2 | async-start | bytes 13369344
  176.3 0.7 copy-start.1
Sparse Core Ops, SparseCore 0:
  59.8 89.2 all-gather.2
  176.5 93.8 reduce-scatter.3

commit v7 on v6

--- a/solution.py
+++ b/solution.py
@@ -108,34 +108,46 @@
         peer = lax.rem(me + k, n)
         pl.semaphore_signal(barrier, inc=1, device_id=(peer, col), device_id_type=mesh_id)
     pl.semaphore_wait(barrier, n - 1)
-    shifts = [1, 1, 2, 4]
-    for r, d in enumerate(shifts):
-        source = x_ref if r == 0 else state.at[r - 1]
+    row = lax.broadcasted_iota(jnp.int32, x_ref.shape, 1)
+    identity = jnp.where(row < size, 0.0, 1.0).astype(jnp.float32)
+
+    def compose(later, earlier):
+        fade = later[:, size : size + 1, :]
+        return jnp.concatenate(
+            [
+                fade * earlier[:, :size, :] + later[:, :size, :],
+                later[:, size:, :] * earlier[:, size:, :],
+            ],
+            axis=1,
+        )
+
+    def send(source, slot, d):
         copy = pltpu.make_async_remote_copy(
             src_ref=source,
-            dst_ref=received.at[r],
-            send_sem=send_sem.at[r],
-            recv_sem=recv_sem.at[r],
+            dst_ref=received.at[slot],
+            send_sem=send_sem.at[slot],
+            recv_sem=recv_sem.at[slot],
             device_id=(lax.rem(me + d, n), col),
             device_id_type=mesh_id,
         )
         copy.start()
+        return copy
+
+    def arrived(slot, d):
+        return jnp.where(me - d >= 0, received[slot], identity)
+
+    first = send(x_ref, 0, 1)
+    second = send(x_ref, 1, 2)
+    first.wait()
+    second.wait()
+    state[0] = compose(arrived(0, 1), arrived(1, 2))
+    shifts = [2, 4]
+    for r, d in enumerate(shifts):
+        copy = send(state.at[r], r + 2, d)
         copy.wait()
-        has_input = me - d >= 0
-        other = received[r]
-        if r == 0:
-            row = lax.broadcasted_iota(jnp.int32, other.shape, 1)
-            identity = jnp.where(row < size, 0.0, 1.0).astype(jnp.float32)
-            state[r] = jnp.where(has_input, other, identity)
-        else:
-            mine = state[r - 1]
-            fade = mine[:, size : size + 1, :]
-            combined_state = fade * other[:, :size, :] + mine[:, :size, :]
-            combined_fade = mine[:, size:, :] * other[:, size:, :]
-            state[r, :, :size, :] = jnp.where(has_input, combined_state, mine[:, :size, :])
-            state[r, :, size:, :] = jnp.where(has_input, combined_fade, mine[:, size:, :])
-
-    o_ref[...] = state[len(shifts) - 1, :, :size, :]
+        state[r + 1] = compose(state[r], arrived(r + 2, d))
+
+    o_ref[...] = state[len(shifts), :, :size, :]
 
 
 def incoming_state(packed):

time: 299 us -> 302 us (1.010)
  Pallas kernels: 67.6 us -> 70.9 us
    pallas_call x1, Pallas kernels: 21.9 us -> 28.1 us  [incoming_state(): pl.pallas_call(scan_kernel, out_shape=jax.ShapeDtypeStruct((heads, rows -...]
where the time goes in v7:
time: 302 us; the launch traced here: 301 us
  waiting for transfers between devices  164 us (54%)
  Pallas kernels  70.9 us (23%)
  matrix products  27.6 us (9%)
  local copies, waits for them, and re-layouts  17.4 us (6%)
  between operations  13.6 us (5%)
  other arithmetic  7.46 us (2%)
    unnamed x3, waiting for transfers between devices  85.2 us
    all_gather x1, waiting for transfers between devices, on_device(): portion = lax.all_gather(exchange(outgoing, 0), 'exp', axis=0)  78.8 us
    pallas_call x2, Pallas kernels, exchange(): pl.pallas_call(exchange_kernel, out_shape=jax.ShapeDtypeStruct(x.shape, x...  31.3 us
    pallas_call x1, Pallas kernels, incoming_state(): pl.pallas_call(scan_kernel, out_shape=jax.ShapeDtypeStruct((heads, rows -...  28.1 us
    dot_general x1, matrix products, on_device(): jnp.einsum('esjcd,jedf->sjcf', portion, jnp.concatenate([gate_blocks, up_...  14.2 us
    pallas_call x1, Pallas kernels, down_projection(): pl.pallas_call(functools.partial(down_kernel, blocks_per_step, block_widt...  11.5 us
    reshape x1, local copies, waits for them, and re-layouts, on_device(): up_blocks = up_weight.reshape(experts_here, shards, features, hidden_units)  10.5 us
    dot_general x1, matrix products, on_device(): jnp.einsum('esjcd,edj->sjc', portion, router_blocks, preferred_element_ty...  7.86 us
  transfers between devices with their start and end apart: 2, of which 2 were waited for; matrix products, arithmetic and copies ran while one was open for 6% of the time, Pallas kernels for 0%

profile of v7, /device:TPU:1, one launch (start us, length us, event | category | flops | bytes accessed | tf_op | source)
XLA Modules:
  0.0 301.0 jit_solution(16252902530365180296)
XLA Ops:
  6.6 0.8 copy.116
  7.7 0.7 reshape.127
  8.4 0.9 reduce-window.14
  10.0 1.1 copy.105
  11.1 1.1 copy.110
  12.4 0.7 pad_maximum_fusion.x_ref
  13.1 28.1 %shard_map.109 = f32[3,128,128]{2,1,0:T(8,128)} custom-call(f32[3,136,128]{2,1,0:T(8,128)} %pad_maximum_fusion.x_ref), custom_call_target="tpu_custom_call" | custom-call | tf_op jit(solution)/shard_map/pallas_call | solution.py:156
  41.2 1.1 copy.104
  42.3 1.3 fusion.16
  43.5 0.5 multiply_reduce_fusion
  44.3 1.2 reduce-window.16
  46.7 1.3 convolution_convert_fusion
  48.0 14.9 %shard_map.110 = bf16[8,2,64,384]{3,2,1,0:T(8,128)(2,1)} custom-call(bf16[8,2,64,384]{3,2,1,0:T(8,128)(2,1)} %bitcast.96), custom_call_target="tpu_custom_call" | custom-call | tf_op jit(solution)/shard_map/pallas_call | solution.py:86
  63.0 10.5 %copy_bitcast_fusion = (bf16[2,16,384,288]{2,3,1,0:T(8,128)(2,1)}, bf16[2,16,384,288]{2,3,1,0:T(8,128)(2,1)}) fusion(bf16[2,36,16,8,384]{4,3,2,1,0:T(8,128)(2,1)} %bitcast.94, bf16[2,36,16,8,384]{4,3,2,1,0:T(8,128)(2,1)} %bitcast.95), kind=kLoop, calls=%fused_computation.7 | loop fusion | bytes 28311552 | tf_op jit(solution)/shard_map/reshape | solution.py:248
  73.5 78.8 %all-gather.3.cloned.1.call-done = bf16[128,2,64,384]{3,2,1,0:T(8,128)(2,1)} async-done(((bf16[8,2,64,384]{3,2,1,0:T(8,128)(2,1)}), bf16[128,2,64,384]{3,2,1,0:T(8,128)(2,1)}) %all-gather.3.cloned.1.call-update) | async-done | bytes 12582928 | tf_op jit(solution)/shard_map/all_gather | solution.py:241
  152.2 14.2 %fusion.7 = f32[8,2,64,576]{3,2,1,0:T(8,128)S(1)} fusion(bf16[16,8,2,64,384]{4,3,2,1,0:T(8,128)(2,1)} %bitcast.111, bf16[2,16,384,288]{2,3,1,0:T(8,128)(2,1)} %get-tuple-element.9, bf16[2,16,384,288]{2,3,1,0:T(8,128)(2,1)} %get-tuple-element.10), kind=kOutput, calls=%fused_computation.11 | convolution fusion | flops 7276068864 | bytes 29097984 | tf_op jit(solution)/shard_map/esjcd,jedf->sjcf/dot_general | solution.py:250
  166.4 1.5 fusion.10.h_ref
  168.0 11.5 %shard_map.111 = bf16[16,8,2,64,384]{4,3,2,1,0:T(8,128)(2,1)} custom-call(bf16[8,2,64,288]{3,2,1,0:T(8,128)(2,1)} %fusion.10.h_ref, bf16[2,288,6144]{2,1,0:T(8,128)(2,1)} %w_ref.1), custom_call_target="tpu_custom_call" | custom-call | flops 3623878656 | bytes 20250624 | tf_op jit(solution)/shard_map/pallas_call | solution.py:32
  179.5 0.7 copy-done.1
  180.2 7.9 %fusion.4 = f32[2,1,8,64,1]{3,1,2,0,4:T(1,128)S(1)} fusion(bf16[16,8,2,64,384]{4,3,2,1,0:T(8,128)(2,1)} %bitcast.112, bf16[16,384,2,1,1]{1,0,2,3,4:T(8,128)(2,1)S(1)} %bitcast.106), kind=kOutput, calls=%fused_computation.5 | convolution fusion | flops 12582912 | bytes 12611584 | tf_op jit(solution)/shard_map/esjcd,edj->sjc/dot_general | solution.py:258
  188.1 85.2 %reduce-scatter.4.cloned.1.call-done = bf16[1,8,2,64,384]{4,3,2,1,0:T(8,128)(2,1)} async-done(((bf16[16,8,2,64,384]{4,3,2,1,0:T(8,128)(2,1)}), bf16[1,8,2,64,384]{4,3,2,1,0:T(8,128)(2,1)}) %reduce-scatter.4.cloned.1.call-update) | async-done | bytes 786448
  273.3 2.2 fusion.11.x_ref
  275.5 16.4 %shard_map.112 = bf16[8,2,64,384]{3,2,1,0:T(8,128)(2,1)} custom-call(bf16[8,2,64,384]{3,2,1,0:T(8,128)(2,1)} %fusion.11.x_ref), custom_call_target="tpu_custom_call" | custom-call | tf_op jit(solution)/shard_map/pallas_call | solution.py:86
  291.9 2.3 fusion.17
  (44 shorter events, 2.7 us)
Async XLA Ops:
  6.5 39.6 %copy-start.2 = (s32[256,2]{0,1:T(2,128)S(1)}, s32[256,2]{0,1:T(2,128)}, u32[]{:S(2)}) copy-start(s32[256,2]{0,1:T(2,128)} %param.17) | copy-start | bytes 6148
  6.5 37.8 %copy-start.3 = (bf16[384]{0:T(512)(128)(2,1)S(1)}, bf16[384]{0:T(512)(128)(2,1)}, u32[]{:S(2)}) copy-start(bf16[384]{0:T(512)(128)(2,1)} %param.16) | copy-start | bytes 2308
  6.5 40.1 %copy-start = (bf16[256,384]{1,0:T(8,128)(2,1)S(1)}, bf16[256,384]{1,0:T(8,128)(2,1)}, u32[]{:S(2)}) copy-start(bf16[256,384]{1,0:T(8,128)(2,1)} %param.15) | copy-start | bytes 589828
  6.5 145.7 %all-gather.3.cloned.1.call-start = ((), (), s32[]{:S(2)}) async-start(), calls=%async_computation.1 | async-start | bytes 13369344 | tf_op jit(solution)/shard_map/all_gather | solution.py:241
  62.9 210.4 %reduce-scatter.4.cloned.1.call-start = ((), (), s32[]{:S(2)}) async-start(), calls=%async_computation.2 | async-start | bytes 13369344
  179.5 0.7 copy-start.1
Sparse Core Ops, SparseCore 0:
  63.0 89.1 all-gather.2
  179.6 93.6 reduce-scatter.3

commit v8 on v6

--- a/solution.py
+++ b/solution.py
@@ -192,21 +192,11 @@
         [local_state, jnp.broadcast_to(section_fade[:, None, None], (heads_here, 8, head_size))],
         axis=1,
     )
-    incoming = incoming_state(packed)
-    inter_part = jnp.einsum(
-        "thd,hde->the", query_rows.astype(jnp.float32), incoming, precision=lax.Precision.HIGHEST
-    )
-    attn_out = intra_part + jnp.exp(cumulative).T[:, :, None] * inter_part
-    mean_square = jnp.mean(attn_out * attn_out, axis=2, keepdims=True)
-    normed = (attn_out / jnp.sqrt(mean_square + 1e-06)).reshape(length, heads_here * head_size)
-    stream = (residual.astype(jnp.float32) + norm_gain.astype(jnp.float32) * normed).astype(
-        jnp.bfloat16
-    )
     experts_here = router_weight.shape[1]
     groups = lax.axis_size("seq")
     expert_count = experts_here * groups
     capacity = 4 * length // expert_count
-    features = stream.shape[1]
+    features = residual.shape[1]
     choices_per_token = expert_ids.shape[1]
     flat_ids = expert_ids.reshape(-1)
     expert_iota = lax.broadcasted_iota(jnp.int32, (1, expert_count), 1)
@@ -221,6 +211,17 @@
         .reshape(expert_count * capacity, length, choices_per_token)
         .sum(axis=2)
     )
+    packed, route_matrix = lax.optimization_barrier((packed, route_matrix))
+    incoming = incoming_state(packed)
+    inter_part = jnp.einsum(
+        "thd,hde->the", query_rows.astype(jnp.float32), incoming, precision=lax.Precision.HIGHEST
+    )
+    attn_out = intra_part + jnp.exp(cumulative).T[:, :, None] * inter_part
+    mean_square = jnp.mean(attn_out * attn_out, axis=2, keepdims=True)
+    normed = (attn_out / jnp.sqrt(mean_square + 1e-06)).reshape(length, heads_here * head_size)
+    stream = (residual.astype(jnp.float32) + norm_gain.astype(jnp.float32) * normed).astype(
+        jnp.bfloat16
+    )
     outgoing = jnp.dot(route_matrix, stream, preferred_element_type=jnp.float32).astype(
         jnp.bfloat16
     )

time: 299 us -> 299 us (level)
  no operation moved by 1% of the time
where the time goes in v8:
time: 299 us
  waiting for transfers between devices  164 us (55%)
  Pallas kernels  67.6 us (23%)
  matrix products  27.7 us (9%)
  local copies, waits for them, and re-layouts  17.4 us (6%)
  between operations  13.6 us (5%)
  other arithmetic  8.14 us (3%)
    unnamed x3, waiting for transfers between devices  85.3 us
    all_gather x1, waiting for transfers between devices, on_device(): portion = lax.all_gather(exchange(outgoing, 0), 'exp', axis=0)  78.9 us
    pallas_call x2, Pallas kernels, exchange(): pl.pallas_call(exchange_kernel, out_shape=jax.ShapeDtypeStruct(x.shape, x...  34.2 us
    pallas_call x1, Pallas kernels, incoming_state(): pl.pallas_call(scan_kernel, out_shape=jax.ShapeDtypeStruct((heads, rows -...  21.9 us
    dot_general x1, matrix products, on_device(): jnp.einsum('esjcd,jedf->sjcf', portion, jnp.concatenate([gate_blocks, up_...  14.2 us
    pallas_call x1, Pallas kernels, down_projection(): pl.pallas_call(functools.partial(down_kernel, blocks_per_step, block_widt...  11.5 us
    reshape x1, local copies, waits for them, and re-layouts, on_device(): up_blocks = up_weight.reshape(experts_here, shards, features, hidden_units)  10.5 us
    dot_general x1, matrix products, on_device(): jnp.einsum('esjcd,edj->sjc', portion, router_blocks, preferred_element_ty...  7.86 us
  transfers between devices with their start and end apart: 2, of which 2 were waited for; matrix products, arithmetic and copies ran while one was open for 6% of the time, Pallas kernels for 0%

profile of v8, /device:TPU:1, one launch (start us, length us, event | category | flops | bytes accessed | tf_op | source)
XLA Modules:
  0.0 298.6 jit_solution(17091395372347117338)
XLA Ops:
  6.5 0.8 copy.115
  7.7 0.7 reshape.127
  8.4 0.9 reduce-window.14
  10.0 1.1 copy.107
  11.1 1.1 copy.112
  12.1 1.2 reduce-window.16
  13.9 0.7 multiply_add_fusion
  15.3 0.7 pad_maximum_fusion.x_ref
  16.0 21.9 %shard_map.109 = f32[3,128,128]{2,1,0:T(8,128)} custom-call(f32[3,136,128]{2,1,0:T(8,128)} %pad_maximum_fusion.x_ref), custom_call_target="tpu_custom_call" | custom-call | tf_op jit(solution)/shard_map/pallas_call | solution.py:144
  38.0 1.1 copy.106
  39.0 1.3 fusion.16
  41.2 1.3 convolution_convert_fusion
  42.5 17.8 %shard_map.110 = bf16[8,2,64,384]{3,2,1,0:T(8,128)(2,1)} custom-call(bf16[8,2,64,384]{3,2,1,0:T(8,128)(2,1)} %bitcast.96), custom_call_target="tpu_custom_call" | custom-call | tf_op jit(solution)/shard_map/pallas_call | solution.py:86
  60.4 10.5 %copy_bitcast_fusion = (bf16[2,16,384,288]{2,3,1,0:T(8,128)(2,1)}, bf16[2,16,384,288]{2,3,1,0:T(8,128)(2,1)}) fusion(bf16[2,36,16,8,384]{4,3,2,1,0:T(8,128)(2,1)} %bitcast.94, bf16[2,36,16,8,384]{4,3,2,1,0:T(8,128)(2,1)} %bitcast.95), kind=kLoop, calls=%fused_computation.7 | loop fusion | bytes 28311552 | tf_op jit(solution)/shard_map/reshape | solution.py:237
  70.9 78.9 %all-gather.3.cloned.1.call-done = bf16[128,2,64,384]{3,2,1,0:T(8,128)(2,1)} async-done(((bf16[8,2,64,384]{3,2,1,0:T(8,128)(2,1)}), bf16[128,2,64,384]{3,2,1,0:T(8,128)(2,1)}) %all-gather.3.cloned.1.call-update) | async-done | bytes 12582928 | tf_op jit(solution)/shard_map/all_gather | solution.py:230
  149.8 14.2 %fusion.7 = f32[8,2,64,576]{3,2,1,0:T(8,128)S(1)} fusion(bf16[16,8,2,64,384]{4,3,2,1,0:T(8,128)(2,1)} %bitcast.111, bf16[2,16,384,288]{2,3,1,0:T(8,128)(2,1)} %get-tuple-element.13, bf16[2,16,384,288]{2,3,1,0:T(8,128)(2,1)} %get-tuple-element.14), kind=kOutput, calls=%fused_computation.11 | convolution fusion | flops 7276068864 | bytes 29097984 | tf_op jit(solution)/shard_map/esjcd,jedf->sjcf/dot_general | solution.py:239
  164.0 1.5 fusion.10.h_ref
  165.5 11.5 %shard_map.111 = bf16[16,8,2,64,384]{4,3,2,1,0:T(8,128)(2,1)} custom-call(bf16[8,2,64,288]{3,2,1,0:T(8,128)(2,1)} %fusion.10.h_ref, bf16[2,288,6144]{2,1,0:T(8,128)(2,1)} %w_ref.1), custom_call_target="tpu_custom_call" | custom-call | flops 3623878656 | bytes 20250624 | tf_op jit(solution)/shard_map/pallas_call | solution.py:32
  177.0 0.7 copy-done.1
  177.8 7.9 %fusion.4 = f32[2,1,8,64,1]{3,1,2,0,4:T(1,128)S(1)} fusion(bf16[16,8,2,64,384]{4,3,2,1,0:T(8,128)(2,1)} %bitcast.112, bf16[16,384,2,1,1]{1,0,2,3,4:T(8,128)(2,1)S(1)} %bitcast.106), kind=kOutput, calls=%fused_computation.5 | convolution fusion | flops 12582912 | bytes 12611584 | tf_op jit(solution)/shard_map/esjcd,edj->sjc/dot_general | solution.py:247
  185.7 85.3 %reduce-scatter.4.cloned.1.call-done = bf16[1,8,2,64,384]{4,3,2,1,0:T(8,128)(2,1)} async-done(((bf16[16,8,2,64,384]{4,3,2,1,0:T(8,128)(2,1)}), bf16[1,8,2,64,384]{4,3,2,1,0:T(8,128)(2,1)}) %reduce-scatter.4.cloned.1.call-update) | async-done | bytes 786448
  271.0 2.2 fusion.11.x_ref
  273.2 16.3 %shard_map.112 = bf16[8,2,64,384]{3,2,1,0:T(8,128)(2,1)} custom-call(bf16[8,2,64,384]{3,2,1,0:T(8,128)(2,1)} %fusion.11.x_ref), custom_call_target="tpu_custom_call" | custom-call | tf_op jit(solution)/shard_map/pallas_call | solution.py:86
  289.5 2.3 fusion.17
  (42 shorter events, 3.2 us)
Async XLA Ops:
  6.5 34.5 %copy-start.2 = (bf16[384]{0:T(512)(128)(2,1)S(1)}, bf16[384]{0:T(512)(128)(2,1)}, u32[]{:S(2)}) copy-start(bf16[384]{0:T(512)(128)(2,1)} %param.16) | copy-start | bytes 2308
  6.5 34.6 %copy-start = (bf16[256,384]{1,0:T(8,128)(2,1)S(1)}, bf16[256,384]{1,0:T(8,128)(2,1)}, u32[]{:S(2)}) copy-start(bf16[256,384]{1,0:T(8,128)(2,1)} %param.15) | copy-start | bytes 589828
  6.5 143.2 %all-gather.3.cloned.1.call-start = ((), (), s32[]{:S(2)}) async-start(), calls=%async_computation.1 | async-start | bytes 13369344 | tf_op jit(solution)/shard_map/all_gather | solution.py:230
  60.4 210.6 %reduce-scatter.4.cloned.1.call-start = ((), (), s32[]{:S(2)}) async-start(), calls=%async_computation.2 | async-start | bytes 13369344
  177.0 0.7 copy-start.1
Sparse Core Ops, SparseCore 0:
  60.5 89.2 all-gather.2
  177.2 93.7 reduce-scatter.3

commit v9 on v6

--- a/solution.py
+++ b/solution.py
@@ -111,16 +111,20 @@
     shifts = [1, 1, 2, 4]
     for r, d in enumerate(shifts):
         source = x_ref if r == 0 else state.at[r - 1]
-        copy = pltpu.make_async_remote_copy(
-            src_ref=source,
-            dst_ref=received.at[r],
-            send_sem=send_sem.at[r],
-            recv_sem=recv_sem.at[r],
-            device_id=(lax.rem(me + d, n), col),
-            device_id_type=mesh_id,
-        )
-        copy.start()
-        copy.wait()
+        copies = []
+        for h in range(x_ref.shape[0]):
+            copy = pltpu.make_async_remote_copy(
+                src_ref=source.at[h],
+                dst_ref=received.at[r, h],
+                send_sem=send_sem.at[r, h],
+                recv_sem=recv_sem.at[r, h],
+                device_id=(lax.rem(me + d, n), col),
+                device_id_type=mesh_id,
+            )
+            copy.start()
+            copies.append(copy)
+        for copy in copies:
+            copy.wait()
         has_input = me - d >= 0
         other = received[r]
         if r == 0:
@@ -149,8 +153,8 @@
         scratch_shapes=[
             pltpu.VMEM((steps, heads, rows, width), jnp.float32),
             pltpu.VMEM((steps, heads, rows, width), jnp.float32),
-            pltpu.SemaphoreType.DMA((steps,)),
-            pltpu.SemaphoreType.DMA((steps,)),
+            pltpu.SemaphoreType.DMA((steps, heads)),
+            pltpu.SemaphoreType.DMA((steps, heads)),
         ],
         compiler_params=pltpu.CompilerParams(collective_id=2, has_side_effects=True),
     )(packed)

time: 299 us -> 299 us (level)
  no operation moved by 1% of the time
where the time goes in v9:
time: 299 us; the launch traced here: 298 us
  waiting for transfers between devices  164 us (55%)
  Pallas kernels  67.7 us (23%)
  matrix products  27.7 us (9%)
  local copies, waits for them, and re-layouts  17.4 us (6%)
  between operations  13.6 us (5%)
  other arithmetic  7.46 us (2%)
    unnamed x3, waiting for transfers between devices  85.5 us
    all_gather x1, waiting for transfers between devices, on_device(): portion = lax.all_gather(exchange(outgoing, 0), 'exp', axis=0)  78.9 us
    pallas_call x2, Pallas kernels, exchange(): pl.pallas_call(exchange_kernel, out_shape=jax.ShapeDtypeStruct(x.shape, x...  34.2 us
    pallas_call x1, Pallas kernels, incoming_state(): pl.pallas_call(scan_kernel, out_shape=jax.ShapeDtypeStruct((heads, rows -...  22.1 us
    dot_general x1, matrix products, on_device(): jnp.einsum('esjcd,jedf->sjcf', portion, jnp.concatenate([gate_blocks, up_...  14.2 us
    pallas_call x1, Pallas kernels, down_projection(): pl.pallas_call(functools.partial(down_kernel, blocks_per_step, block_widt...  11.5 us
    reshape x1, local copies, waits for them, and re-layouts, on_device(): up_blocks = up_weight.reshape(experts_here, shards, features, hidden_units)  10.5 us
    dot_general x1, matrix products, on_device(): jnp.einsum('esjcd,edj->sjc', portion, router_blocks, preferred_element_ty...  7.86 us
  transfers between devices with their start and end apart: 2, of which 2 were waited for; matrix products, arithmetic and copies ran while one was open for 6% of the time, Pallas kernels for 0%

profile of v9, /device:TPU:1, one launch (start us, length us, event | category | flops | bytes accessed | tf_op | source)
XLA Modules:
  0.0 298.2 jit_solution(11679522534087992148)
XLA Ops:
  6.6 0.8 copy.116
  7.7 0.7 reshape.127
  8.4 0.9 reduce-window.14
  10.0 1.1 copy.105
  11.1 1.1 copy.110
  12.4 0.7 pad_maximum_fusion.x_ref
  13.1 22.1 %shard_map.109 = f32[3,128,128]{2,1,0:T(8,128)} custom-call(f32[3,136,128]{2,1,0:T(8,128)} %pad_maximum_fusion.x_ref), custom_call_target="tpu_custom_call" | custom-call | tf_op jit(solution)/shard_map/pallas_call | solution.py:148
  35.2 1.1 copy.104
  36.2 1.3 fusion.16
  37.5 0.5 multiply_reduce_fusion
  38.3 1.2 reduce-window.16
  40.6 1.3 convolution_convert_fusion
  42.0 17.8 %shard_map.110 = bf16[8,2,64,384]{3,2,1,0:T(8,128)(2,1)} custom-call(bf16[8,2,64,384]{3,2,1,0:T(8,128)(2,1)} %bitcast.96), custom_call_target="tpu_custom_call" | custom-call | tf_op jit(solution)/shard_map/pallas_call | solution.py:86
  59.9 10.5 %copy_bitcast_fusion = (bf16[2,16,384,288]{2,3,1,0:T(8,128)(2,1)}, bf16[2,16,384,288]{2,3,1,0:T(8,128)(2,1)}) fusion(bf16[2,36,16,8,384]{4,3,2,1,0:T(8,128)(2,1)} %bitcast.94, bf16[2,36,16,8,384]{4,3,2,1,0:T(8,128)(2,1)} %bitcast.95), kind=kLoop, calls=%fused_computation.7 | loop fusion | bytes 28311552 | tf_op jit(solution)/shard_map/reshape | solution.py:240
  70.4 78.9 %all-gather.3.cloned.1.call-done = bf16[128,2,64,384]{3,2,1,0:T(8,128)(2,1)} async-done(((bf16[8,2,64,384]{3,2,1,0:T(8,128)(2,1)}), bf16[128,2,64,384]{3,2,1,0:T(8,128)(2,1)}) %all-gather.3.cloned.1.call-update) | async-done | bytes 12582928 | tf_op jit(solution)/shard_map/all_gather | solution.py:233
  149.2 14.2 %fusion.7 = f32[8,2,64,576]{3,2,1,0:T(8,128)S(1)} fusion(bf16[16,8,2,64,384]{4,3,2,1,0:T(8,128)(2,1)} %bitcast.111, bf16[2,16,384,288]{2,3,1,0:T(8,128)(2,1)} %get-tuple-element.9, bf16[2,16,384,288]{2,3,1,0:T(8,128)(2,1)} %get-tuple-element.10), kind=kOutput, calls=%fused_computation.11 | convolution fusion | flops 7276068864 | bytes 29097984 | tf_op jit(solution)/shard_map/esjcd,jedf->sjcf/dot_general | solution.py:242
  163.4 1.5 fusion.10.h_ref
  165.0 11.5 %shard_map.111 = bf16[16,8,2,64,384]{4,3,2,1,0:T(8,128)(2,1)} custom-call(bf16[8,2,64,288]{3,2,1,0:T(8,128)(2,1)} %fusion.10.h_ref, bf16[2,288,6144]{2,1,0:T(8,128)(2,1)} %w_ref.1), custom_call_target="tpu_custom_call" | custom-call | flops 3623878656 | bytes 20250624 | tf_op jit(solution)/shard_map/pallas_call | solution.py:32
  176.5 0.7 copy-done.1
  177.2 7.9 %fusion.4 = f32[2,1,8,64,1]{3,1,2,0,4:T(1,128)S(1)} fusion(bf16[16,8,2,64,384]{4,3,2,1,0:T(8,128)(2,1)} %bitcast.112, bf16[16,384,2,1,1]{1,0,2,3,4:T(8,128)(2,1)S(1)} %bitcast.106), kind=kOutput, calls=%fused_computation.5 | convolution fusion | flops 12582912 | bytes 12611584 | tf_op jit(solution)/shard_map/esjcd,edj->sjc/dot_general | solution.py:250
  185.1 85.4 %reduce-scatter.4.cloned.1.call-done = bf16[1,8,2,64,384]{4,3,2,1,0:T(8,128)(2,1)} async-done(((bf16[16,8,2,64,384]{4,3,2,1,0:T(8,128)(2,1)}), bf16[1,8,2,64,384]{4,3,2,1,0:T(8,128)(2,1)}) %reduce-scatter.4.cloned.1.call-update) | async-done | bytes 786448
  270.5 2.2 fusion.11.x_ref
  272.8 16.3 %shard_map.112 = bf16[8,2,64,384]{3,2,1,0:T(8,128)(2,1)} custom-call(bf16[8,2,64,384]{3,2,1,0:T(8,128)(2,1)} %fusion.11.x_ref), custom_call_target="tpu_custom_call" | custom-call | tf_op jit(solution)/shard_map/pallas_call | solution.py:86
  289.1 2.3 fusion.17
  (44 shorter events, 2.7 us)
Async XLA Ops:
  6.5 33.5 %copy-start.2 = (s32[256,2]{0,1:T(2,128)S(1)}, s32[256,2]{0,1:T(2,128)}, u32[]{:S(2)}) copy-start(s32[256,2]{0,1:T(2,128)} %param.17) | copy-start | bytes 6148
  6.5 31.8 %copy-start.3 = (bf16[384]{0:T(512)(128)(2,1)S(1)}, bf16[384]{0:T(512)(128)(2,1)}, u32[]{:S(2)}) copy-start(bf16[384]{0:T(512)(128)(2,1)} %param.16) | copy-start | bytes 2308
  6.5 34.0 %copy-start = (bf16[256,384]{1,0:T(8,128)(2,1)S(1)}, bf16[256,384]{1,0:T(8,128)(2,1)}, u32[]{:S(2)}) copy-start(bf16[256,384]{1,0:T(8,128)(2,1)} %param.15) | copy-start | bytes 589828
  6.5 142.7 %all-gather.3.cloned.1.call-start = ((), (), s32[]{:S(2)}) async-start(), calls=%async_computation.1 | async-start | bytes 13369344 | tf_op jit(solution)/shard_map/all_gather | solution.py:233
  59.8 210.7 %reduce-scatter.4.cloned.1.call-start = ((), (), s32[]{:S(2)}) async-start(), calls=%async_computation.2 | async-start | bytes 13369344
  176.5 0.7 copy-start.1
Sparse Core Ops, SparseCore 0:
  59.9 89.2 all-gather.2
  176.6 93.8 reduce-scatter.3

commit v10 on v6

--- a/solution.py
+++ b/solution.py
@@ -27,7 +27,7 @@
     sections, experts_here, capacity, hidden = hidden_act.shape
     features = down_weight.shape[2]
     block_width = features // shards
-    blocks_per_step = 8
+    blocks_per_step = 16
     steps = shards // blocks_per_step
     return pl.pallas_call(
         functools.partial(down_kernel, blocks_per_step, block_width),

time: 299 us -> 299 us (level)
  no operation moved by 1% of the time
where the time goes in v10:
time: 299 us; the launch traced here: 298 us
  waiting for transfers between devices  164 us (55%)
  Pallas kernels  67.7 us (23%)
  matrix products  27.7 us (9%)
  local copies, waits for them, and re-layouts  17.4 us (6%)
  between operations  13.6 us (5%)
  other arithmetic  7.46 us (2%)
    unnamed x3, waiting for transfers between devices  85.4 us
    all_gather x1, waiting for transfers between devices, on_device(): portion = lax.all_gather(exchange(outgoing, 0), 'exp', axis=0)  78.9 us
    pallas_call x2, Pallas kernels, exchange(): pl.pallas_call(exchange_kernel, out_shape=jax.ShapeDtypeStruct(x.shape, x...  34.2 us
    pallas_call x1, Pallas kernels, incoming_state(): pl.pallas_call(scan_kernel, out_shape=jax.ShapeDtypeStruct((heads, rows -...  21.9 us
    dot_general x1, matrix products, on_device(): jnp.einsum('esjcd,jedf->sjcf', portion, jnp.concatenate([gate_blocks, up_...  14.2 us
    pallas_call x1, Pallas kernels, down_projection(): pl.pallas_call(functools.partial(down_kernel, blocks_per_step, block_widt...  11.7 us
    reshape x1, local copies, waits for them, and re-layouts, on_device(): up_blocks = up_weight.reshape(experts_here, shards, features, hidden_units)  10.5 us
    dot_general x1, matrix products, on_device(): jnp.einsum('esjcd,edj->sjc', portion, router_blocks, preferred_element_ty...  7.86 us
  transfers between devices with their start and end apart: 2, of which 2 were waited for; matrix products, arithmetic and copies ran while one was open for 6% of the time, Pallas kernels for 0%

profile of v10, /device:TPU:1, one launch (start us, length us, event | category | flops | bytes accessed | tf_op | source)
XLA Modules:
  0.0 298.2 jit_solution(4520438727996651848)
XLA Ops:
  6.6 0.8 copy.116
  7.7 0.7 reshape.127
  8.4 0.9 reduce-window.14
  10.0 1.1 copy.105
  11.1 1.1 copy.110
  12.4 0.7 pad_maximum_fusion.x_ref
  13.1 21.9 %shard_map.109 = f32[3,128,128]{2,1,0:T(8,128)} custom-call(f32[3,136,128]{2,1,0:T(8,128)} %pad_maximum_fusion.x_ref), custom_call_target="tpu_custom_call" | custom-call | tf_op jit(solution)/shard_map/pallas_call | solution.py:144
  35.0 1.1 copy.104
  36.1 1.3 fusion.16
  37.4 0.5 multiply_reduce_fusion
  38.2 1.2 reduce-window.16
  40.5 1.3 convolution_convert_fusion
  41.8 17.8 %shard_map.110 = bf16[8,2,64,384]{3,2,1,0:T(8,128)(2,1)} custom-call(bf16[8,2,64,384]{3,2,1,0:T(8,128)(2,1)} %bitcast.96), custom_call_target="tpu_custom_call" | custom-call | tf_op jit(solution)/shard_map/pallas_call | solution.py:86
  59.7 10.5 %copy_bitcast_fusion = (bf16[2,16,384,288]{2,3,1,0:T(8,128)(2,1)}, bf16[2,16,384,288]{2,3,1,0:T(8,128)(2,1)}) fusion(bf16[2,36,16,8,384]{4,3,2,1,0:T(8,128)(2,1)} %bitcast.94, bf16[2,36,16,8,384]{4,3,2,1,0:T(8,128)(2,1)} %bitcast.95), kind=kLoop, calls=%fused_computation.7 | loop fusion | bytes 28311552 | tf_op jit(solution)/shard_map/reshape | solution.py:236
  70.2 78.9 %all-gather.3.cloned.1.call-done = bf16[128,2,64,384]{3,2,1,0:T(8,128)(2,1)} async-done(((bf16[8,2,64,384]{3,2,1,0:T(8,128)(2,1)}), bf16[128,2,64,384]{3,2,1,0:T(8,128)(2,1)}) %all-gather.3.cloned.1.call-update) | async-done | bytes 12582928 | tf_op jit(solution)/shard_map/all_gather | solution.py:229
  149.1 14.2 %fusion.7 = f32[8,2,64,576]{3,2,1,0:T(8,128)S(1)} fusion(bf16[16,8,2,64,384]{4,3,2,1,0:T(8,128)(2,1)} %bitcast.111, bf16[2,16,384,288]{2,3,1,0:T(8,128)(2,1)} %get-tuple-element.9, bf16[2,16,384,288]{2,3,1,0:T(8,128)(2,1)} %get-tuple-element.10), kind=kOutput, calls=%fused_computation.11 | convolution fusion | flops 7276068864 | bytes 29097984 | tf_op jit(solution)/shard_map/esjcd,jedf->sjcf/dot_general | solution.py:238
  163.3 1.5 fusion.10.h_ref
  164.8 11.7 %shard_map.111 = bf16[16,8,2,64,384]{4,3,2,1,0:T(8,128)(2,1)} custom-call(bf16[8,2,64,288]{3,2,1,0:T(8,128)(2,1)} %fusion.10.h_ref, bf16[2,288,6144]{2,1,0:T(8,128)(2,1)} %w_ref.1), custom_call_target="tpu_custom_call" | custom-call | flops 3623878656 | bytes 20250624 | tf_op jit(solution)/shard_map/pallas_call | solution.py:32
  176.5 0.7 copy-done.1
  177.2 7.9 %fusion.4 = f32[2,1,8,64,1]{3,1,2,0,4:T(1,128)S(1)} fusion(bf16[16,8,2,64,384]{4,3,2,1,0:T(8,128)(2,1)} %bitcast.112, bf16[16,384,2,1,1]{1,0,2,3,4:T(8,128)(2,1)S(1)} %bitcast.106), kind=kOutput, calls=%fused_computation.5 | convolution fusion | flops 12582912 | bytes 12611584 | tf_op jit(solution)/shard_map/esjcd,edj->sjc/dot_general | solution.py:246
  185.1 85.4 %reduce-scatter.4.cloned.1.call-done = bf16[1,8,2,64,384]{4,3,2,1,0:T(8,128)(2,1)} async-done(((bf16[16,8,2,64,384]{4,3,2,1,0:T(8,128)(2,1)}), bf16[1,8,2,64,384]{4,3,2,1,0:T(8,128)(2,1)}) %reduce-scatter.4.cloned.1.call-update) | async-done | bytes 786448
  270.5 2.2 fusion.11.x_ref
  272.7 16.3 %shard_map.112 = bf16[8,2,64,384]{3,2,1,0:T(8,128)(2,1)} custom-call(bf16[8,2,64,384]{3,2,1,0:T(8,128)(2,1)} %fusion.11.x_ref), custom_call_target="tpu_custom_call" | custom-call | tf_op jit(solution)/shard_map/pallas_call | solution.py:86
  289.1 2.3 fusion.17
  (44 shorter events, 2.7 us)
Async XLA Ops:
  6.5 33.4 %copy-start.2 = (s32[256,2]{0,1:T(2,128)S(1)}, s32[256,2]{0,1:T(2,128)}, u32[]{:S(2)}) copy-start(s32[256,2]{0,1:T(2,128)} %param.17) | copy-start | bytes 6148
  6.5 31.6 %copy-start.3 = (bf16[384]{0:T(512)(128)(2,1)S(1)}, bf16[384]{0:T(512)(128)(2,1)}, u32[]{:S(2)}) copy-start(bf16[384]{0:T(512)(128)(2,1)} %param.16) | copy-start | bytes 2308
  6.5 33.9 %copy-start = (bf16[256,384]{1,0:T(8,128)(2,1)S(1)}, bf16[256,384]{1,0:T(8,128)(2,1)}, u32[]{:S(2)}) copy-start(bf16[256,384]{1,0:T(8,128)(2,1)} %param.15) | copy-start | bytes 589828
  6.5 142.6 %all-gather.3.cloned.1.call-start = ((), (), s32[]{:S(2)}) async-start(), calls=%async_computation.1 | async-start | bytes 13369344 | tf_op jit(solution)/shard_map/all_gather | solution.py:229
  59.7 210.8 %reduce-scatter.4.cloned.1.call-start = ((), (), s32[]{:S(2)}) async-start(), calls=%async_computation.2 | async-start | bytes 13369344
  176.5 0.7 copy-start.1
Sparse Core Ops, SparseCore 0:
  59.8 89.2 all-gather.2
  176.6 93.8 reduce-scatter.3

commit v11 on v6

--- a/solution.py
+++ b/solution.py
@@ -14,16 +14,17 @@
     return lax.ppermute(array, axis, pairs)
 
 
-def down_kernel(blocks_per_step, block_width, h_ref, w_ref, o_ref):
+def down_kernel(blocks_per_step, block_width, h_ref, s_ref, w_ref, o_ref):
     sections, capacity, hidden = h_ref.shape
     rows = h_ref[...].reshape(sections * capacity, hidden)
     product = jnp.dot(rows, w_ref[...], preferred_element_type=jnp.float32)
+    product = product * s_ref[...].reshape(sections * capacity, 1)
     for i in range(blocks_per_step):
         piece = product[:, i * block_width : (i + 1) * block_width]
         o_ref[i] = piece.astype(o_ref.dtype).reshape(sections, capacity, block_width)
 
 
-def down_projection(hidden_act, down_weight, shards):
+def down_projection(hidden_act, scale, down_weight, shards):
     sections, experts_here, capacity, hidden = hidden_act.shape
     features = down_weight.shape[2]
     block_width = features // shards
@@ -37,6 +38,7 @@
         grid=(experts_here, steps),
         in_specs=[
             pl.BlockSpec((sections, None, capacity, hidden), lambda j, b: (0, j, 0, 0)),
+            pl.BlockSpec((sections, None, capacity, 1), lambda j, b: (0, j, 0, 0)),
             pl.BlockSpec((None, hidden, blocks_per_step * block_width), lambda j, b: (j, 0, b)),
         ],
         out_specs=pl.BlockSpec(
@@ -48,7 +50,7 @@
             bytes_accessed=2 * (hidden_act.size + down_weight.size + hidden_act.size // hidden * features),
             transcendentals=0,
         ),
-    )(hidden_act, down_weight)
+    )(hidden_act, scale, down_weight)
 
 
 def exchange_kernel(x_ref, o_ref, send_sem, recv_sem, local_sem):
@@ -235,25 +237,24 @@
     gate_blocks = gate_weight.reshape(experts_here, shards, features, hidden_units)
     up_blocks = up_weight.reshape(experts_here, shards, features, hidden_units)
     router_blocks = router_weight.reshape(shards, features, experts_here)
+    router_columns = router_blocks.transpose(2, 0, 1)[..., None]
     gate_up = jnp.einsum(
         "esjcd,jedf->sjcf",
         portion,
-        jnp.concatenate([gate_blocks, up_blocks], axis=3),
+        jnp.concatenate([gate_blocks, up_blocks, router_columns], axis=3),
         preferred_element_type=jnp.float32,
     )
     gate_acc = gate_up[..., :hidden_units]
-    upward = gate_up[..., hidden_units:]
-    logits = jnp.einsum(
-        "esjcd,edj->sjc", portion, router_blocks, preferred_element_type=jnp.float32
-    )
+    upward = gate_up[..., hidden_units : 2 * hidden_units]
+    logits = gate_up[..., 2 * hidden_units]
     hidden_act = (jax.nn.silu(gate_acc) * upward).astype(jnp.bfloat16)
     expert_out = lax.psum_scatter(
-        down_projection(hidden_act, down_weight, shards),
+        down_projection(hidden_act, jax.nn.sigmoid(logits)[..., None], down_weight, shards),
         "exp",
         scatter_dimension=0,
         tiled=True,
-    )[0].astype(jnp.float32)
-    routed = (jax.nn.sigmoid(logits)[..., None] * expert_out).astype(jnp.bfloat16)
+    )[0]
+    routed = expert_out
     returned = exchange(routed, 1)
     returned = returned.reshape(expert_count * capacity, features)
     combined = lax.dot_general(

time: 299 us -> 299 us (level)
  waiting for transfers between devices: 164 us -> 173 us
  matrix products: 27.7 us -> 19.6 us
    unnamed x3, waiting for transfers between devices: 85.5 us -> 94.1 us
    dot_general x1 -> x0, matrix products: 7.86 us -> none  [on_device(): jnp.einsum('esjcd,edj->sjc', portion, router_blocks, preferred_element_ty...]
  transfers between devices with their start and end apart: 2 -> 2, of which waited for: 2 -> 2; matrix products, arithmetic and copies ran while one was open for 6% -> 4% of each run, Pallas kernels for 0% -> 0%
where the time goes in v11:
time: 299 us; the launch traced here: 298 us
  waiting for transfers between devices  173 us (58%)
  Pallas kernels  67.7 us (23%)
  matrix products  19.6 us (7%)
  local copies, waits for them, and re-layouts  16.7 us (6%)
  between operations  13.6 us (5%)
  other arithmetic  7.64 us (3%)
    unnamed x3, waiting for transfers between devices  94.1 us
    all_gather x1, waiting for transfers between devices, on_device(): portion = lax.all_gather(exchange(outgoing, 0), 'exp', axis=0)  78.8 us
    pallas_call x2, Pallas kernels, exchange(): pl.pallas_call(exchange_kernel, out_shape=jax.ShapeDtypeStruct(x.shape, x...  34.1 us
    pallas_call x1, Pallas kernels, incoming_state(): pl.pallas_call(scan_kernel, out_shape=jax.ShapeDtypeStruct((heads, rows -...  21.9 us
    dot_general x1, matrix products, on_device(): jnp.einsum('esjcd,jedf->sjcf', portion, jnp.concatenate([gate_blocks, up_...  14 us
    pallas_call x1, Pallas kernels, down_projection(): pl.pallas_call(functools.partial(down_kernel, blocks_per_step, block_widt...  11.7 us
    reshape x1, local copies, waits for them, and re-layouts, on_device(): up_blocks = up_weight.reshape(experts_here, shards, features, hidden_units)  10.5 us
  transfers between devices with their start and end apart: 2, of which 2 were waited for; matrix products, arithmetic and copies ran while one was open for 4% of the time, Pallas kernels for 0%

profile of v11, /device:TPU:1, one launch (start us, length us, event | category | flops | bytes accessed | tf_op | source)
XLA Modules:
  0.0 298.1 jit_solution(9040535682807877400)
XLA Ops:
  6.6 0.9 copy.120
  7.7 0.7 convert_element_type.43
  8.4 0.7 reshape.124
  9.1 0.9 reduce-window.14
  10.7 1.2 reduce-window.16
  12.4 0.7 multiply_add_fusion
  13.1 1.1 copy.108
  14.2 1.1 copy.109
  15.3 1.1 copy.114
  16.6 0.7 pad_maximum_fusion.x_ref
  17.3 21.9 %shard_map.109 = f32[3,128,128]{2,1,0:T(8,128)} custom-call(f32[3,136,128]{2,1,0:T(8,128)} %pad_maximum_fusion.x_ref), custom_call_target="tpu_custom_call" | custom-call | tf_op jit(solution)/shard_map/pallas_call | solution.py:146
  39.2 1.3 fusion.15
  40.5 0.5 multiply_reduce_fusion
  41.8 1.3 convolution_convert_fusion
  43.1 17.8 %shard_map.110 = bf16[8,2,64,384]{3,2,1,0:T(8,128)(2,1)} custom-call(bf16[8,2,64,384]{3,2,1,0:T(8,128)(2,1)} %bitcast.86), custom_call_target="tpu_custom_call" | custom-call | tf_op jit(solution)/shard_map/pallas_call | solution.py:88
  61.1 10.5 %copy_bitcast_fusion = (bf16[2,16,384,288]{2,3,1,0:T(8,128)(2,1)}, bf16[2,16,384,288]{2,3,1,0:T(8,128)(2,1)}) fusion(bf16[2,36,16,8,384]{4,3,2,1,0:T(8,128)(2,1)} %bitcast.84, bf16[2,36,16,8,384]{4,3,2,1,0:T(8,128)(2,1)} %bitcast.85), kind=kLoop, calls=%fused_computation.7 | loop fusion | bytes 28311552 | tf_op jit(solution)/shard_map/reshape | solution.py:238
  71.6 78.8 %all-gather.3.cloned.1.call-done = bf16[128,2,64,384]{3,2,1,0:T(8,128)(2,1)} async-done(((bf16[8,2,64,384]{3,2,1,0:T(8,128)(2,1)}), bf16[128,2,64,384]{3,2,1,0:T(8,128)(2,1)}) %all-gather.3.cloned.1.call-update) | async-done | bytes 12582928 | tf_op jit(solution)/shard_map/all_gather | solution.py:231
  150.4 14.0 %fusion.7 = f32[8,2,64,577]{3,2,1,0:T(8,128)S(1)} fusion(bf16[16,8,2,64,384]{4,3,2,1,0:T(8,128)(2,1)} %bitcast.102, bf16[2,16,384,1]{2,3,1,0:T(2,128)(2,1)S(1)} %copy.126, bf16[2,16,384,288]{2,3,1,0:T(8,128)(2,1)} %get-tuple-element.9, bf16[2,16,384,288]{2,3,1,0:T(8,128)(2,1)} %get-tuple-element.10), kind=kOutput, calls=%fused_computation.11 | convolution fusion | flops 7302881280 | bytes 29126656 | tf_op jit(solution)/shard_map/esjcd,jedf->sjcf/dot_general | solution.py:241
  164.4 1.0 fusion.24.s_ref
  165.4 1.6 fusion.10.h_ref
  167.0 11.7 %shard_map.111 = bf16[16,8,2,64,384]{4,3,2,1,0:T(8,128)(2,1)} custom-call(bf16[8,2,64,288]{3,2,1,0:T(8,128)(2,1)} %fusion.10.h_ref, f32[8,2,64,1]{3,2,1,0:T(8,128)} %fusion.24.s_ref, bf16[2,288,6144]{2,1,0:T(8,128)(2,1)} %w_ref.1), custom_call_target="tpu_custom_call" | custom-call | flops 3623878656 | bytes 20250624 | tf_op jit(solution)/shard_map/pallas_call | solution.py:33
  178.7 94.1 %reduce-scatter.4.cloned.1.call-done = bf16[1,8,2,64,384]{4,3,2,1,0:T(8,128)(2,1)} async-done(((bf16[16,8,2,64,384]{4,3,2,1,0:T(8,128)(2,1)}), bf16[1,8,2,64,384]{4,3,2,1,0:T(8,128)(2,1)}) %reduce-scatter.4.cloned.1.call-update) | async-done | bytes 786448
  272.7 16.3 %shard_map.112 = bf16[8,2,64,384]{3,2,1,0:T(8,128)(2,1)} custom-call(bf16[8,2,64,384]{3,2,1,0:T(8,128)(2,1)} %bitcast.88), custom_call_target="tpu_custom_call" | custom-call | tf_op jit(solution)/shard_map/pallas_call | solution.py:88
  289.0 2.3 fusion.16
  (39 shorter events, 2.7 us)
Async XLA Ops:
  6.5 35.2 %copy-start = (bf16[256,384]{1,0:T(8,128)(2,1)S(1)}, bf16[256,384]{1,0:T(8,128)(2,1)}, u32[]{:S(2)}) copy-start(bf16[256,384]{1,0:T(8,128)(2,1)} %param.15) | copy-start | bytes 589828
  6.5 54.5 %copy-start.1 = (bf16[6144,2]{0,1:T(2,128)(2,1)S(1)}, bf16[6144,2]{0,1:T(2,128)(2,1)}, u32[]{:S(2)}) copy-start(bf16[6144,2]{0,1:T(2,128)(2,1)} %param.18) | copy-start | bytes 73732
  6.5 143.9 %all-gather.3.cloned.1.call-start = ((), (), s32[]{:S(2)}) async-start(), calls=%async_computation.1 | async-start | bytes 13369344 | tf_op jit(solution)/shard_map/all_gather | solution.py:231
  61.0 211.7 %reduce-scatter.4.cloned.1.call-start = ((), (), s32[]{:S(2)}) async-start(), calls=%async_computation.2 | async-start | bytes 13369344
Sparse Core Ops, SparseCore 0:
  61.1 89.2 all-gather.2
  178.8 93.8 reduce-scatter.3

commit v12 on v5

--- a/solution.py
+++ b/solution.py
@@ -51,8 +51,8 @@
     )(hidden_act, down_weight)
 
 
-def exchange_kernel(x_ref, o_ref, send_sem, recv_sem, local_sem):
-    n = x_ref.shape[0]
+def exchange_kernel(spread, x_ref, o_ref, send_sem, recv_sem, local_sem):
+    n = o_ref.shape[0]
     me = lax.axis_index("seq")
     col = lax.axis_index("exp")
     mesh_id = pl.DeviceIdType.MESH
@@ -61,13 +61,13 @@
         peer = lax.rem(me + k, n)
         pl.semaphore_signal(barrier, inc=1, device_id=(peer, col), device_id_type=mesh_id)
     pl.semaphore_wait(barrier, n - 1)
-    local = pltpu.make_async_copy(x_ref.at[me], o_ref.at[me], local_sem)
+    local = pltpu.make_async_copy(x_ref if spread else x_ref.at[me], o_ref.at[me], local_sem)
     local.start()
     copies = []
     for k in range(1, n):
         peer = lax.rem(me + k, n)
         copy = pltpu.make_async_remote_copy(
-            src_ref=x_ref.at[peer],
+            src_ref=x_ref if spread else x_ref.at[peer],
             dst_ref=o_ref.at[me],
             send_sem=send_sem.at[k],
             recv_sem=recv_sem.at[k],
@@ -81,11 +81,12 @@
         copy.wait()
 
 
-def exchange(x, collective_id):
-    n = x.shape[0]
+def exchange(x, collective_id, spread=False):
+    n = lax.axis_size("seq") if spread else x.shape[0]
+    shape = (n,) + x.shape if spread else x.shape
     return pl.pallas_call(
-        exchange_kernel,
-        out_shape=jax.ShapeDtypeStruct(x.shape, x.dtype),
+        functools.partial(exchange_kernel, spread),
+        out_shape=jax.ShapeDtypeStruct(shape, x.dtype),
         in_specs=[pl.BlockSpec(memory_space=pltpu.VMEM)],
         out_specs=pl.BlockSpec(memory_space=pltpu.VMEM),
         scratch_shapes=[
@@ -134,7 +135,7 @@
         [local_state, jnp.broadcast_to(section_log_fade[:, None, None], (heads_here, 8, head_size))],
         axis=1,
     )
-    gathered = lax.all_gather(packed, "seq", axis=0)
+    gathered = exchange(packed, 2, spread=True)
     all_states = gathered[:, :, :head_size, :]
     all_log_fades = gathered[:, :, head_size, 0]
     me = lax.axis_index("seq")

time: 299 us -> 304 us (1.017)
  Pallas kernels: 42.7 us -> 70.2 us
  waiting for transfers between devices: 187 us -> 165 us
    pallas_call x2 -> x3, Pallas kernels: 31.1 us -> 58.7 us  [exchange(): pl.pallas_call(functools.partial(exchange_kernel, spread), out_shape=jax....]
    all_gather x1 -> x0, waiting for transfers between devices: 22.6 us -> none  [on_device(): gathered = lax.all_gather(packed, 'seq', axis=0)]
    unnamed x4 -> x3, waiting for transfers between devices: 85.4 us -> 85.4 us
  transfers between devices with their start and end apart: 3 -> 2, of which waited for: 3 -> 2; matrix products, arithmetic and copies ran while one was open for 8% -> 6% of each run, Pallas kernels for 0% -> 0%
where the time goes in v12:
time: 304 us; the launch traced here: 303 us
  waiting for transfers between devices  165 us (54%)
  Pallas kernels  70.2 us (23%)
  matrix products  26.7 us (9%)
  local copies, waits for them, and re-layouts  18.5 us (6%)
  between operations  13.6 us (4%)
  other arithmetic  9.2 us (3%)
    unnamed x3, waiting for transfers between devices  85.4 us
    all_gather x1, waiting for transfers between devices, on_device(): portion = lax.all_gather(exchange(outgoing, 0), 'exp', axis=0)  79.4 us
    pallas_call x3, Pallas kernels, exchange(): pl.pallas_call(functools.partial(exchange_kernel, spread), out_shape=jax....  58.7 us
    dot_general x1, matrix products, on_device(): jnp.einsum('esjcd,jedf->sjcf', portion, jnp.concatenate([gate_blocks, up_...  14.2 us
    pallas_call x1, Pallas kernels, down_projection(): pl.pallas_call(functools.partial(down_kernel, blocks_per_step, block_widt...  11.5 us
    reshape x1, local copies, waits for them, and re-layouts, on_device(): up_blocks = up_weight.reshape(experts_here, shards, features, hidden_units)  10.5 us
    dot_general x1, matrix products, on_device(): jnp.einsum('esjcd,edj->sjc', portion, router_blocks, preferred_element_ty...  7.86 us
  transfers between devices with their start and end apart: 2, of which 2 were waited for; matrix products, arithmetic and copies ran while one was open for 6% of the time, Pallas kernels for 0%

profile of v12, /device:TPU:1, one launch (start us, length us, event | category | flops | bytes accessed | tf_op | source)
XLA Modules:
  0.0 303.1 jit_solution(3152599971995146230)
XLA Ops:
  6.6 0.8 copy.128
  7.7 0.7 reshape.166
  8.4 0.9 reduce-window.14
  10.0 1.1 copy.115
  11.1 1.1 copy.120
  12.4 0.7 pad_maximum_fusion.x_ref
  13.1 27.7 %shard_map.109 = f32[8,3,136,128]{3,2,1,0:T(8,128)} custom-call(f32[3,136,128]{2,1,0:T(8,128)} %pad_maximum_fusion.x_ref), custom_call_target="tpu_custom_call" | custom-call | tf_op jit(solution)/shard_map/pallas_call | solution.py:87
  40.8 0.9 slice.31
  42.1 1.6 multiply_reduce_fusion
  43.7 1.1 copy.114
  45.9 1.2 reduce-window.16
  48.2 1.3 convolution_convert_fusion
  49.5 14.6 %shard_map.110 = bf16[8,2,64,384]{3,2,1,0:T(8,128)(2,1)} custom-call(bf16[8,2,64,384]{3,2,1,0:T(8,128)(2,1)} %bitcast.96), custom_call_target="tpu_custom_call" | custom-call | tf_op jit(solution)/shard_map/pallas_call | solution.py:87
  64.2 10.5 %copy_bitcast_fusion = (bf16[2,16,384,288]{2,3,1,0:T(8,128)(2,1)}, bf16[2,16,384,288]{2,3,1,0:T(8,128)(2,1)}) fusion(bf16[2,36,16,8,384]{4,3,2,1,0:T(8,128)(2,1)} %bitcast.94, bf16[2,36,16,8,384]{4,3,2,1,0:T(8,128)(2,1)} %bitcast.95), kind=kLoop, calls=%fused_computation.7 | loop fusion | bytes 28311552 | tf_op jit(solution)/shard_map/reshape | solution.py:192
  74.7 79.4 %all-gather.3.cloned.1.call-done = bf16[128,2,64,384]{3,2,1,0:T(8,128)(2,1)} async-done(((bf16[8,2,64,384]{3,2,1,0:T(8,128)(2,1)}), bf16[128,2,64,384]{3,2,1,0:T(8,128)(2,1)}) %all-gather.3.cloned.1.call-update) | async-done | bytes 12582928 | tf_op jit(solution)/shard_map/all_gather | solution.py:185
  154.1 14.2 %fusion.7 = f32[8,2,64,576]{3,2,1,0:T(8,128)S(1)} fusion(bf16[16,8,2,64,384]{4,3,2,1,0:T(8,128)(2,1)} %bitcast.113, bf16[2,16,384,288]{2,3,1,0:T(8,128)(2,1)} %get-tuple-element.9, bf16[2,16,384,288]{2,3,1,0:T(8,128)(2,1)} %get-tuple-element.10), kind=kOutput, calls=%fused_computation.11 | convolution fusion | flops 7276068864 | bytes 29097984 | tf_op jit(solution)/shard_map/esjcd,jedf->sjcf/dot_general | solution.py:194
  168.3 1.5 fusion.10.h_ref
  169.8 11.5 %shard_map.111 = bf16[16,8,2,64,384]{4,3,2,1,0:T(8,128)(2,1)} custom-call(bf16[8,2,64,288]{3,2,1,0:T(8,128)(2,1)} %fusion.10.h_ref, bf16[2,288,6144]{2,1,0:T(8,128)(2,1)} %w_ref.1), custom_call_target="tpu_custom_call" | custom-call | flops 3623878656 | bytes 20250624 | tf_op jit(solution)/shard_map/pallas_call | solution.py:32
  181.4 0.7 copy-done.1
  182.1 7.9 %fusion.4 = f32[2,1,8,64,1]{3,1,2,0,4:T(1,128)S(1)} fusion(bf16[16,8,2,64,384]{4,3,2,1,0:T(8,128)(2,1)} %bitcast.114, bf16[16,384,2,1,1]{1,0,2,3,4:T(8,128)(2,1)S(1)} %bitcast.106), kind=kOutput, calls=%fused_computation.5 | convolution fusion | flops 12582912 | bytes 12611584 | tf_op jit(solution)/shard_map/esjcd,edj->sjc/dot_general | solution.py:202
  190.0 85.4 %reduce-scatter.4.cloned.1.call-done = bf16[1,8,2,64,384]{4,3,2,1,0:T(8,128)(2,1)} async-done(((bf16[16,8,2,64,384]{4,3,2,1,0:T(8,128)(2,1)}), bf16[1,8,2,64,384]{4,3,2,1,0:T(8,128)(2,1)}) %reduce-scatter.4.cloned.1.call-update) | async-done | bytes 786448
  275.4 2.2 fusion.11.x_ref
  277.6 16.3 %shard_map.112 = bf16[8,2,64,384]{3,2,1,0:T(8,128)(2,1)} custom-call(bf16[8,2,64,384]{3,2,1,0:T(8,128)(2,1)} %fusion.11.x_ref), custom_call_target="tpu_custom_call" | custom-call | tf_op jit(solution)/shard_map/pallas_call | solution.py:87
  293.9 2.3 fusion.17
  (51 shorter events, 3.9 us)
Async XLA Ops:
  6.5 41.1 %copy-start.2 = (s32[256,2]{0,1:T(2,128)S(1)}, s32[256,2]{0,1:T(2,128)}, u32[]{:S(2)}) copy-start(s32[256,2]{0,1:T(2,128)} %param.17) | copy-start | bytes 6148
  6.5 39.3 %copy-start.3 = (bf16[384]{0:T(512)(128)(2,1)S(1)}, bf16[384]{0:T(512)(128)(2,1)}, u32[]{:S(2)}) copy-start(bf16[384]{0:T(512)(128)(2,1)} %param.16) | copy-start | bytes 2308
  6.5 41.6 %copy-start = (bf16[256,384]{1,0:T(8,128)(2,1)S(1)}, bf16[256,384]{1,0:T(8,128)(2,1)}, u32[]{:S(2)}) copy-start(bf16[256,384]{1,0:T(8,128)(2,1)} %param.15) | copy-start | bytes 589828
  6.5 147.6 %all-gather.3.cloned.1.call-start = ((), (), s32[]{:S(2)}) async-start(), calls=%async_computation.1 | async-start | bytes 13369344 | tf_op jit(solution)/shard_map/all_gather | solution.py:185
  64.2 211.2 %reduce-scatter.4.cloned.1.call-start = ((), (), s32[]{:S(2)}) async-start(), calls=%async_computation.2 | async-start | bytes 13369344
  181.3 0.7 copy-start.1
Sparse Core Ops, SparseCore 0:
  64.3 89.7 all-gather.2
  181.5 93.8 reduce-scatter.3

commit v13 on v6

--- a/solution.py
+++ b/solution.py
@@ -109,6 +109,7 @@
         pl.semaphore_signal(barrier, inc=1, device_id=(peer, col), device_id_type=mesh_id)
     pl.semaphore_wait(barrier, n - 1)
     shifts = [1, 1, 2, 4]
+    sent = []
     for r, d in enumerate(shifts):
         source = x_ref if r == 0 else state.at[r - 1]
         copy = pltpu.make_async_remote_copy(
@@ -120,7 +121,8 @@
             device_id_type=mesh_id,
         )
         copy.start()
-        copy.wait()
+        sent.append(copy)
+        copy.wait_recv()
         has_input = me - d >= 0
         other = received[r]
         if r == 0:
@@ -136,6 +138,8 @@
             state[r, :, size:, :] = jnp.where(has_input, combined_fade, mine[:, size:, :])
 
     o_ref[...] = state[len(shifts) - 1, :, :size, :]
+    for copy in sent:
+        copy.wait_send()
 
 
 def incoming_state(packed):

time: 299 us -> 299 us (level)
  no operation moved by 1% of the time
where the time goes in v13:
time: 299 us; the launch traced here: 298 us
  waiting for transfers between devices  164 us (55%)
  Pallas kernels  67.8 us (23%)
  matrix products  27.7 us (9%)
  local copies, waits for them, and re-layouts  17.4 us (6%)
  between operations  13.6 us (5%)
  other arithmetic  7.46 us (2%)
    unnamed x3, waiting for transfers between devices  85.2 us
    all_gather x1, waiting for transfers between devices, on_device(): portion = lax.all_gather(exchange(outgoing, 0), 'exp', axis=0)  78.8 us
    pallas_call x2, Pallas kernels, exchange(): pl.pallas_call(exchange_kernel, out_shape=jax.ShapeDtypeStruct(x.shape, x...  33.4 us
    pallas_call x1, Pallas kernels, incoming_state(): pl.pallas_call(scan_kernel, out_shape=jax.ShapeDtypeStruct((heads, rows -...  22.8 us
    dot_general x1, matrix products, on_device(): jnp.einsum('esjcd,jedf->sjcf', portion, jnp.concatenate([gate_blocks, up_...  14.2 us
    pallas_call x1, Pallas kernels, down_projection(): pl.pallas_call(functools.partial(down_kernel, blocks_per_step, block_widt...  11.5 us
    reshape x1, local copies, waits for them, and re-layouts, on_device(): up_blocks = up_weight.reshape(experts_here, shards, features, hidden_units)  10.5 us
    dot_general x1, matrix products, on_device(): jnp.einsum('esjcd,edj->sjc', portion, router_blocks, preferred_element_ty...  7.86 us
  transfers between devices with their start and end apart: 2, of which 2 were waited for; matrix products, arithmetic and copies ran while one was open for 6% of the time, Pallas kernels for 0%

profile of v13, /device:TPU:1, one launch (start us, length us, event | category | flops | bytes accessed | tf_op | source)
XLA Modules:
  0.0 297.9 jit_solution(13640458493808343927)
XLA Ops:
  6.6 0.8 copy.116
  7.7 0.7 reshape.127
  8.4 0.9 reduce-window.14
  10.0 1.1 copy.105
  11.1 1.1 copy.110
  12.4 0.7 pad_maximum_fusion.x_ref
  13.1 22.8 %shard_map.109 = f32[3,128,128]{2,1,0:T(8,128)} custom-call(f32[3,136,128]{2,1,0:T(8,128)} %pad_maximum_fusion.x_ref), custom_call_target="tpu_custom_call" | custom-call | tf_op jit(solution)/shard_map/pallas_call | solution.py:148
  35.9 1.1 copy.104
  37.0 1.3 fusion.16
  38.3 0.5 multiply_reduce_fusion
  39.1 1.2 reduce-window.16
  41.4 1.3 convolution_convert_fusion
  42.7 17.1 %shard_map.110 = bf16[8,2,64,384]{3,2,1,0:T(8,128)(2,1)} custom-call(bf16[8,2,64,384]{3,2,1,0:T(8,128)(2,1)} %bitcast.96), custom_call_target="tpu_custom_call" | custom-call | tf_op jit(solution)/shard_map/pallas_call | solution.py:86
  59.9 10.5 %copy_bitcast_fusion = (bf16[2,16,384,288]{2,3,1,0:T(8,128)(2,1)}, bf16[2,16,384,288]{2,3,1,0:T(8,128)(2,1)}) fusion(bf16[2,36,16,8,384]{4,3,2,1,0:T(8,128)(2,1)} %bitcast.94, bf16[2,36,16,8,384]{4,3,2,1,0:T(8,128)(2,1)} %bitcast.95), kind=kLoop, calls=%fused_computation.7 | loop fusion | bytes 28311552 | tf_op jit(solution)/shard_map/reshape | solution.py:240
  70.4 78.8 %all-gather.3.cloned.1.call-done = bf16[128,2,64,384]{3,2,1,0:T(8,128)(2,1)} async-done(((bf16[8,2,64,384]{3,2,1,0:T(8,128)(2,1)}), bf16[128,2,64,384]{3,2,1,0:T(8,128)(2,1)}) %all-gather.3.cloned.1.call-update) | async-done | bytes 12582928 | tf_op jit(solution)/shard_map/all_gather | solution.py:233
  149.2 14.2 %fusion.7 = f32[8,2,64,576]{3,2,1,0:T(8,128)S(1)} fusion(bf16[16,8,2,64,384]{4,3,2,1,0:T(8,128)(2,1)} %bitcast.111, bf16[2,16,384,288]{2,3,1,0:T(8,128)(2,1)} %get-tuple-element.9, bf16[2,16,384,288]{2,3,1,0:T(8,128)(2,1)} %get-tuple-element.10), kind=kOutput, calls=%fused_computation.11 | convolution fusion | flops 7276068864 | bytes 29097984 | tf_op jit(solution)/shard_map/esjcd,jedf->sjcf/dot_general | solution.py:242
  163.3 1.5 fusion.10.h_ref
  164.9 11.5 %shard_map.111 = bf16[16,8,2,64,384]{4,3,2,1,0:T(8,128)(2,1)} custom-call(bf16[8,2,64,288]{3,2,1,0:T(8,128)(2,1)} %fusion.10.h_ref, bf16[2,288,6144]{2,1,0:T(8,128)(2,1)} %w_ref.1), custom_call_target="tpu_custom_call" | custom-call | flops 3623878656 | bytes 20250624 | tf_op jit(solution)/shard_map/pallas_call | solution.py:32
  176.4 0.7 copy-done.1
  177.1 7.9 %fusion.4 = f32[2,1,8,64,1]{3,1,2,0,4:T(1,128)S(1)} fusion(bf16[16,8,2,64,384]{4,3,2,1,0:T(8,128)(2,1)} %bitcast.112, bf16[16,384,2,1,1]{1,0,2,3,4:T(8,128)(2,1)S(1)} %bitcast.106), kind=kOutput, calls=%fused_computation.5 | convolution fusion | flops 12582912 | bytes 12611584 | tf_op jit(solution)/shard_map/esjcd,edj->sjc/dot_general | solution.py:250
  185.0 85.2 %reduce-scatter.4.cloned.1.call-done = bf16[1,8,2,64,384]{4,3,2,1,0:T(8,128)(2,1)} async-done(((bf16[16,8,2,64,384]{4,3,2,1,0:T(8,128)(2,1)}), bf16[1,8,2,64,384]{4,3,2,1,0:T(8,128)(2,1)}) %reduce-scatter.4.cloned.1.call-update) | async-done | bytes 786448
  270.2 2.2 fusion.11.x_ref
  272.5 16.4 %shard_map.112 = bf16[8,2,64,384]{3,2,1,0:T(8,128)(2,1)} custom-call(bf16[8,2,64,384]{3,2,1,0:T(8,128)(2,1)} %fusion.11.x_ref), custom_call_target="tpu_custom_call" | custom-call | tf_op jit(solution)/shard_map/pallas_call | solution.py:86
  288.8 2.3 fusion.17
  (44 shorter events, 2.7 us)
Async XLA Ops:
  6.5 34.3 %copy-start.2 = (s32[256,2]{0,1:T(2,128)S(1)}, s32[256,2]{0,1:T(2,128)}, u32[]{:S(2)}) copy-start(s32[256,2]{0,1:T(2,128)} %param.17) | copy-start | bytes 6148
  6.5 32.5 %copy-start.3 = (bf16[384]{0:T(512)(128)(2,1)S(1)}, bf16[384]{0:T(512)(128)(2,1)}, u32[]{:S(2)}) copy-start(bf16[384]{0:T(512)(128)(2,1)} %param.16) | copy-start | bytes 2308
  6.5 34.8 %copy-start = (bf16[256,384]{1,0:T(8,128)(2,1)S(1)}, bf16[256,384]{1,0:T(8,128)(2,1)}, u32[]{:S(2)}) copy-start(bf16[256,384]{1,0:T(8,128)(2,1)} %param.15) | copy-start | bytes 589828
  6.5 142.6 %all-gather.3.cloned.1.call-start = ((), (), s32[]{:S(2)}) async-start(), calls=%async_computation.1 | async-start | bytes 13369344 | tf_op jit(solution)/shard_map/all_gather | solution.py:233
  59.8 210.4 %reduce-scatter.4.cloned.1.call-start = ((), (), s32[]{:S(2)}) async-start(), calls=%async_computation.2 | async-start | bytes 13369344
  176.4 0.7 copy-start.1
Sparse Core Ops, SparseCore 0:
  60.0 89.1 all-gather.2
  176.5 93.6 reduce-scatter.3

commit v14 on v6

--- a/solution.py
+++ b/solution.py
@@ -104,10 +104,11 @@
     mesh_id = pl.DeviceIdType.MESH
     size = x_ref.shape[1] - 8
     barrier = pltpu.get_barrier_semaphore()
-    for k in range(1, n):
+    partners = [1, n - 1, 2, n - 2, 4]
+    for k in partners:
         peer = lax.rem(me + k, n)
         pl.semaphore_signal(barrier, inc=1, device_id=(peer, col), device_id_type=mesh_id)
-    pl.semaphore_wait(barrier, n - 1)
+    pl.semaphore_wait(barrier, len(partners))
     shifts = [1, 1, 2, 4]
     for r, d in enumerate(shifts):
         source = x_ref if r == 0 else state.at[r - 1]

time: 299 us -> 298 us (level)
  no operation moved by 1% of the time
where the time goes in v14:
time: 298 us
  waiting for transfers between devices  165 us (55%)
  Pallas kernels  67 us (22%)
  matrix products  27.7 us (9%)
  local copies, waits for them, and re-layouts  17.4 us (6%)
  between operations  13.6 us (5%)
  other arithmetic  7.46 us (3%)
    unnamed x3, waiting for transfers between devices  85.3 us
    all_gather x1, waiting for transfers between devices, on_device(): portion = lax.all_gather(exchange(outgoing, 0), 'exp', axis=0)  79.3 us
    pallas_call x2, Pallas kernels, exchange(): pl.pallas_call(exchange_kernel, out_shape=jax.ShapeDtypeStruct(x.shape, x...  34.2 us
    pallas_call x1, Pallas kernels, incoming_state(): pl.pallas_call(scan_kernel, out_shape=jax.ShapeDtypeStruct((heads, rows -...  21.4 us
    dot_general x1, matrix products, on_device(): jnp.einsum('esjcd,jedf->sjcf', portion, jnp.concatenate([gate_blocks, up_...  14.2 us
    pallas_call x1, Pallas kernels, down_projection(): pl.pallas_call(functools.partial(down_kernel, blocks_per_step, block_widt...  11.5 us
    reshape x1, local copies, waits for them, and re-layouts, on_device(): up_blocks = up_weight.reshape(experts_here, shards, features, hidden_units)  10.5 us
    dot_general x1, matrix products, on_device(): jnp.einsum('esjcd,edj->sjc', portion, router_blocks, preferred_element_ty...  7.86 us
  transfers between devices with their start and end apart: 2, of which 2 were waited for; matrix products, arithmetic and copies ran while one was open for 6% of the time, Pallas kernels for 0%

profile of v14, /device:TPU:1, one launch (start us, length us, event | category | flops | bytes accessed | tf_op | source)
XLA Modules:
  0.0 297.8 jit_solution(4199838650797650549)
XLA Ops:
  6.6 0.8 copy.116
  7.7 0.7 reshape.127
  8.4 0.9 reduce-window.14
  10.0 1.1 copy.105
  11.1 1.1 copy.110
  12.4 0.7 pad_maximum_fusion.x_ref
  13.1 21.4 %shard_map.109 = f32[3,128,128]{2,1,0:T(8,128)} custom-call(f32[3,136,128]{2,1,0:T(8,128)} %pad_maximum_fusion.x_ref), custom_call_target="tpu_custom_call" | custom-call | tf_op jit(solution)/shard_map/pallas_call | solution.py:145
  34.5 1.1 copy.104
  35.5 1.3 fusion.16
  36.8 0.5 multiply_reduce_fusion
  37.6 1.2 reduce-window.16
  39.9 1.3 convolution_convert_fusion
  41.2 17.8 %shard_map.110 = bf16[8,2,64,384]{3,2,1,0:T(8,128)(2,1)} custom-call(bf16[8,2,64,384]{3,2,1,0:T(8,128)(2,1)} %bitcast.96), custom_call_target="tpu_custom_call" | custom-call | tf_op jit(solution)/shard_map/pallas_call | solution.py:86
  59.2 10.5 %copy_bitcast_fusion = (bf16[2,16,384,288]{2,3,1,0:T(8,128)(2,1)}, bf16[2,16,384,288]{2,3,1,0:T(8,128)(2,1)}) fusion(bf16[2,36,16,8,384]{4,3,2,1,0:T(8,128)(2,1)} %bitcast.94, bf16[2,36,16,8,384]{4,3,2,1,0:T(8,128)(2,1)} %bitcast.95), kind=kLoop, calls=%fused_computation.7 | loop fusion | bytes 28311552 | tf_op jit(solution)/shard_map/reshape | solution.py:237
  69.6 79.3 %all-gather.3.cloned.1.call-done = bf16[128,2,64,384]{3,2,1,0:T(8,128)(2,1)} async-done(((bf16[8,2,64,384]{3,2,1,0:T(8,128)(2,1)}), bf16[128,2,64,384]{3,2,1,0:T(8,128)(2,1)}) %all-gather.3.cloned.1.call-update) | async-done | bytes 12582928 | tf_op jit(solution)/shard_map/all_gather | solution.py:230
  149.0 14.2 %fusion.7 = f32[8,2,64,576]{3,2,1,0:T(8,128)S(1)} fusion(bf16[16,8,2,64,384]{4,3,2,1,0:T(8,128)(2,1)} %bitcast.111, bf16[2,16,384,288]{2,3,1,0:T(8,128)(2,1)} %get-tuple-element.9, bf16[2,16,384,288]{2,3,1,0:T(8,128)(2,1)} %get-tuple-element.10), kind=kOutput, calls=%fused_computation.11 | convolution fusion | flops 7276068864 | bytes 29097984 | tf_op jit(solution)/shard_map/esjcd,jedf->sjcf/dot_general | solution.py:239
  163.1 1.5 fusion.10.h_ref
  164.7 11.5 %shard_map.111 = bf16[16,8,2,64,384]{4,3,2,1,0:T(8,128)(2,1)} custom-call(bf16[8,2,64,288]{3,2,1,0:T(8,128)(2,1)} %fusion.10.h_ref, bf16[2,288,6144]{2,1,0:T(8,128)(2,1)} %w_ref.1), custom_call_target="tpu_custom_call" | custom-call | flops 3623878656 | bytes 20250624 | tf_op jit(solution)/shard_map/pallas_call | solution.py:32
  176.2 0.7 copy-done.1
  176.9 7.9 %fusion.4 = f32[2,1,8,64,1]{3,1,2,0,4:T(1,128)S(1)} fusion(bf16[16,8,2,64,384]{4,3,2,1,0:T(8,128)(2,1)} %bitcast.112, bf16[16,384,2,1,1]{1,0,2,3,4:T(8,128)(2,1)S(1)} %bitcast.106), kind=kOutput, calls=%fused_computation.5 | convolution fusion | flops 12582912 | bytes 12611584 | tf_op jit(solution)/shard_map/esjcd,edj->sjc/dot_general | solution.py:247
  184.8 85.2 %reduce-scatter.4.cloned.1.call-done = bf16[1,8,2,64,384]{4,3,2,1,0:T(8,128)(2,1)} async-done(((bf16[16,8,2,64,384]{4,3,2,1,0:T(8,128)(2,1)}), bf16[1,8,2,64,384]{4,3,2,1,0:T(8,128)(2,1)}) %reduce-scatter.4.cloned.1.call-update) | async-done | bytes 786448
  270.1 2.2 fusion.11.x_ref
  272.3 16.3 %shard_map.112 = bf16[8,2,64,384]{3,2,1,0:T(8,128)(2,1)} custom-call(bf16[8,2,64,384]{3,2,1,0:T(8,128)(2,1)} %fusion.11.x_ref), custom_call_target="tpu_custom_call" | custom-call | tf_op jit(solution)/shard_map/pallas_call | solution.py:86
  288.6 2.3 fusion.17
  (44 shorter events, 2.7 us)
Async XLA Ops:
  6.5 32.8 %copy-start.2 = (s32[256,2]{0,1:T(2,128)S(1)}, s32[256,2]{0,1:T(2,128)}, u32[]{:S(2)}) copy-start(s32[256,2]{0,1:T(2,128)} %param.17) | copy-start | bytes 6148
  6.5 31.1 %copy-start.3 = (bf16[384]{0:T(512)(128)(2,1)S(1)}, bf16[384]{0:T(512)(128)(2,1)}, u32[]{:S(2)}) copy-start(bf16[384]{0:T(512)(128)(2,1)} %param.16) | copy-start | bytes 2308
  6.5 33.3 %copy-start = (bf16[256,384]{1,0:T(8,128)(2,1)S(1)}, bf16[256,384]{1,0:T(8,128)(2,1)}, u32[]{:S(2)}) copy-start(bf16[256,384]{1,0:T(8,128)(2,1)} %param.15) | copy-start | bytes 589828
  6.5 142.4 %all-gather.3.cloned.1.call-start = ((), (), s32[]{:S(2)}) async-start(), calls=%async_computation.1 | async-start | bytes 13369344 | tf_op jit(solution)/shard_map/all_gather | solution.py:230
  59.1 211.0 %reduce-scatter.4.cloned.1.call-start = ((), (), s32[]{:S(2)}) async-start(), calls=%async_computation.2 | async-start | bytes 13369344
  176.2 0.7 copy-start.1
Sparse Core Ops, SparseCore 0:
  59.2 89.6 all-gather.2
  176.3 93.6 reduce-scatter.3

commit v15 on v6

--- a/solution.py
+++ b/solution.py
@@ -15,8 +15,11 @@
 
 
 def down_kernel(blocks_per_step, block_width, h_ref, w_ref, o_ref):
-    sections, capacity, hidden = h_ref.shape
-    rows = h_ref[...].reshape(sections * capacity, hidden)
+    sections, capacity, both = h_ref.shape
+    hidden = both // 2
+    pair = h_ref[...].reshape(sections * capacity, both)
+    gate_acc = pair[:, :hidden]
+    rows = (gate_acc / (1.0 + jnp.exp(-gate_acc)) * pair[:, hidden:]).astype(jnp.bfloat16)
     product = jnp.dot(rows, w_ref[...], preferred_element_type=jnp.float32)
     for i in range(blocks_per_step):
         piece = product[:, i * block_width : (i + 1) * block_width]
@@ -24,7 +27,8 @@
 
 
 def down_projection(hidden_act, down_weight, shards):
-    sections, experts_here, capacity, hidden = hidden_act.shape
+    sections, experts_here, capacity, both = hidden_act.shape
+    hidden = both // 2
     features = down_weight.shape[2]
     block_width = features // shards
     blocks_per_step = 8
@@ -36,7 +40,7 @@
         ),
         grid=(experts_here, steps),
         in_specs=[
-            pl.BlockSpec((sections, None, capacity, hidden), lambda j, b: (0, j, 0, 0)),
+            pl.BlockSpec((sections, None, capacity, both), lambda j, b: (0, j, 0, 0)),
             pl.BlockSpec((None, hidden, blocks_per_step * block_width), lambda j, b: (j, 0, b)),
         ],
         out_specs=pl.BlockSpec(
@@ -45,7 +49,7 @@
         ),
         cost_estimate=pl.CostEstimate(
             flops=2 * sections * experts_here * capacity * hidden * features,
-            bytes_accessed=2 * (hidden_act.size + down_weight.size + hidden_act.size // hidden * features),
+            bytes_accessed=4 * hidden_act.size + 2 * (down_weight.size + hidden_act.size // both * features),
             transcendentals=0,
         ),
     )(hidden_act, down_weight)
@@ -241,14 +245,11 @@
         jnp.concatenate([gate_blocks, up_blocks], axis=3),
         preferred_element_type=jnp.float32,
     )
-    gate_acc = gate_up[..., :hidden_units]
-    upward = gate_up[..., hidden_units:]
     logits = jnp.einsum(
         "esjcd,edj->sjc", portion, router_blocks, preferred_element_type=jnp.float32
     )
-    hidden_act = (jax.nn.silu(gate_acc) * upward).astype(jnp.bfloat16)
     expert_out = lax.psum_scatter(
-        down_projection(hidden_act, down_weight, shards),
+        down_projection(gate_up, down_weight, shards),
         "exp",
         scatter_dimension=0,
         tiled=True,

time: 299 us -> 300 us (level)
  no operation moved by 1% of the time
where the time goes in v15:
time: 300 us; the launch traced here: 299 us
  waiting for transfers between devices  164 us (55%)
  Pallas kernels  68.7 us (23%)
  matrix products  29.1 us (10%)
  local copies, waits for them, and re-layouts  17.4 us (6%)
  between operations  13.6 us (5%)
  other arithmetic  5.93 us (2%)
    unnamed x3, waiting for transfers between devices  85.6 us
    all_gather x1, waiting for transfers between devices, on_device(): portion = lax.all_gather(exchange(outgoing, 0), 'exp', axis=0)  78.9 us
    pallas_call x2, Pallas kernels, exchange(): pl.pallas_call(exchange_kernel, out_shape=jax.ShapeDtypeStruct(x.shape, x...  34.1 us
    pallas_call x1, Pallas kernels, incoming_state(): pl.pallas_call(scan_kernel, out_shape=jax.ShapeDtypeStruct((heads, rows -...  21.9 us
    dot_general x1, matrix products, on_device(): jnp.einsum('esjcd,jedf->sjcf', portion, jnp.concatenate([gate_blocks, up_...  15.6 us
    pallas_call x1, Pallas kernels, down_projection(): pl.pallas_call(functools.partial(down_kernel, blocks_per_step, block_widt...  12.7 us
    reshape x1, local copies, waits for them, and re-layouts, on_device(): up_blocks = up_weight.reshape(experts_here, shards, features, hidden_units)  10.5 us
    dot_general x1, matrix products, on_device(): jnp.einsum('esjcd,edj->sjc', portion, router_blocks, preferred_element_ty...  7.86 us
  transfers between devices with their start and end apart: 2, of which 2 were waited for; matrix products, arithmetic and copies ran while one was open for 6% of the time, Pallas kernels for 0%

profile of v15, /device:TPU:1, one launch (start us, length us, event | category | flops | bytes accessed | tf_op | source)
XLA Modules:
  0.0 299.2 jit_solution(16704187071013555822)
XLA Ops:
  6.6 0.8 copy.113
  7.7 0.7 reshape.127
  8.4 0.9 reduce-window.14
  10.0 1.1 copy.102
  11.1 1.1 copy.107
  12.4 0.7 pad_maximum_fusion.x_ref
  13.1 21.9 %shard_map.109 = f32[3,128,128]{2,1,0:T(8,128)} custom-call(f32[3,136,128]{2,1,0:T(8,128)} %pad_maximum_fusion.x_ref), custom_call_target="tpu_custom_call" | custom-call | tf_op jit(solution)/shard_map/pallas_call | solution.py:148
  35.0 1.1 copy.101
  36.1 1.3 fusion.15
  37.4 0.5 multiply_reduce_fusion
  38.2 1.2 reduce-window.16
  39.9 0.5 fusion.17
  40.5 1.3 convolution_convert_fusion
  41.8 17.8 %shard_map.110 = bf16[8,2,64,384]{3,2,1,0:T(8,128)(2,1)} custom-call(bf16[8,2,64,384]{3,2,1,0:T(8,128)(2,1)} %bitcast.97), custom_call_target="tpu_custom_call" | custom-call | tf_op jit(solution)/shard_map/pallas_call | solution.py:90
  59.7 10.5 %copy_bitcast_fusion = (bf16[2,16,384,288]{2,3,1,0:T(8,128)(2,1)}, bf16[2,16,384,288]{2,3,1,0:T(8,128)(2,1)}) fusion(bf16[2,36,16,8,384]{4,3,2,1,0:T(8,128)(2,1)} %bitcast.95, bf16[2,36,16,8,384]{4,3,2,1,0:T(8,128)(2,1)} %bitcast.96), kind=kLoop, calls=%fused_computation.7 | loop fusion | bytes 28311552 | tf_op jit(solution)/shard_map/reshape | solution.py:240
  70.2 78.9 %all-gather.3.cloned.1.call-done = bf16[128,2,64,384]{3,2,1,0:T(8,128)(2,1)} async-done(((bf16[8,2,64,384]{3,2,1,0:T(8,128)(2,1)}), bf16[128,2,64,384]{3,2,1,0:T(8,128)(2,1)}) %all-gather.3.cloned.1.call-update) | async-done | bytes 12582928 | tf_op jit(solution)/shard_map/all_gather | solution.py:233
  149.1 15.6 %fusion.7.h_ref = f32[8,2,64,576]{3,2,1,0:T(8,128)} fusion(bf16[16,8,2,64,384]{4,3,2,1,0:T(8,128)(2,1)} %bitcast.112, bf16[2,16,384,288]{2,3,1,0:T(8,128)(2,1)} %get-tuple-element.9, bf16[2,16,384,288]{2,3,1,0:T(8,128)(2,1)} %get-tuple-element.10), kind=kOutput, calls=%fused_computation.11 | convolution fusion | flops 7276068864 | bytes 29097984 | tf_op jit(solution)/shard_map/esjcd,jedf->sjcf/dot_general | solution.py:242
  164.7 12.7 %shard_map.111 = bf16[16,8,2,64,384]{4,3,2,1,0:T(8,128)(2,1)} custom-call(f32[8,2,64,576]{3,2,1,0:T(8,128)} %fusion.7.h_ref, bf16[2,288,6144]{2,1,0:T(8,128)(2,1)} %w_ref.1), custom_call_target="tpu_custom_call" | custom-call | flops 3623878656 | bytes 22020096 | tf_op jit(solution)/shard_map/pallas_call | solution.py:36
  177.4 0.7 copy-done.1
  178.1 7.9 %fusion.3 = f32[2,1,8,64,1]{3,1,2,0,4:T(1,128)S(1)} fusion(bf16[16,8,2,64,384]{4,3,2,1,0:T(8,128)(2,1)} %bitcast.113, bf16[16,384,2,1,1]{1,0,2,3,4:T(8,128)(2,1)S(1)} %bitcast.107), kind=kOutput, calls=%fused_computation.4 | convolution fusion | flops 12582912 | bytes 12611584 | tf_op jit(solution)/shard_map/esjcd,edj->sjc/dot_general | solution.py:248
  186.0 85.5 %reduce-scatter.4.cloned.1.call-done = bf16[1,8,2,64,384]{4,3,2,1,0:T(8,128)(2,1)} async-done(((bf16[16,8,2,64,384]{4,3,2,1,0:T(8,128)(2,1)}), bf16[1,8,2,64,384]{4,3,2,1,0:T(8,128)(2,1)}) %reduce-scatter.4.cloned.1.call-update) | async-done | bytes 786448
  271.6 2.2 fusion.10.x_ref
  273.8 16.3 %shard_map.112 = bf16[8,2,64,384]{3,2,1,0:T(8,128)(2,1)} custom-call(bf16[8,2,64,384]{3,2,1,0:T(8,128)(2,1)} %fusion.10.x_ref), custom_call_target="tpu_custom_call" | custom-call | tf_op jit(solution)/shard_map/pallas_call | solution.py:90
  290.1 2.3 fusion.16
  (43 shorter events, 2.2 us)
Async XLA Ops:
  6.5 33.4 %copy-start.2 = (s32[256,2]{0,1:T(2,128)S(1)}, s32[256,2]{0,1:T(2,128)}, u32[]{:S(2)}) copy-start(s32[256,2]{0,1:T(2,128)} %param.17) | copy-start | bytes 6148
  6.5 31.6 %copy-start.3 = (bf16[384]{0:T(512)(128)(2,1)S(1)}, bf16[384]{0:T(512)(128)(2,1)}, u32[]{:S(2)}) copy-start(bf16[384]{0:T(512)(128)(2,1)} %param.16) | copy-start | bytes 2308
  6.5 33.9 %copy-start = (bf16[256,384]{1,0:T(8,128)(2,1)S(1)}, bf16[256,384]{1,0:T(8,128)(2,1)}, u32[]{:S(2)}) copy-start(bf16[256,384]{1,0:T(8,128)(2,1)} %param.15) | copy-start | bytes 589828
  6.5 142.6 %all-gather.3.cloned.1.call-start = ((), (), s32[]{:S(2)}) async-start(), calls=%async_computation.1 | async-start | bytes 13369344 | tf_op jit(solution)/shard_map/all_gather | solution.py:233
  59.7 211.9 %reduce-scatter.4.cloned.1.call-start = ((), (), s32[]{:S(2)}) async-start(), calls=%async_computation.2 | async-start | bytes 13369344
  177.4 0.7 copy-start.1
Sparse Core Ops, SparseCore 0:
  59.8 89.2 all-gather.2
  177.5 93.9 reduce-scatter.3
